TPU v7x, 512 devices: a whole 4x4x16 slice. The times are simulated.
512 devices in a mesh: dom: 16 (over x_lo, y, core), space: 32 (over x_hi, z).
Axes of the slice: x: 4 (x_hi: 2, x_lo: 2; x = x_hi * 2 + x_lo), y: 4, z: 16, core: 2. Of those that a mesh axis runs over, the one named last changes fastest.
Arguments:
- orbitals: bfloat16 [16, 2, 128, 16, 8, 128], P('dom', None, 'space'), may hold values from -6 to 6
- initial: bfloat16 [16, 2, 128, 16, 8, 128], P('dom', None, 'space'), may hold values from -4 to 4
- potential: float32 [16, 128, 128], P('dom', 'space'), may hold values from -1 to 1
- external: float32 [16, 128, 128], P('dom', 'space'), may hold values from -1 to 1
- occupation: float32 [128], replicated, may hold values from 0.5 to 2
- coupling: float32 [128, 128], replicated, may hold values from -1.25 to 1.25
- neighbours: int32 [16, 2], replicated, may hold values from 0 to 15, as said below
- offsets: int32 [16, 2], replicated, may hold values from 0 to 12
Outputs:
- evolved: bfloat16 [16, 2, 128, 16, 8, 128], P('dom', None, 'space')
- intersection: float32 [16, 2, 128, 128], P('dom')
- new_potential: float32 [16, 128, 128], P('dom', 'space')
Inputs may be any that keep to these rules, and one draw needn't show every extreme that they name: Following upper neighbours visits all 16 domains in one cycle, and the lower neighbour of a domain's upper neighbour is that domain.
All inputs are finite; a program needn't handle non-finite values.
Results may differ from a plain program's by a relative error of at most 0.007.
Values may be sent and summed in bfloat16 or wider, within the bound.
No kernel may reach another device: no remote copies, remote signals or barrier semaphores. Data moves between devices by JAX's collectives and lax.ppermute only.
A program may use at most 64 MiB of HBM per device.

v0:
```python
import jax
import jax.numpy as jnp
from jax import lax
from jax.sharding import PartitionSpec as P

TAYLOR = 4
STEPS = 2
BUF = 4


time_step = 0.4
half_step = 0.2
xc_factor = 0.9847450218426965


def padded_2(value, sides, width):
    for axis, dim in sides:
        devices, length = (lax.axis_size(axis), value.shape[dim])
        up = [(i, (i + 1) % devices) for i in range(devices - 1)]
        down = [(j, i) for i, j in up]
        last = lax.slice_in_dim(value, length - width, length, axis=dim)
        leading = lax.slice_in_dim(value, 0, width, axis=dim)
        before = lax.ppermute(last, axis, up)
        after = lax.ppermute(leading, axis, down)
        value = jnp.concatenate([before, value, after], axis=dim)
    return value


def laplace(source):
    center = source[:, 1:-1]
    total = source[:, 2:] + source[:, :-2] - 6.0 * center
    padded = jnp.pad(center, ((0, 0), (0, 0), (1, 1), (1, 1), (0, 0)))
    total = total + padded[:, :, 2:, 1:-1] + padded[:, :, :-2, 1:-1]
    total = total + padded[:, :, 1:-1, 2:] + padded[:, :, 1:-1, :-2]
    return total


def phase_turn(field, angle):
    cosv = jnp.cos(angle)[..., None]
    sinv = jnp.sin(angle)[..., None]
    return jnp.stack([cosv * field[0] + sinv * field[1], cosv * field[1] - sinv * field[0]])


def kinetic_body(field):
    running = field
    taylor_term = lax.optimization_barrier(field.astype(jnp.bfloat16))
    for order in range(1, TAYLOR + 1):
        widened = padded_2(taylor_term, (("space", 1),), 1)
        curvature = laplace(widened.astype(jnp.float32))
        factor = time_step / (2.0 * order)
        update = jnp.stack([-factor * curvature[1], factor * curvature[0]])
        running = running + update
        taylor_term = lax.optimization_barrier(update.astype(jnp.bfloat16))
    return running


def contract(left, right):
    return lax.dot_general(
        left, right, (((0,), (0,)), ((), ())), preferred_element_type=jnp.float32
    )


def select_owner(stacked, owner, domain_ids):
    picked = (domain_ids == owner).reshape((stacked.shape[0],) + (1,) * (stacked.ndim - 1))
    return jnp.sum(jnp.where(picked, stacked, 0.0), axis=0)


def shards(orbitals, initial, potential, external, occupation, coupling, neighbours, offsets):
    field = orbitals[0].astype(jnp.float32)
    start = initial[0]
    slab, rows_y, cols_z, orbit_count = field.shape[1:]
    angle = half_step * potential[0].reshape(slab, rows_y, cols_z)
    cells_total = slab * lax.axis_size("space") * rows_y * cols_z
    flat_start = start.reshape(-1, orbit_count)
    start_real = start[0].reshape(-1, orbit_count)
    start_imag = start[1].reshape(-1, orbit_count)
    shape_one = (slab, rows_y, cols_z, orbit_count)
    intersection = jnp.zeros((2, orbit_count, orbit_count), jnp.float32)
    for section in range(STEPS):
        field = phase_turn(field, angle)
        field = kinetic_body(field)
        field = phase_turn(field, angle)
        rounded = field.astype(jnp.bfloat16)
        over_real = contract(flat_start, rounded.reshape(-1, orbit_count))
        over_imag = contract(start_real, rounded[1].reshape(-1, orbit_count)) - contract(
            start_imag, rounded[0].reshape(-1, orbit_count)
        )
        partial_sum = jnp.stack([over_real, over_imag]) * (1.0 / cells_total)
        intersection = lax.psum(partial_sum, "space")
        mix_real = jnp.dot(coupling, intersection[0], precision=lax.Precision.HIGHEST).astype(
            jnp.bfloat16
        )
        mix_imag = jnp.dot(coupling, intersection[1], precision=lax.Precision.HIGHEST).astype(
            jnp.bfloat16
        )
        corr_real = jnp.dot(start_real, mix_real, preferred_element_type=jnp.float32) - jnp.dot(
            start_imag, mix_imag, preferred_element_type=jnp.float32
        )
        corr_imag = jnp.dot(start_real, mix_imag, preferred_element_type=jnp.float32) + jnp.dot(
            start_imag, mix_real, preferred_element_type=jnp.float32
        )
        field = field + time_step * jnp.stack(
            [corr_imag.reshape(shape_one), -corr_real.reshape(shape_one)]
        )
    density = jnp.sum(field * field * occupation, axis=(0, 4))
    domain_count = neighbours.shape[0]
    domain_ids = jnp.arange(domain_count, dtype=jnp.int32)
    own_index = lax.axis_index("dom")

    def lookup(column, index):
        return jnp.sum(jnp.where(domain_ids == index, column, 0))

    lower_owner = lookup(neighbours[:, 0], own_index)
    upper_owner = lookup(neighbours[:, 1], own_index)
    gathered = lax.all_gather(density.reshape(1, slab, rows_y * cols_z), "dom", axis=0, tiled=True)
    lower_slab = select_owner(gathered, lower_owner, domain_ids).reshape(slab, rows_y, cols_z)
    upper_slab = select_owner(gathered, upper_owner, domain_ids).reshape(slab, rows_y, cols_z)
    lower_brick = lax.dynamic_slice_in_dim(lower_slab, lookup(offsets[:, 0], own_index), BUF, 1)
    upper_brick = lax.dynamic_slice_in_dim(upper_slab, lookup(offsets[:, 1], own_index), BUF, 1)
    planes = jnp.arange(BUF, dtype=jnp.float32)
    weight_low = ((planes + 1.0) / (BUF + 1.0)).reshape(1, BUF, 1)
    weight_high = ((BUF - planes) / (BUF + 1.0)).reshape(1, BUF, 1)
    low = density[:, :BUF] * weight_low + lower_brick * (1.0 - weight_low)
    high = density[:, rows_y - BUF :] * weight_high + upper_brick * (1.0 - weight_high)
    blended = jnp.concatenate([low, density[:, BUF : rows_y - BUF], high], axis=1)
    new_grid = external[0].reshape(slab, rows_y, cols_z) - xc_factor * jnp.cbrt(blended + 1e-06)
    evolved = phase_turn(field, half_step * new_grid).astype(jnp.bfloat16)
    return (evolved[None], intersection[None], new_grid.reshape(1, slab, rows_y * cols_z))


def solution(mesh):
    return jax.shard_map(
        shards,
        mesh=mesh,
        in_specs=(
            P("dom", None, "space", None, None, None),
            P("dom", None, "space", None, None, None),
            P("dom", "space", None),
            P("dom", "space", None),
            P(),
            P(),
            P(),
            P(),
        ),
        out_specs=(
            P("dom", None, "space", None, None, None),
            P("dom", None, None, None),
            P("dom", "space", None),
        ),
        check_vma=False,
    )
```

profile of v0, /device:TPU:1, one launch (start us, length us, event | category | flops | bytes accessed | tf_op | source)
XLA Modules:
  0.0 693.3 jit_solution(5470068621964557350)
XLA Ops:
  7.2 0.7 multiply_cosine_fusion
  8.1 1.0 convert_element_type.111
  9.1 0.2 multiply_add_fusion.3
  9.4 4.4 collective-permute-start
  13.8 1.3 collective-permute-start.1
  15.1 3.9 collective-permute-done.1
  19.1 0.2 fusion.11
  19.4 3.8 collective-permute-start.2
  23.2 1.3 collective-permute-start.3
  24.5 4.8 collective-permute-done.3
  29.5 0.2 fusion.15
  29.8 4.6 collective-permute-start.4
  34.3 1.3 collective-permute-start.5
  35.7 3.7 collective-permute-done.5
  39.5 0.2 fusion.19
  39.8 4.0 collective-permute-start.6
  43.8 1.3 collective-permute-start.7
  45.2 3.9 collective-permute-done.7
  49.2 0.2 fusion.23
  49.6 0.2 multiply_add_fusion.2
  49.9 0.2 fusion.84
  50.1 0.3 convolution_bitcast_fusion.1
  50.4 0.2 fusion.7
  50.7 0.7 maximum_multiply_fusion.2
  51.4 268.0 %all-reduce.11.cloned.1.call-done = f32[2,128,128]{1,2,0:T(8,128)} async-done(((f32[2,128,128]{1,2,0:T(8,128)}), f32[2,128,128]{1,2,0:T(8,128)}) %all-reduce.11.cloned.1.call-update) | async-done | bytes 131088 | tf_op jit(solution)/shard_map/psum | solution.py:89
  319.4 1.1 convolution_convert_fusion.3
  320.7 1.1 convolution_convert_fusion.2
  321.8 0.2 fusion.86
  322.0 0.2 fusion.5
  322.3 0.2 fusion.4
  322.7 0.2 multiply_add_fusion.1
  323.0 3.2 collective-permute-start.8
  326.2 1.3 collective-permute-start.9
  327.5 4.1 collective-permute-done.9
  331.7 0.2 fusion.27
  332.0 1.5 collective-permute-start.10
  333.6 1.3 collective-permute-start.11
  334.9 0.7 fusion.70
  335.6 3.0 collective-permute-done.11
  338.7 0.2 fusion.31
  339.0 2.3 collective-permute-start.12
  341.3 1.3 collective-permute-start.13
  342.7 3.7 collective-permute-done.13
  346.4 0.2 fusion.35
  346.8 3.4 collective-permute-start.14
  350.1 1.3 collective-permute-start.15
  351.4 0.7 iota_compare_fusion
  352.1 3.4 collective-permute-done.15
  355.6 0.2 fusion.39
  356.1 0.2 multiply_add_fusion
  356.4 0.2 fusion.87
  356.6 0.3 convolution_bitcast_fusion
  356.9 0.2 fusion.6
  357.1 0.7 maximum_multiply_fusion.3
  357.8 0.6 iota_compare_fusion.2
  362.4 281.4 %all-reduce.13.cloned.1.call-done = f32[2,128,128]{1,2,0:T(8,128)} async-done(((f32[2,128,128]{1,2,0:T(8,128)}), f32[2,128,128]{1,2,0:T(8,128)}) %all-reduce.13.cloned.1.call-update) | async-done | bytes 131088 | tf_op jit(solution)/shard_map/psum | solution.py:89
  643.8 1.1 convolution_convert_fusion.1
  645.1 1.1 convolution_convert_fusion
  646.8 0.2 fusion.1
  647.6 36.0 %all_gather.3 = f32[16,4,128]{2,1,0:T(4,128)S(1)} all-gather(f32[1,4,128]{2,1,0:T(4,128)S(1)} %reshape.209), channel_id=1, replica_groups=mesh['dom'=16,'space'=32] {'dom'}, dimensions={0}, use_global_device_ids=true | all-gather | bytes 34816 | tf_op jit(solution)/shard_map/all_gather | solution.py:115
  684.2 0.6 sub.128
  684.8 0.8 copy.25
  685.5 0.2 fusion.60
  685.8 0.7 pad_maximum_fusion.10
  (96 shorter events, 4.8 us)
Async XLA Ops:
  7.2 312.2 %copy-start = (f32[128,128]{1,0:T(8,128)S(1)}, f32[128,128]{1,0:T(8,128)}, u32[]{:S(2)}) copy-start(f32[128,128]{1,0:T(8,128)} %param.13) | copy-start | bytes 196612
  7.2 312.2 %all-reduce.11.cloned.1.call-start = ((), (), s32[]{:S(2)}) async-start(), calls=%async_computation | async-start | bytes 262144 | tf_op jit(solution)/shard_map/psum | solution.py:89
  9.4 5.7 collective-permute-start
  13.8 5.2 collective-permute-start.1
  19.4 5.2 collective-permute-start.2
  23.2 6.1 collective-permute-start.3
  29.8 5.9 collective-permute-start.4
  34.3 5.0 collective-permute-start.5
  39.7 5.4 copy-start.1
  39.8 5.3 collective-permute-start.6
  43.8 5.3 collective-permute-start.7
  51.3 592.5 %all-reduce.13.cloned.1.call-start = ((), (), s32[]{:S(2)}) async-start(), calls=%async_computation.1 | async-start | bytes 262144 | tf_op jit(solution)/shard_map/psum | solution.py:89
  323.0 4.5 collective-permute-start.8
  326.2 5.4 collective-permute-start.9
  332.0 2.9 copy-start.4
  332.0 2.9 copy-start.5
  332.0 3.5 collective-permute-start.10
  333.6 5.0 collective-permute-start.11
  339.0 3.6 collective-permute-start.12
  341.3 5.0 collective-permute-start.13
  346.8 5.3 collective-permute-start.14
  350.1 5.4 collective-permute-start.15
  356.3 4.6 copy-start.3
  646.6 0.7 copy-start.6
  647.3 37.5 %copy-start.2 = (f32[2,128,128]{1,2,0:T(8,128)S(1)}, f32[2,128,128]{1,2,0:T(8,128)}, u32[]{:S(2)}) copy-start(f32[2,128,128]{1,2,0:T(8,128)} %all-reduce.13.cloned.1.call-done) | copy-start | bytes 393220
Sparse Core Ops, SparseCore 0:
  51.5 267.8 all-reduce.10
  357.9 285.8 all-reduce.12
where the time goes:
time: 694 us; the launch traced here: 693 us
  waiting for transfers between devices  580 us (84%)
  starting transfers between devices  37.6 us (5%)
  blocking collectives  36 us (5%)
  between operations  18.8 us (3%)
  other arithmetic  11 us (2%)
  matrix products  7.38 us (1%)
    psum x2, waiting for transfers between devices, shards(): intersection = lax.psum(partial_sum, 'space')  549 us
    all_gather x1, blocking collectives, shards(): lax.all_gather(density.reshape(1, slab, rows_y * cols_z), 'dom', axis=0,...  36 us
    ppermute x8, waiting for transfers between devices, padded_2(): after = lax.ppermute(leading, axis, down)  30.5 us
    ppermute x8, starting transfers between devices, padded_2(): before = lax.ppermute(last, axis, up)  27.2 us
  transfers between devices with their start and end apart: 18, of which 10 were waited for; matrix products, arithmetic and copies ran while one was open for 0% of the time, Pallas kernels for 0%

commit v1 on v0

v1 whole, which is shorter than its diff:
```python
import jax
import jax.numpy as jnp
from jax import lax
from jax.sharding import PartitionSpec as P

TAYLOR = 4
BUF = 4

time_step = 0.4
half_step = 0.2
xc_factor = 0.9847450218426965


def halo(value, axis):
    devices = lax.axis_size(axis)
    up = [(i, i + 1) for i in range(devices - 1)]
    down = [(i + 1, i) for i in range(devices - 1)]
    before = lax.ppermute(value, axis, up)
    after = lax.ppermute(value, axis, down)
    return jnp.concatenate([before, value, after], axis=1)


def laplace(source):
    center = source[:, 1:-1]
    total = source[:, 2:] + source[:, :-2] - 6.0 * center
    padded = jnp.pad(center, ((0, 0), (0, 0), (1, 1), (1, 1), (0, 0)))
    total = total + padded[:, :, 2:, 1:-1] + padded[:, :, :-2, 1:-1]
    total = total + padded[:, :, 1:-1, 2:] + padded[:, :, 1:-1, :-2]
    return total


def phase_turn(field, angle):
    cosv = jnp.cos(angle)[..., None]
    sinv = jnp.sin(angle)[..., None]
    return jnp.stack([cosv * field[0] + sinv * field[1], cosv * field[1] - sinv * field[0]])


def kinetic_body(field, wide, inside):
    slab = field.shape[1]
    running = field
    term = wide
    for order in range(1, TAYLOR + 1):
        curvature = laplace(term.astype(jnp.float32))
        factor = time_step / (2.0 * order)
        keep = inside[order : inside.shape[0] - order].reshape(-1, 1, 1, 1) * factor
        update = jnp.stack([-keep * curvature[1], keep * curvature[0]])
        skip = (update.shape[1] - slab) // 2
        running = running + update[:, skip : skip + slab]
        term = lax.optimization_barrier(update.astype(jnp.bfloat16))
    return running


def contract(left, right):
    return lax.dot_general(
        left, right, (((0,), (0,)), ((), ())), preferred_element_type=jnp.float32
    )


def overlap(start_real, start_imag, rounded):
    orbits = start_real.shape[-1]
    real = rounded[0].reshape(-1, orbits)
    imag = rounded[1].reshape(-1, orbits)
    over_real = contract(start_real, real) + contract(start_imag, imag)
    over_imag = contract(start_real, imag) - contract(start_imag, real)
    return jnp.stack([over_real, over_imag])


def space_sum(partial, axis):
    devices = lax.axis_size(axis)
    parts = lax.all_to_all(partial.astype(jnp.bfloat16), axis, 0, 0, tiled=True)
    rows = partial.shape[0] // devices
    mine = jnp.sum(parts.reshape(devices, rows, -1).astype(jnp.float32), axis=0)
    spread = jnp.broadcast_to(mine.astype(jnp.bfloat16)[None], (devices,) + mine.shape)
    return lax.all_to_all(lax.optimization_barrier(spread), axis, 0, 0, tiled=True)


def high_dot(left, right):
    return jnp.dot(left, right, precision=lax.Precision.HIGHEST)


def half_dot(left, right):
    return jnp.dot(left, right, preferred_element_type=jnp.float32)


def select_owner(stacked, owner, domain_ids):
    picked = (domain_ids == owner).reshape((stacked.shape[0],) + (1,) * (stacked.ndim - 1))
    return jnp.sum(jnp.where(picked, stacked, 0.0), axis=0)


def shards(orbitals, initial, potential, external, occupation, coupling, neighbours, offsets):
    start = initial[0]
    slab, rows_y, cols_z, orbits = start.shape[1:]
    devices = lax.axis_size("space")
    place = lax.axis_index("space")
    angle = half_step * potential[0].reshape(slab, rows_y, cols_z)
    cells_total = slab * devices * rows_y * cols_z
    shape_one = (slab, rows_y, cols_z, orbits)
    start_real = start[0].reshape(-1, orbits)
    start_imag = start[1].reshape(-1, orbits)
    low_in = jnp.full((slab,), jnp.where(place > 0, 1.0, 0.0), jnp.float32)
    high_in = jnp.full((slab,), jnp.where(place < devices - 1, 1.0, 0.0), jnp.float32)
    inside = jnp.concatenate([low_in, jnp.ones((slab,), jnp.float32), high_in])

    turned = phase_turn(orbitals[0].astype(jnp.float32), angle)
    turned_start = phase_turn(start.astype(jnp.float32), angle)
    sent = lax.optimization_barrier(turned.astype(jnp.bfloat16))
    sent_start = lax.optimization_barrier(turned_start.astype(jnp.bfloat16))
    wide = halo(sent, "space")
    wide_start = halo(sent_start, "space")
    first = phase_turn(kinetic_body(turned, wide, inside), angle)
    turned = phase_turn(first, angle)
    sent = lax.optimization_barrier(turned.astype(jnp.bfloat16))
    wide = halo(sent, "space")
    moved = phase_turn(kinetic_body(turned_start, wide_start, inside), angle).astype(jnp.bfloat16)
    moved = lax.optimization_barrier(moved)
    second = phase_turn(kinetic_body(turned, wide, inside), angle)

    partial = jnp.concatenate(
        [
            overlap(start_real, start_imag, first.astype(jnp.bfloat16)),
            overlap(start_real, start_imag, second.astype(jnp.bfloat16)),
            overlap(start_real, start_imag, moved),
        ]
    ) * (1.0 / cells_total)
    summed = space_sum(partial.reshape(-1, orbits), "space").reshape(6, orbits, orbits)
    wide_sum = summed.astype(jnp.float32)
    mix1_real = high_dot(coupling, wide_sum[0]).astype(jnp.bfloat16)
    mix1_imag = high_dot(coupling, wide_sum[1]).astype(jnp.bfloat16)
    gram_real, gram_imag = summed[4], summed[5]
    over_real = wide_sum[2] + time_step * (
        half_dot(gram_real, mix1_imag) + half_dot(gram_imag, mix1_real)
    )
    over_imag = wide_sum[3] - time_step * (
        half_dot(gram_real, mix1_real) - half_dot(gram_imag, mix1_imag)
    )
    intersection = jnp.stack([over_real, over_imag])
    mix2_real = high_dot(coupling, over_real).astype(jnp.bfloat16)
    mix2_imag = high_dot(coupling, over_imag).astype(jnp.bfloat16)
    moved_real = moved[0].reshape(-1, orbits)
    moved_imag = moved[1].reshape(-1, orbits)
    corr_real = (
        half_dot(moved_real, mix1_real)
        - half_dot(moved_imag, mix1_imag)
        + half_dot(start_real, mix2_real)
        - half_dot(start_imag, mix2_imag)
    )
    corr_imag = (
        half_dot(moved_real, mix1_imag)
        + half_dot(moved_imag, mix1_real)
        + half_dot(start_real, mix2_imag)
        + half_dot(start_imag, mix2_real)
    )
    field = second + time_step * jnp.stack(
        [corr_imag.reshape(shape_one), -corr_real.reshape(shape_one)]
    )

    density = jnp.sum(field * field * occupation, axis=(0, 4))
    domain_count = neighbours.shape[0]
    domain_ids = jnp.arange(domain_count, dtype=jnp.int32)
    own_index = lax.axis_index("dom")

    def lookup(column, index):
        return jnp.sum(jnp.where(domain_ids == index, column, 0))

    lower_owner = lookup(neighbours[:, 0], own_index)
    upper_owner = lookup(neighbours[:, 1], own_index)
    flat = density.reshape(1, slab, rows_y * cols_z)
    gathered = lax.all_to_all(
        jnp.broadcast_to(flat, (domain_count,) + flat.shape[1:]), "dom", 0, 0, tiled=True
    )
    lower_slab = select_owner(gathered, lower_owner, domain_ids).reshape(slab, rows_y, cols_z)
    upper_slab = select_owner(gathered, upper_owner, domain_ids).reshape(slab, rows_y, cols_z)
    lower_brick = lax.dynamic_slice_in_dim(lower_slab, lookup(offsets[:, 0], own_index), BUF, 1)
    upper_brick = lax.dynamic_slice_in_dim(upper_slab, lookup(offsets[:, 1], own_index), BUF, 1)
    planes = jnp.arange(BUF, dtype=jnp.float32)
    weight_low = ((planes + 1.0) / (BUF + 1.0)).reshape(1, BUF, 1)
    weight_high = ((BUF - planes) / (BUF + 1.0)).reshape(1, BUF, 1)
    low = density[:, :BUF] * weight_low + lower_brick * (1.0 - weight_low)
    high = density[:, rows_y - BUF :] * weight_high + upper_brick * (1.0 - weight_high)
    blended = jnp.concatenate([low, density[:, BUF : rows_y - BUF], high], axis=1)
    new_grid = external[0].reshape(slab, rows_y, cols_z) - xc_factor * jnp.cbrt(blended + 1e-06)
    evolved = phase_turn(field, half_step * new_grid).astype(jnp.bfloat16)
    return (evolved[None], intersection[None], new_grid.reshape(1, slab, rows_y * cols_z))


def solution(mesh):
    return jax.shard_map(
        shards,
        mesh=mesh,
        in_specs=(
            P("dom", None, "space", None, None, None),
            P("dom", None, "space", None, None, None),
            P("dom", "space", None),
            P("dom", "space", None),
            P(),
            P(),
            P(),
            P(),
        ),
        out_specs=(
            P("dom", None, "space", None, None, None),
            P("dom", None, None, None),
            P("dom", "space", None),
        ),
        check_vma=False,
    )
```

time: 694 us -> 126 us (0.18)
  waiting for transfers between devices: 580 us -> 28.3 us
  between operations: 18.8 us -> 5.48 us
    psum x2 -> x0, waiting for transfers between devices: 549 us -> none  [shards(): intersection = lax.psum(partial_sum, 'space')]
    all_gather x1 -> x0, blocking collectives: 36 us -> none  [shards(): lax.all_gather(density.reshape(1, slab, rows_y * cols_z), 'dom', axis=0,...]
    all_to_all x0 -> x1, blocking collectives: none -> 32.6 us  [space_sum(): parts = lax.all_to_all(partial.astype(jnp.bfloat16), axis, 0, 0, tiled=True)]
    ppermute x16 -> x6, starting transfers between devices: 37.5 us -> 17.7 us  [the longest x3 13.8 us: halo(): before = lax.ppermute(value, axis, up)]
    ppermute x16 -> x6, waiting for transfers between devices: 30.6 us -> 12 us  [the longest x3 8.95 us: halo(): after = lax.ppermute(value, axis, down)]
    all_to_all x0 -> x2, waiting for transfers between devices: none -> 16.3 us  [the longest x1 11.2 us: space_sum(): lax.all_to_all(lax.optimization_barrier(spread), axis, 0, 0, tiled=True)]
    all_to_all x0 -> x2, starting transfers between devices: none -> 15.4 us  [the longest x1 10.4 us: shards(): lax.all_to_all(jnp.broadcast_to(flat, (domain_count,) + flat.shape[1:]),...]
  transfers between devices with their start and end apart: 18 -> 8, of which waited for: 10 -> 7; matrix products, arithmetic and copies ran while one was open for 0% -> 4% of each run, Pallas kernels for 0% -> 0%
where the time goes in v1:
time: 126 us; the launch traced here: 125 us
  starting transfers between devices  33.1 us (26%)
  blocking collectives  32.6 us (26%)
  waiting for transfers between devices  28.3 us (22%)
  other arithmetic  16.3 us (13%)
  matrix products  5.94 us (5%)
  between operations  5.48 us (4%)
  local copies, waits for them, and re-layouts  3.24 us (3%)
    all_to_all x1, blocking collectives, space_sum(): parts = lax.all_to_all(partial.astype(jnp.bfloat16), axis, 0, 0, tiled=True)  32.6 us
    ppermute x3, starting transfers between devices, halo(): before = lax.ppermute(value, axis, up)  13.8 us
    all_to_all x1, waiting for transfers between devices, space_sum(): lax.all_to_all(lax.optimization_barrier(spread), axis, 0, 0, tiled=True)  11.2 us
    all_to_all x1, starting transfers between devices, shards(): lax.all_to_all(jnp.broadcast_to(flat, (domain_count,) + flat.shape[1:]),...  10.4 us
    ppermute x3, waiting for transfers between devices, halo(): after = lax.ppermute(value, axis, down)  8.95 us
    all_to_all x1, waiting for transfers between devices, shards(): lax.all_to_all(jnp.broadcast_to(flat, (domain_count,) + flat.shape[1:]),...  5.13 us
    all_to_all x1, starting transfers between devices, space_sum(): lax.all_to_all(lax.optimization_barrier(spread), axis, 0, 0, tiled=True)  5.01 us
    add x12, other arithmetic, laplace(): total = total + padded[:, :, 1:-1, 2:] + padded[:, :, 1:-1, :-2]  3.95 us
  transfers between devices with their start and end apart: 8, of which 7 were waited for; matrix products, arithmetic and copies ran while one was open for 4% of the time, Pallas kernels for 0%

profile of v1, /device:TPU:1, one launch (start us, length us, event | category | flops | bytes accessed | tf_op | source)
XLA Modules:
  0.0 125.0 jit_solution(14235769528757427878)
XLA Ops:
  0.6 0.8 multiply_cosine_fusion
  1.6 1.0 convert_element_type.137
  2.6 1.0 convert_element_type.154
  3.6 0.2 multiply_add_fusion
  3.9 4.5 %collective-permute-start.4 = (bf16[2,4,16,8,128]{4,3,2,1,0:T(8,128)(2,1)S(1)}, bf16[2,4,16,8,128]{4,3,2,1,0:T(8,128)(2,1)S(1)}, u32[]{:S(2)}, u32[]{:S(2)}) collective-permute-start(bf16[2,4,16,8,128]{4,3,2,1,0:T(8,128)(2,1)S(1)} %fusion.112), channel_id=1, source_target_pairs={{0,1},{1,2},{2,3},{3,4},{4,5},{5,6},{6,7},{7,8},{8,9},{9,10},{10,1... | collective-permute-start | bytes 786440 | tf_op jit(solution)/shard_map/ppermute | solution.py:18
  8.4 1.3 %collective-permute-start.5 = (bf16[2,4,16,8,128]{4,3,2,1,0:T(8,128)(2,1)S(1)}, bf16[2,4,16,8,128]{4,3,2,1,0:T(8,128)(2,1)S(1)}, u32[]{:S(2)}, u32[]{:S(2)}) collective-permute-start(bf16[2,4,16,8,128]{4,3,2,1,0:T(8,128)(2,1)S(1)} %fusion.112), channel_id=1, source_target_pairs={{1,0},{2,1},{3,2},{4,3},{5,4},{6,5},{7,6},{8,7},{9,8},{10,9},{11,1... | collective-permute-start | bytes 786440 | tf_op jit(solution)/shard_map/ppermute | solution.py:19
  9.7 4.2 %collective-permute-start = (bf16[2,4,16,8,128]{4,3,2,1,0:T(8,128)(2,1)S(1)}, bf16[2,4,16,8,128]{4,3,2,1,0:T(8,128)(2,1)S(1)}, u32[]{:S(2)}, u32[]{:S(2)}) collective-permute-start(bf16[2,4,16,8,128]{4,3,2,1,0:T(8,128)(2,1)S(1)} %fusion.115), channel_id=1, source_target_pairs={{0,1},{1,2},{2,3},{3,4},{4,5},{5,6},{6,7},{7,8},{8,9},{9,10},{10,1... | collective-permute-start | bytes 786440 | tf_op jit(solution)/shard_map/ppermute | solution.py:18
  13.9 1.3 %collective-permute-start.1 = (bf16[2,4,16,8,128]{4,3,2,1,0:T(8,128)(2,1)S(1)}, bf16[2,4,16,8,128]{4,3,2,1,0:T(8,128)(2,1)S(1)}, u32[]{:S(2)}, u32[]{:S(2)}) collective-permute-start(bf16[2,4,16,8,128]{4,3,2,1,0:T(8,128)(2,1)S(1)} %fusion.115), channel_id=1, source_target_pairs={{1,0},{2,1},{3,2},{4,3},{5,4},{6,5},{7,6},{8,7},{9,8},{10,9},{11,1... | collective-permute-start | bytes 786440 | tf_op jit(solution)/shard_map/ppermute | solution.py:19
  15.9 0.5 fusion.14
  16.4 2.0 %collective-permute-done = bf16[2,4,16,8,128]{4,3,2,1,0:T(8,128)(2,1)S(1)} collective-permute-done((bf16[2,4,16,8,128]{4,3,2,1,0:T(8,128)(2,1)S(1)}, bf16[2,4,16,8,128]{4,3,2,1,0:T(8,128)(2,1)S(1)}, u32[]{:S(2)}, u32[]{:S(2)}) %collective-permute-start) | collective-permute-done | bytes 262176 | tf_op jit(solution)/shard_map/ppermute | solution.py:18
  18.4 4.1 %collective-permute-done.1 = bf16[2,4,16,8,128]{4,3,2,1,0:T(8,128)(2,1)S(1)} collective-permute-done((bf16[2,4,16,8,128]{4,3,2,1,0:T(8,128)(2,1)S(1)}, bf16[2,4,16,8,128]{4,3,2,1,0:T(8,128)(2,1)S(1)}, u32[]{:S(2)}, u32[]{:S(2)}) %collective-permute-start.1) | collective-permute-done | bytes 262176 | tf_op jit(solution)/shard_map/ppermute | solution.py:19
  22.8 0.5 fusion.6
  23.2 0.3 slice_multiply_fusion.5
  24.3 0.4 fusion.53
  24.6 0.4 fusion.45
  25.0 0.3 slice_multiply_fusion.11
  25.8 0.3 fusion.71
  26.1 0.3 fusion.63
  26.4 0.2 slice_multiply_fusion.16
  27.5 0.2 fusion.83
  27.8 0.3 add_convert_fusion.1
  28.2 5.1 %collective-permute-start.2 = (bf16[2,4,16,8,128]{4,3,2,1,0:T(8,128)(2,1)S(1)}, bf16[2,4,16,8,128]{4,3,2,1,0:T(8,128)(2,1)S(1)}, u32[]{:S(2)}, u32[]{:S(2)}) collective-permute-start(bf16[2,4,16,8,128]{4,3,2,1,0:T(8,128)(2,1)S(1)} %fusion.114), channel_id=1, source_target_pairs={{0,1},{1,2},{2,3},{3,4},{4,5},{5,6},{6,7},{7,8},{8,9},{9,10},{10,1... | collective-permute-start | bytes 786440 | tf_op jit(solution)/shard_map/ppermute | solution.py:18
  33.3 1.3 %collective-permute-start.3 = (bf16[2,4,16,8,128]{4,3,2,1,0:T(8,128)(2,1)S(1)}, bf16[2,4,16,8,128]{4,3,2,1,0:T(8,128)(2,1)S(1)}, u32[]{:S(2)}, u32[]{:S(2)}) collective-permute-start(bf16[2,4,16,8,128]{4,3,2,1,0:T(8,128)(2,1)S(1)} %fusion.114), channel_id=1, source_target_pairs={{1,0},{2,1},{3,2},{4,3},{5,4},{6,5},{7,6},{8,7},{9,8},{10,9},{11,1... | collective-permute-start | bytes 786440 | tf_op jit(solution)/shard_map/ppermute | solution.py:19
  34.7 0.2 fusion.143
  34.9 0.2 fusion.139
  35.1 0.2 fusion.140
  35.4 0.2 fusion.38
  35.6 0.2 fusion.144
  35.8 0.2 fusion.36
  36.1 1.0 collective-permute-done.2
  37.1 4.8 %collective-permute-done.3 = bf16[2,4,16,8,128]{4,3,2,1,0:T(8,128)(2,1)S(1)} collective-permute-done((bf16[2,4,16,8,128]{4,3,2,1,0:T(8,128)(2,1)S(1)}, bf16[2,4,16,8,128]{4,3,2,1,0:T(8,128)(2,1)S(1)}, u32[]{:S(2)}, u32[]{:S(2)}) %collective-permute-start.3) | collective-permute-done | bytes 262176 | tf_op jit(solution)/shard_map/ppermute | solution.py:19
  42.1 0.5 fusion.10
  43.1 0.4 fusion.49
  43.9 0.3 fusion.67
  44.9 0.2 multiply_add_fusion.1
  45.2 0.2 fusion.141
  45.4 0.2 fusion.142
  45.6 0.2 fusion.34
  45.9 0.2 fusion.32
  46.2 0.2 fusion.30
  46.4 0.2 fusion.28
  46.7 32.6 %all_to_all.16 = bf16[32,24,128]{2,1,0:T(8,128)(2,1)S(1)} all-to-all(bf16[32,24,128]{2,1,0:T(8,128)(2,1)S(1)} %bitcast.217), channel_id=1, replica_groups=mesh['dom'=16,'space'=32] {'space'}, dimensions={0} | all-to-all | bytes 393216 | tf_op jit(solution)/shard_map/all_to_all | solution.py:70
  79.3 0.7 broadcast_in_dim.65
  80.0 5.0 %all-to-all-start.1 = ((bf16[32,24,128]{2,1,0:T(8,128)(2,1)}), bf16[32,24,128]{2,1,0:T(8,128)(2,1)S(1)}, u32[]{:S(2)}, u32[]{:S(2)}) async-start(bf16[32,24,128]{2,1,0:T(8,128)(2,1)} %broadcast_in_dim.65), calls=%async_computation.1 | async-start | bytes 393216 | tf_op jit(solution)/shard_map/all_to_all | solution.py:74
  85.1 0.7 fusion.128
  89.7 0.6 iota_compare_fusion
  90.3 0.6 iota_compare_fusion.2
  91.0 11.2 %all-to-all-done.1 = bf16[32,24,128]{2,1,0:T(8,128)(2,1)S(1)} async-done(((bf16[32,24,128]{2,1,0:T(8,128)(2,1)}), bf16[32,24,128]{2,1,0:T(8,128)(2,1)S(1)}, u32[]{:S(2)}, u32[]{:S(2)}) %all-to-all-start.1) | async-done | bytes 196640 | tf_op jit(solution)/shard_map/all_to_all | solution.py:74
  102.2 0.2 convolution_convert_fusion.3
  102.5 0.2 convolution_convert_fusion.2
  102.8 0.2 fusion.145
  103.2 0.2 fusion.146
  103.6 0.3 convolution_convert_fusion
  104.4 0.3 convolution_convert_fusion.1
  105.1 0.2 fusion.22
  105.3 0.2 fusion.20
  105.5 0.2 copy-done.5
  106.0 0.6 broadcast_in_dim.69
  106.6 10.4 %all-to-all-start.2 = ((f32[16,4,128]{2,1,0:T(4,128)}), f32[16,4,128]{2,1,0:T(4,128)S(1)}, u32[]{:S(2)}, u32[]{:S(2)}) async-start(f32[16,4,128]{2,1,0:T(4,128)} %broadcast_in_dim.69), calls=%async_computation.2 | async-start | bytes 65536 | tf_op jit(solution)/shard_map/all_to_all | solution.py:168
  117.0 0.7 maximum_bitcast_fusion
  117.7 5.1 %all-to-all-done.2 = f32[16,4,128]{2,1,0:T(4,128)S(1)} async-done(((f32[16,4,128]{2,1,0:T(4,128)}), f32[16,4,128]{2,1,0:T(4,128)S(1)}, u32[]{:S(2)}, u32[]{:S(2)}) %all-to-all-start.2) | async-done | bytes 32800 | tf_op jit(solution)/shard_map/all_to_all | solution.py:168
  123.5 0.6 sub.170
  124.1 0.2 fusion.116
  124.3 0.7 pad_maximum_fusion.14
  (96 shorter events, 7.5 us)
Async XLA Ops:
  0.6 101.6 %copy-start = (f32[128,128]{1,0:T(8,128)S(1)}, f32[128,128]{1,0:T(8,128)}, u32[]{:S(2)}) copy-start(f32[128,128]{1,0:T(8,128)} %param.13) | copy-start | bytes 196612
  3.8 11.7 %copy-start.1 = (bf16[1,2,4,16,8,128]{5,4,3,2,1,0:T(8,128)(2,1)S(1)}, bf16[1,2,4,16,8,128]{5,4,3,2,1,0:T(8,128)(2,1)}, u32[]{:S(2)}) copy-start(bf16[1,2,4,16,8,128]{5,4,3,2,1,0:T(8,128)(2,1)} %param.9) | copy-start | bytes 786436
  3.9 11.7 %collective-permute-start.4 = (bf16[2,4,16,8,128]{4,3,2,1,0:T(8,128)(2,1)S(1)}, bf16[2,4,16,8,128]{4,3,2,1,0:T(8,128)(2,1)S(1)}, u32[]{:S(2)}, u32[]{:S(2)}) collective-permute-start(bf16[2,4,16,8,128]{4,3,2,1,0:T(8,128)(2,1)S(1)} %fusion.112), channel_id=1, source_target_pairs={{0,1},{1,2},{2,3},{3,4},{4,5},{5,6},{6,7},{7,8},{8,9},{9,10},{10,1... | collective-permute-start | bytes 786440 | tf_op jit(solution)/shard_map/ppermute | solution.py:18
  8.4 7.3 %collective-permute-start.5 = (bf16[2,4,16,8,128]{4,3,2,1,0:T(8,128)(2,1)S(1)}, bf16[2,4,16,8,128]{4,3,2,1,0:T(8,128)(2,1)S(1)}, u32[]{:S(2)}, u32[]{:S(2)}) collective-permute-start(bf16[2,4,16,8,128]{4,3,2,1,0:T(8,128)(2,1)S(1)} %fusion.112), channel_id=1, source_target_pairs={{1,0},{2,1},{3,2},{4,3},{5,4},{6,5},{7,6},{8,7},{9,8},{10,9},{11,1... | collective-permute-start | bytes 786440 | tf_op jit(solution)/shard_map/ppermute | solution.py:19
  9.7 8.7 %collective-permute-start = (bf16[2,4,16,8,128]{4,3,2,1,0:T(8,128)(2,1)S(1)}, bf16[2,4,16,8,128]{4,3,2,1,0:T(8,128)(2,1)S(1)}, u32[]{:S(2)}, u32[]{:S(2)}) collective-permute-start(bf16[2,4,16,8,128]{4,3,2,1,0:T(8,128)(2,1)S(1)} %fusion.115), channel_id=1, source_target_pairs={{0,1},{1,2},{2,3},{3,4},{4,5},{5,6},{6,7},{7,8},{8,9},{9,10},{10,1... | collective-permute-start | bytes 786440 | tf_op jit(solution)/shard_map/ppermute | solution.py:18
  13.9 8.6 %collective-permute-start.1 = (bf16[2,4,16,8,128]{4,3,2,1,0:T(8,128)(2,1)S(1)}, bf16[2,4,16,8,128]{4,3,2,1,0:T(8,128)(2,1)S(1)}, u32[]{:S(2)}, u32[]{:S(2)}) collective-permute-start(bf16[2,4,16,8,128]{4,3,2,1,0:T(8,128)(2,1)S(1)} %fusion.115), channel_id=1, source_target_pairs={{1,0},{2,1},{3,2},{4,3},{5,4},{6,5},{7,6},{8,7},{9,8},{10,9},{11,1... | collective-permute-start | bytes 786440 | tf_op jit(solution)/shard_map/ppermute | solution.py:19
  28.2 8.9 %collective-permute-start.2 = (bf16[2,4,16,8,128]{4,3,2,1,0:T(8,128)(2,1)S(1)}, bf16[2,4,16,8,128]{4,3,2,1,0:T(8,128)(2,1)S(1)}, u32[]{:S(2)}, u32[]{:S(2)}) collective-permute-start(bf16[2,4,16,8,128]{4,3,2,1,0:T(8,128)(2,1)S(1)} %fusion.114), channel_id=1, source_target_pairs={{0,1},{1,2},{2,3},{3,4},{4,5},{5,6},{6,7},{7,8},{8,9},{9,10},{10,1... | collective-permute-start | bytes 786440 | tf_op jit(solution)/shard_map/ppermute | solution.py:18
  33.3 8.6 %collective-permute-start.3 = (bf16[2,4,16,8,128]{4,3,2,1,0:T(8,128)(2,1)S(1)}, bf16[2,4,16,8,128]{4,3,2,1,0:T(8,128)(2,1)S(1)}, u32[]{:S(2)}, u32[]{:S(2)}) collective-permute-start(bf16[2,4,16,8,128]{4,3,2,1,0:T(8,128)(2,1)S(1)} %fusion.114), channel_id=1, source_target_pairs={{1,0},{2,1},{3,2},{4,3},{5,4},{6,5},{7,6},{8,7},{9,8},{10,9},{11,1... | collective-permute-start | bytes 786440 | tf_op jit(solution)/shard_map/ppermute | solution.py:19
  46.1 38.9 %copy-start.3 = (s32[16,2]{0,1:T(2,128)S(1)}, s32[16,2]{0,1:T(2,128)}, u32[]{:S(2)}) copy-start(s32[16,2]{0,1:T(2,128)} %param.15) | copy-start | bytes 388
  46.1 38.9 %copy-start.4 = (s32[16,2]{0,1:T(2,128)S(1)}, s32[16,2]{0,1:T(2,128)}, u32[]{:S(2)}) copy-start(s32[16,2]{0,1:T(2,128)} %param.14) | copy-start | bytes 388
  46.1 42.2 %copy-start.2 = (f32[1,4,128]{2,1,0:T(4,128)S(1)}, f32[1,4,128]{2,1,0:T(4,128)}, u32[]{:S(2)}) copy-start(f32[1,4,128]{2,1,0:T(4,128)} %param.11) | copy-start | bytes 6148
  80.0 22.1 %all-to-all-start.1 = ((bf16[32,24,128]{2,1,0:T(8,128)(2,1)}), bf16[32,24,128]{2,1,0:T(8,128)(2,1)S(1)}, u32[]{:S(2)}, u32[]{:S(2)}) async-start(bf16[32,24,128]{2,1,0:T(8,128)(2,1)} %broadcast_in_dim.65), calls=%async_computation.1 | async-start | bytes 393216 | tf_op jit(solution)/shard_map/all_to_all | solution.py:74
  105.1 0.7 copy-start.5
  106.6 16.2 %all-to-all-start.2 = ((f32[16,4,128]{2,1,0:T(4,128)}), f32[16,4,128]{2,1,0:T(4,128)S(1)}, u32[]{:S(2)}, u32[]{:S(2)}) async-start(f32[16,4,128]{2,1,0:T(4,128)} %broadcast_in_dim.69), calls=%async_computation.2 | async-start | bytes 65536 | tf_op jit(solution)/shard_map/all_to_all | solution.py:168

commit v2 on v1

--- a/solution.py
+++ b/solution.py
@@ -5,39 +5,49 @@
 
 TAYLOR = 4
 BUF = 4
+NEAR = 4
 
 time_step = 0.4
 half_step = 0.2
 xc_factor = 0.9847450218426965
 
 
-def halo(value, axis):
+def neighbour_pair(value, axis):
     devices = lax.axis_size(axis)
     up = [(i, i + 1) for i in range(devices - 1)]
     down = [(i + 1, i) for i in range(devices - 1)]
-    before = lax.ppermute(value, axis, up)
-    after = lax.ppermute(value, axis, down)
-    return jnp.concatenate([before, value, after], axis=1)
+    return lax.ppermute(value, axis, up), lax.ppermute(value, axis, down)
+
+
+def pieces(value):
+    high = lax.reduce_precision(value, 8, 7)
+    rest = value - high
+    middle = lax.reduce_precision(rest, 8, 7)
+    low = rest - middle
+    return jnp.concatenate([high, middle, low]).astype(jnp.bfloat16)
+
+
+def joined(parts, rows):
+    wide = parts.astype(jnp.float32)
+    return wide[:rows] + wide[rows : 2 * rows] + wide[2 * rows : 3 * rows]
 
 
 def laplace(source):
-    center = source[:, 1:-1]
-    total = source[:, 2:] + source[:, :-2] - 6.0 * center
-    padded = jnp.pad(center, ((0, 0), (0, 0), (1, 1), (1, 1), (0, 0)))
-    total = total + padded[:, :, 2:, 1:-1] + padded[:, :, :-2, 1:-1]
-    total = total + padded[:, :, 1:-1, 2:] + padded[:, :, 1:-1, :-2]
+    center = source[..., 1:-1, :, :, :]
+    total = source[..., 2:, :, :, :] + source[..., :-2, :, :, :] - 6.0 * center
+    lead = ((0, 0),) * (center.ndim - 3)
+    padded = jnp.pad(center, lead + ((1, 1), (1, 1), (0, 0)))
+    total = total + padded[..., 2:, 1:-1, :] + padded[..., :-2, 1:-1, :]
+    total = total + padded[..., 1:-1, 2:, :] + padded[..., 1:-1, :-2, :]
     return total
 
 
-def phase_turn(field, angle):
-    cosv = jnp.cos(angle)[..., None]
-    sinv = jnp.sin(angle)[..., None]
+def phase_turn(field, cosv, sinv):
     return jnp.stack([cosv * field[0] + sinv * field[1], cosv * field[1] - sinv * field[0]])
 
 
-def kinetic_body(field, wide, inside):
-    slab = field.shape[1]
-    running = field
+def kinetic_body(running, wide, inside):
+    slab = running.shape[1]
     term = wide
     for order in range(1, TAYLOR + 1):
         curvature = laplace(term.astype(jnp.float32))
@@ -65,13 +75,31 @@
     return jnp.stack([over_real, over_imag])
 
 
+def scatter_sum(value, axis, groups):
+    members = len(groups[0])
+    parts = lax.all_to_all(value, axis, 0, 0, tiled=True, axis_index_groups=groups)
+    rows = value.shape[0] // members
+    return jnp.sum(parts.reshape(members, rows, -1).astype(jnp.float32), axis=0)
+
+
+def gather_rows(value, axis, groups):
+    members = len(groups[0])
+    spread = jnp.broadcast_to(value[None], (members,) + value.shape)
+    spread = lax.optimization_barrier(spread)
+    out = lax.all_to_all(spread, axis, 0, 0, tiled=True, axis_index_groups=groups)
+    return out.reshape(-1, value.shape[-1])
+
+
 def space_sum(partial, axis):
     devices = lax.axis_size(axis)
-    parts = lax.all_to_all(partial.astype(jnp.bfloat16), axis, 0, 0, tiled=True)
-    rows = partial.shape[0] // devices
-    mine = jnp.sum(parts.reshape(devices, rows, -1).astype(jnp.float32), axis=0)
-    spread = jnp.broadcast_to(mine.astype(jnp.bfloat16)[None], (devices,) + mine.shape)
-    return lax.all_to_all(lax.optimization_barrier(spread), axis, 0, 0, tiled=True)
+    inner = NEAR if devices % NEAR == 0 else 1
+    outer = devices // inner
+    near = [[q * inner + r for r in range(inner)] for q in range(outer)]
+    far = [[q * inner + r for q in range(outer)] for r in range(inner)]
+    mine = scatter_sum(partial.astype(jnp.bfloat16), axis, near)
+    mine = scatter_sum(mine.astype(jnp.bfloat16), axis, far)
+    mine = gather_rows(mine.astype(jnp.bfloat16), axis, far)
+    return gather_rows(mine, axis, near)
 
 
 def high_dot(left, right):
@@ -92,7 +120,6 @@
     slab, rows_y, cols_z, orbits = start.shape[1:]
     devices = lax.axis_size("space")
     place = lax.axis_index("space")
-    angle = half_step * potential[0].reshape(slab, rows_y, cols_z)
     cells_total = slab * devices * rows_y * cols_z
     shape_one = (slab, rows_y, cols_z, orbits)
     start_real = start[0].reshape(-1, orbits)
@@ -101,27 +128,51 @@
     high_in = jnp.full((slab,), jnp.where(place < devices - 1, 1.0, 0.0), jnp.float32)
     inside = jnp.concatenate([low_in, jnp.ones((slab,), jnp.float32), high_in])
 
-    turned = phase_turn(orbitals[0].astype(jnp.float32), angle)
-    turned_start = phase_turn(start.astype(jnp.float32), angle)
+    flat_rows = 2 * slab * rows_y * cols_z
+    spare = -3 * slab % 16
+    extra = jnp.pad(pieces(potential[0]), ((0, spare), (0, 0)))
+    message = jnp.concatenate([start.reshape(flat_rows, orbits), extra])
+    below, above = neighbour_pair(message, "space")
+    field_below, field_above = neighbour_pair(orbitals[0], "space")
+    full = (2,) + shape_one
+    wide_start = jnp.concatenate(
+        [below[:flat_rows].reshape(full), start, above[:flat_rows].reshape(full)], axis=1
+    ).astype(jnp.float32)
+    wide_field = jnp.concatenate([field_below, orbitals[0], field_above], axis=1)
+    wide_field = wide_field.astype(jnp.float32)
+    wide_potential = jnp.concatenate(
+        [joined(below[flat_rows:], slab), potential[0], joined(above[flat_rows:], slab)]
+    )
+    angle = half_step * wide_potential.reshape(3 * slab, rows_y, cols_z)
+    cosv = jnp.cos(angle)[..., None]
+    sinv = jnp.sin(angle)[..., None]
+    own = slice(slab, 2 * slab)
+
+    def evolve(turned_wide):
+        sent = lax.optimization_barrier(turned_wide.astype(jnp.bfloat16))
+        moved = kinetic_body(turned_wide[:, own], sent, inside)
+        return phase_turn(moved, cosv[own], sinv[own])
+
+    part_real = evolve(jnp.stack([cosv * wide_start[0], -sinv * wide_start[0]]))
+    part_imag = evolve(jnp.stack([cosv * wide_start[1], -sinv * wide_start[1]]))
+    moved = jnp.stack([part_real[0] - part_imag[1], part_real[1] + part_imag[0]])
+    adjoint = jnp.stack([part_real[0] + part_imag[1], part_imag[0] - part_real[1]])
+    moved = lax.optimization_barrier(moved.astype(jnp.bfloat16))
+    adjoint = lax.optimization_barrier(adjoint.astype(jnp.bfloat16))
+    first = evolve(phase_turn(wide_field, cosv, sinv))
+    turned = phase_turn(first, cosv[own], sinv[own])
     sent = lax.optimization_barrier(turned.astype(jnp.bfloat16))
-    sent_start = lax.optimization_barrier(turned_start.astype(jnp.bfloat16))
-    wide = halo(sent, "space")
-    wide_start = halo(sent_start, "space")
-    first = phase_turn(kinetic_body(turned, wide, inside), angle)
-    turned = phase_turn(first, angle)
-    sent = lax.optimization_barrier(turned.astype(jnp.bfloat16))
-    wide = halo(sent, "space")
-    moved = phase_turn(kinetic_body(turned_start, wide_start, inside), angle).astype(jnp.bfloat16)
-    moved = lax.optimization_barrier(moved)
-    second = phase_turn(kinetic_body(turned, wide, inside), angle)
-
+    sent_below, sent_above = neighbour_pair(sent, "space")
+    rounded = first.astype(jnp.bfloat16)
     partial = jnp.concatenate(
         [
-            overlap(start_real, start_imag, first.astype(jnp.bfloat16)),
-            overlap(start_real, start_imag, second.astype(jnp.bfloat16)),
+            overlap(start_real, start_imag, rounded),
+            overlap(adjoint[0].reshape(-1, orbits), adjoint[1].reshape(-1, orbits), rounded),
             overlap(start_real, start_imag, moved),
         ]
     ) * (1.0 / cells_total)
+    wide = jnp.concatenate([sent_below, sent, sent_above], axis=1)
+    second = phase_turn(kinetic_body(turned, wide, inside), cosv[own], sinv[own])
     summed = space_sum(partial.reshape(-1, orbits), "space").reshape(6, orbits, orbits)
     wide_sum = summed.astype(jnp.float32)
     mix1_real = high_dot(coupling, wide_sum[0]).astype(jnp.bfloat16)
@@ -179,7 +230,8 @@
     high = density[:, rows_y - BUF :] * weight_high + upper_brick * (1.0 - weight_high)
     blended = jnp.concatenate([low, density[:, BUF : rows_y - BUF], high], axis=1)
     new_grid = external[0].reshape(slab, rows_y, cols_z) - xc_factor * jnp.cbrt(blended + 1e-06)
-    evolved = phase_turn(field, half_step * new_grid).astype(jnp.bfloat16)
+    turn = (half_step * new_grid)[..., None]
+    evolved = phase_turn(field, jnp.cos(turn), jnp.sin(turn)).astype(jnp.bfloat16)
     return (evolved[None], intersection[None], new_grid.reshape(1, slab, rows_y * cols_z))
 
 

time: 126 us -> 157 us (1.25)
  blocking collectives: 32.6 us -> 0 us
  starting transfers between devices: 33.1 us -> 62.7 us
  other arithmetic: 16.3 us -> 32.3 us
  local copies, waits for them, and re-layouts: 3.24 us -> 11.1 us
  matrix products: 5.94 us -> 10.5 us
  waiting for transfers between devices: 28.3 us -> 32.6 us
    all_to_all x1 -> x0, blocking collectives: 32.6 us -> none  [space_sum(): parts = lax.all_to_all(partial.astype(jnp.bfloat16), axis, 0, 0, tiled=True)]
    all_to_all x1 -> x4, starting transfers between devices: 5.01 us -> 31.9 us  [the longest x2 24.5 us: scatter_sum(): lax.all_to_all(value, axis, 0, 0, tiled=True, axis_index_groups=groups)]
    all_to_all x1 -> x4, waiting for transfers between devices: 11.2 us -> 27.6 us  [the longest x2 14.3 us: scatter_sum(): lax.all_to_all(value, axis, 0, 0, tiled=True, axis_index_groups=groups)]
    ppermute x6, waiting for transfers between devices: 12 us -> 0.02 us  [neighbour_pair(): return (lax.ppermute(value, axis, up), lax.ppermute(value, axis, down))]
    add x12 -> x18, other arithmetic: 3.95 us -> 8.24 us  [the longest x16 8.22 us: laplace(): total = total + padded[..., 1:-1, 2:, :] + padded[..., 1:-1, :-2, :]]
    dot_general x12, matrix products: 2.11 us -> 5.12 us  [half_dot(): return jnp.dot(left, right, preferred_element_type=jnp.float32)]
    unnamed x12 -> x59, local copies, waits for them, and re-layouts: 0.28 us -> 3.06 us
    all_to_all x1, starting transfers between devices: 10.4 us -> 12.9 us  [shards(): lax.all_to_all(jnp.broadcast_to(flat, (domain_count,) + flat.shape[1:]),...]
  transfers between devices with their start and end apart: 8 -> 11, of which waited for: 7 -> 5; matrix products, arithmetic and copies ran while one was open for 4% -> 14% of each run, Pallas kernels for 0% -> 0%
where the time goes in v2:
time: 157 us; the launch traced here: 155 us
  starting transfers between devices  62.7 us (40%)
  waiting for transfers between devices  32.6 us (21%)
  other arithmetic  32.3 us (21%)
  local copies, waits for them, and re-layouts  11.1 us (7%)
  matrix products  10.5 us (7%)
  between operations  5.93 us (4%)
    all_to_all x2, starting transfers between devices, scatter_sum(): lax.all_to_all(value, axis, 0, 0, tiled=True, axis_index_groups=groups)  24.5 us
    ppermute x6, starting transfers between devices, neighbour_pair(): return (lax.ppermute(value, axis, up), lax.ppermute(value, axis, down))  17.9 us
    all_to_all x2, waiting for transfers between devices, scatter_sum(): lax.all_to_all(value, axis, 0, 0, tiled=True, axis_index_groups=groups)  14.3 us
    all_to_all x2, waiting for transfers between devices, gather_rows(): lax.all_to_all(spread, axis, 0, 0, tiled=True, axis_index_groups=groups)  13.2 us
    all_to_all x1, starting transfers between devices, shards(): lax.all_to_all(jnp.broadcast_to(flat, (domain_count,) + flat.shape[1:]),...  12.9 us
    add x16, other arithmetic, laplace(): total = total + padded[..., 1:-1, 2:, :] + padded[..., 1:-1, :-2, :]  8.22 us
    all_to_all x2, starting transfers between devices, gather_rows(): lax.all_to_all(spread, axis, 0, 0, tiled=True, axis_index_groups=groups)  7.33 us
    dot_general x12, matrix products, half_dot(): return jnp.dot(left, right, preferred_element_type=jnp.float32)  5.12 us
  transfers between devices with their start and end apart: 11, of which 5 were waited for; matrix products, arithmetic and copies ran while one was open for 14% of the time, Pallas kernels for 0%

profile of v2, /device:TPU:1, one launch (start us, length us, event | category | flops | bytes accessed | tf_op | source)
XLA Modules:
  0.0 155.1 jit_solution(7223517713699815975)
XLA Ops:
  0.7 0.8 reduce-precision_convert_fusion.1
  1.5 1.0 pad_maximum_fusion.16
  2.5 1.3 collective-permute-start.1
  3.8 5.0 %collective-permute-start = (bf16[1040,128]{1,0:T(8,128)(2,1)S(1)}, bf16[1040,128]{1,0:T(8,128)(2,1)S(1)}, u32[]{:S(2)}, u32[]{:S(2)}) collective-permute-start(bf16[1040,128]{1,0:T(8,128)(2,1)S(1)} %pad_maximum_fusion.16), channel_id=1, source_target_pairs={{0,1},{1,2},{2,3},{3,4},{4,5},{5,6},{6,7},{7,8},{8,9},{9,10},{10,1... | collective-permute-start | bytes 798728 | tf_op jit(solution)/shard_map/ppermute | solution.py:19
  8.8 1.0 copy.160
  9.8 1.3 collective-permute-start.3
  11.1 4.9 %collective-permute-start.2 = (bf16[2,4,16,8,128]{4,2,3,1,0:T(8,128)(2,1)S(1)}, bf16[2,4,16,8,128]{4,2,3,1,0:T(8,128)(2,1)}, u32[]{:S(2)}, u32[]{:S(2)}) collective-permute-start(bf16[2,4,16,8,128]{4,2,3,1,0:T(8,128)(2,1)S(1)} %bitcast.228), channel_id=1, source_target_pairs={{0,1},{1,2},{2,3},{3,4},{4,5},{5,6},{6,7},{7,8},{8,9},{9,10},{10,1... | collective-permute-start | bytes 786440 | tf_op jit(solution)/shard_map/ppermute | solution.py:19
  16.3 1.0 fusion.184
  17.3 0.6 broadcast_subtract_fusion
  17.9 0.7 fusion.174
  18.6 1.2 iota_compare_fusion.3
  19.8 1.2 iota_compare_fusion.1
  23.9 0.7 copy.142
  25.9 0.6 subtract_multiply_fusion.1
  26.5 1.1 maximum_convert_fusion
  28.5 0.9 slice_multiply_fusion.1
  30.7 0.5 fusion.10
  31.1 0.5 fusion.22
  31.6 0.5 fusion.18
  32.1 0.7 slice_multiply_fusion.11
  33.8 0.4 fusion.57
  34.2 0.4 fusion.69
  34.6 0.4 fusion.65
  34.9 0.4 slice_multiply_fusion.19
  36.2 0.3 fusion.81
  37.1 0.4 slice_multiply_fusion.26
  40.6 1.3 collective-permute-start.5
  41.9 4.2 %collective-permute-start.4 = (bf16[2,4,16,8,128]{4,2,3,1,0:T(8,128)(2,1)S(1)}, bf16[2,4,16,8,128]{4,2,3,1,0:T(8,128)(2,1)S(1)}, u32[]{:S(2)}, u32[]{:S(2)}) collective-permute-start(bf16[2,4,16,8,128]{4,2,3,1,0:T(8,128)(2,1)S(1)} %fusion.149), channel_id=1, source_target_pairs={{0,1},{1,2},{2,3},{3,4},{4,5},{5,6},{6,7},{7,8},{8,9},{9,10},{10,1... | collective-permute-start | bytes 786440 | tf_op jit(solution)/shard_map/ppermute | solution.py:19
  48.7 0.7 multiply_convert_fusion
  49.4 8.4 %all-to-all-start = ((bf16[4,192,128]{2,1,0:T(8,128)(2,1)}), bf16[4,192,128]{2,1,0:T(8,128)(2,1)}, u32[]{:S(2)}, u32[]{:S(2)}) async-start(bf16[4,192,128]{2,1,0:T(8,128)(2,1)} %bitcast.34), calls=%async_computation | async-start | bytes 393216 | tf_op jit(solution)/shard_map/all_to_all | solution.py:80
  58.0 0.5 fusion.14
  59.0 0.4 fusion.61
  60.1 2.9 %all-to-all-done = bf16[4,192,128]{2,1,0:T(8,128)(2,1)} async-done(((bf16[4,192,128]{2,1,0:T(8,128)(2,1)}), bf16[4,192,128]{2,1,0:T(8,128)(2,1)}, u32[]{:S(2)}, u32[]{:S(2)}) %all-to-all-start) | async-done | bytes 196640 | tf_op jit(solution)/shard_map/all_to_all | solution.py:80
  63.0 1.6 %reduce_sum.87 = bf16[192,128]{1,0:T(8,128)(2,1)} reduce(bf16[4,192,128]{2,1,0:T(8,128)(2,1)} %all-to-all-done, bf16[]{:T(256)} %constant.20.clone.1), dimensions={0}, to_apply=%region_0.1 | reduce | flops 73728 | bytes 245762 | tf_op jit(solution)/shard_map/reduce_sum | solution.py:82
  64.6 16.1 %all-to-all-start.1 = ((bf16[8,24,128]{2,1,0:T(8,128)(2,1)}), bf16[8,24,128]{2,1,0:T(8,128)(2,1)S(1)}, u32[]{:S(2)}, u32[]{:S(2)}) async-start(bf16[8,24,128]{2,1,0:T(8,128)(2,1)} %bitcast.237), calls=%async_computation.1 | async-start | bytes 98304 | tf_op jit(solution)/shard_map/all_to_all | solution.py:80
  80.7 0.8 slice_multiply_fusion.24
  81.6 0.7 copy-done.1
  82.3 0.8 slice.940
  83.2 11.4 %all-to-all-done.1 = bf16[8,24,128]{2,1,0:T(8,128)(2,1)S(1)} async-done(((bf16[8,24,128]{2,1,0:T(8,128)(2,1)}), bf16[8,24,128]{2,1,0:T(8,128)(2,1)S(1)}, u32[]{:S(2)}, u32[]{:S(2)}) %all-to-all-start.1) | async-done | bytes 49184 | tf_op jit(solution)/shard_map/all_to_all | solution.py:80
  94.6 0.6 reduce_sum.88
  95.2 1.3 broadcast_in_dim.61
  96.5 3.3 %all-to-all-start.2 = ((bf16[8,24,128]{2,1,0:T(8,128)(2,1)}), bf16[8,24,128]{2,1,0:T(8,128)(2,1)S(1)}, u32[]{:S(2)}, u32[]{:S(2)}) async-start(bf16[8,24,128]{2,1,0:T(8,128)(2,1)} %broadcast_in_dim.61), calls=%async_computation.2 | async-start | bytes 98304 | tf_op jit(solution)/shard_map/all_to_all | solution.py:89
  99.9 3.2 %fusion.125 = f32[2,4,16,8,128]{4,2,3,1,0:T(8,128)} fusion(f32[2,4,16,8,128]{4,2,3,1,0:T(8,128)} %slice.940, f32[2,6,16,8,128]{4,2,3,1,0:T(8,128)S(1)} %convert_element_type.190), kind=kLoop, calls=%fused_computation.283 | loop fusion | flops 917504 | bytes 2097152 | tf_op jit(solution)/shard_map/add | solution.py:41
  103.1 10.6 %all-to-all-done.2 = bf16[8,24,128]{2,1,0:T(8,128)(2,1)S(1)} async-done(((bf16[8,24,128]{2,1,0:T(8,128)(2,1)}), bf16[8,24,128]{2,1,0:T(8,128)(2,1)S(1)}, u32[]{:S(2)}, u32[]{:S(2)}) %all-to-all-start.2) | async-done | bytes 49184 | tf_op jit(solution)/shard_map/all_to_all | solution.py:89
  113.7 0.7 broadcast_in_dim.63
  114.4 4.0 %all-to-all-start.3 = ((bf16[4,192,128]{2,1,0:T(8,128)(2,1)}), bf16[4,192,128]{2,1,0:T(8,128)(2,1)}, u32[]{:S(2)}, u32[]{:S(2)}) async-start(bf16[4,192,128]{2,1,0:T(8,128)(2,1)} %broadcast_in_dim.63), calls=%async_computation.3 | async-start | bytes 393216 | tf_op jit(solution)/shard_map/all_to_all | solution.py:89
  118.4 1.1 slice_multiply_fusion.33
  119.5 1.2 fusion.106
  121.0 2.6 %all-to-all-done.3 = bf16[4,192,128]{2,1,0:T(8,128)(2,1)} async-done(((bf16[4,192,128]{2,1,0:T(8,128)(2,1)}), bf16[4,192,128]{2,1,0:T(8,128)(2,1)}, u32[]{:S(2)}, u32[]{:S(2)}) %all-to-all-start.3) | async-done | bytes 196640 | tf_op jit(solution)/shard_map/all_to_all | solution.py:89
  123.6 1.0 convolution_convert_fusion.2
  124.6 1.0 convolution_convert_fusion.3
  125.6 1.0 convert_element_type.212
  126.5 0.9 fusion.159
  127.6 0.9 fusion.158
  128.5 0.9 fusion.33
  129.5 0.3 convolution_convert_fusion
  130.1 0.9 fusion.35
  131.1 0.3 convolution_convert_fusion.1
  133.1 0.6 broadcast_in_dim.67
  133.8 12.9 %all-to-all-start.4 = ((f32[16,4,128]{2,1,0:T(4,128)}), f32[16,4,128]{2,1,0:T(4,128)S(1)}, u32[]{:S(2)}, u32[]{:S(2)}) async-start(f32[16,4,128]{2,1,0:T(4,128)} %broadcast_in_dim.67), calls=%async_computation.4 | async-start | bytes 65536 | tf_op jit(solution)/shard_map/all_to_all | solution.py:219
  146.7 0.7 maximum_bitcast_fusion
  147.4 5.1 %all-to-all-done.4 = f32[16,4,128]{2,1,0:T(4,128)S(1)} async-done(((f32[16,4,128]{2,1,0:T(4,128)}), f32[16,4,128]{2,1,0:T(4,128)S(1)}, u32[]{:S(2)}, u32[]{:S(2)}) %all-to-all-start.4) | async-done | bytes 32800 | tf_op jit(solution)/shard_map/all_to_all | solution.py:219
  153.7 0.8 copy.144
  154.6 0.6 sub.202
  (197 shorter events, 15.6 us)
Async XLA Ops:
  0.6 122.9 %copy-start = (f32[128,128]{1,0:T(8,128)S(1)}, f32[128,128]{1,0:T(8,128)}, u32[]{:S(2)}) copy-start(f32[128,128]{1,0:T(8,128)} %param.13) | copy-start | bytes 196612
  0.6 20.4 %copy-start.15 = (f32[1,4,128]{2,1,0:T(4,128)S(1)}, f32[1,4,128]{2,1,0:T(4,128)}, u32[]{:S(2)}) copy-start(f32[1,4,128]{2,1,0:T(4,128)} %param.10) | copy-start | bytes 6148
  0.7 20.5 %copy-start.11 = (bf16[1,2,4,16,8,128]{5,4,3,2,1,0:T(8,128)(2,1)S(1)}, bf16[1,2,4,16,8,128]{5,4,3,2,1,0:T(8,128)(2,1)}, u32[]{:S(2)}) copy-start(bf16[1,2,4,16,8,128]{5,4,3,2,1,0:T(8,128)(2,1)} %param.9) | copy-start | bytes 786436
  0.7 17.2 %copy-start.18 = (s32[16,2]{0,1:T(2,128)S(1)}, s32[16,2]{0,1:T(2,128)}, u32[]{:S(2)}) copy-start(s32[16,2]{0,1:T(2,128)} %param.15) | copy-start | bytes 388
  0.7 17.2 %copy-start.19 = (s32[16,2]{0,1:T(2,128)S(1)}, s32[16,2]{0,1:T(2,128)}, u32[]{:S(2)}) copy-start(s32[16,2]{0,1:T(2,128)} %param.14) | copy-start | bytes 388
  0.7 23.1 %copy-start.13 = (f32[1,4,128]{2,1,0:T(4,128)S(1)}, f32[1,4,128]{2,1,0:T(4,128)}, u32[]{:S(2)}) copy-start(f32[1,4,128]{2,1,0:T(4,128)} %param.11) | copy-start | bytes 6148
  2.5 25.1 %collective-permute-start.1 = (bf16[1040,128]{1,0:T(8,128)(2,1)S(1)}, bf16[1040,128]{1,0:T(8,128)(2,1)S(1)}, u32[]{:S(2)}, u32[]{:S(2)}) collective-permute-start(bf16[1040,128]{1,0:T(8,128)(2,1)S(1)} %pad_maximum_fusion.16), channel_id=1, source_target_pairs={{1,0},{2,1},{3,2},{4,3},{5,4},{6,5},{7,6},{8,7},{9,8},{10,9},{11,1... | collective-permute-start | bytes 798728 | tf_op jit(solution)/shard_map/ppermute | solution.py:19
  3.8 24.0 %collective-permute-start = (bf16[1040,128]{1,0:T(8,128)(2,1)S(1)}, bf16[1040,128]{1,0:T(8,128)(2,1)S(1)}, u32[]{:S(2)}, u32[]{:S(2)}) collective-permute-start(bf16[1040,128]{1,0:T(8,128)(2,1)S(1)} %pad_maximum_fusion.16), channel_id=1, source_target_pairs={{0,1},{1,2},{2,3},{3,4},{4,5},{5,6},{6,7},{7,8},{8,9},{9,10},{10,1... | collective-permute-start | bytes 798728 | tf_op jit(solution)/shard_map/ppermute | solution.py:19
  9.8 16.7 %collective-permute-start.3 = (bf16[2,4,16,8,128]{4,2,3,1,0:T(8,128)(2,1)S(1)}, bf16[2,4,16,8,128]{4,2,3,1,0:T(8,128)(2,1)S(1)}, u32[]{:S(2)}, u32[]{:S(2)}) collective-permute-start(bf16[2,4,16,8,128]{4,2,3,1,0:T(8,128)(2,1)S(1)} %bitcast.227), channel_id=1, source_target_pairs={{1,0},{2,1},{3,2},{4,3},{5,4},{6,5},{7,6},{8,7},{9,8},{10,9},{11,1... | collective-permute-start | bytes 786440 | tf_op jit(solution)/shard_map/ppermute | solution.py:19
  11.1 15.4 %collective-permute-start.2 = (bf16[2,4,16,8,128]{4,2,3,1,0:T(8,128)(2,1)S(1)}, bf16[2,4,16,8,128]{4,2,3,1,0:T(8,128)(2,1)}, u32[]{:S(2)}, u32[]{:S(2)}) collective-permute-start(bf16[2,4,16,8,128]{4,2,3,1,0:T(8,128)(2,1)S(1)} %bitcast.228), channel_id=1, source_target_pairs={{0,1},{1,2},{2,3},{3,4},{4,5},{5,6},{6,7},{7,8},{8,9},{9,10},{10,1... | collective-permute-start | bytes 786440 | tf_op jit(solution)/shard_map/ppermute | solution.py:19
  16.3 20.8 %copy-start.16 = (f32[6]{0:T(128)}, f32[6]{0:T(128)S(1)}, u32[]{:S(2)}) copy-start(f32[6]{0:T(128)S(1)} %get-tuple-element.109) | copy-start | bytes 76
  16.3 20.8 %copy-start.17 = (f32[6]{0:T(128)}, f32[6]{0:T(128)S(1)}, u32[]{:S(2)}) copy-start(f32[6]{0:T(128)S(1)} %get-tuple-element.110) | copy-start | bytes 76
  38.7 1.9 %copy-start.9 = (f32[1,4,16,8,128]{4,2,3,1,0:T(8,128)}, f32[1,4,16,8,128]{4,2,3,1,0:T(8,128)S(1)}, u32[]{:S(2)}) copy-start(f32[1,4,16,8,128]{4,2,3,1,0:T(8,128)S(1)} %get-tuple-element.71) | copy-start | bytes 786436
  38.7 1.9 %copy-start.10 = (f32[1,4,16,8,128]{4,2,3,1,0:T(8,128)}, f32[1,4,16,8,128]{4,2,3,1,0:T(8,128)S(1)}, u32[]{:S(2)}) copy-start(f32[1,4,16,8,128]{4,2,3,1,0:T(8,128)S(1)} %get-tuple-element.73) | copy-start | bytes 786436
  40.6 17.2 %collective-permute-start.5 = (bf16[2,4,16,8,128]{4,2,3,1,0:T(8,128)(2,1)S(1)}, bf16[2,4,16,8,128]{4,2,3,1,0:T(8,128)(2,1)S(1)}, u32[]{:S(2)}, u32[]{:S(2)}) collective-permute-start(bf16[2,4,16,8,128]{4,2,3,1,0:T(8,128)(2,1)S(1)} %fusion.149), channel_id=1, source_target_pairs={{1,0},{2,1},{3,2},{4,3},{5,4},{6,5},{7,6},{8,7},{9,8},{10,9},{11,1... | collective-permute-start | bytes 786440 | tf_op jit(solution)/shard_map/ppermute | solution.py:19
  41.9 15.9 %collective-permute-start.4 = (bf16[2,4,16,8,128]{4,2,3,1,0:T(8,128)(2,1)S(1)}, bf16[2,4,16,8,128]{4,2,3,1,0:T(8,128)(2,1)S(1)}, u32[]{:S(2)}, u32[]{:S(2)}) collective-permute-start(bf16[2,4,16,8,128]{4,2,3,1,0:T(8,128)(2,1)S(1)} %fusion.149), channel_id=1, source_target_pairs={{0,1},{1,2},{2,3},{3,4},{4,5},{5,6},{6,7},{7,8},{8,9},{9,10},{10,1... | collective-permute-start | bytes 786440 | tf_op jit(solution)/shard_map/ppermute | solution.py:19
  46.7 1.7 %copy-start.7 = (bf16[1,4,16,8,128]{4,3,2,1,0:T(8,128)(2,1)}, bf16[1,4,16,8,128]{4,3,2,1,0:T(8,128)(2,1)S(1)}, u32[]{:S(2)}) copy-start(bf16[1,4,16,8,128]{4,3,2,1,0:T(8,128)(2,1)S(1)} %copy.127) | copy-start | bytes 393220
  47.0 1.2 copy-start.5
  49.4 13.6 %all-to-all-start = ((bf16[4,192,128]{2,1,0:T(8,128)(2,1)}), bf16[4,192,128]{2,1,0:T(8,128)(2,1)}, u32[]{:S(2)}, u32[]{:S(2)}) async-start(bf16[4,192,128]{2,1,0:T(8,128)(2,1)} %bitcast.34), calls=%async_computation | async-start | bytes 393216 | tf_op jit(solution)/shard_map/all_to_all | solution.py:80
  64.6 30.0 %all-to-all-start.1 = ((bf16[8,24,128]{2,1,0:T(8,128)(2,1)}), bf16[8,24,128]{2,1,0:T(8,128)(2,1)S(1)}, u32[]{:S(2)}, u32[]{:S(2)}) async-start(bf16[8,24,128]{2,1,0:T(8,128)(2,1)} %bitcast.237), calls=%async_computation.1 | async-start | bytes 98304 | tf_op jit(solution)/shard_map/all_to_all | solution.py:80
  81.5 0.8 copy-start.1
  81.5 1.6 %copy-start.3 = (f32[1,6,16,8,128]{4,2,3,1,0:T(8,128)}, f32[1,6,16,8,128]{4,2,3,1,0:T(8,128)S(1)}, u32[]{:S(2)}) copy-start(f32[1,6,16,8,128]{4,2,3,1,0:T(8,128)S(1)} %get-tuple-element.60) | copy-start | bytes 1179652
  96.5 17.2 %all-to-all-start.2 = ((bf16[8,24,128]{2,1,0:T(8,128)(2,1)}), bf16[8,24,128]{2,1,0:T(8,128)(2,1)S(1)}, u32[]{:S(2)}, u32[]{:S(2)}) async-start(bf16[8,24,128]{2,1,0:T(8,128)(2,1)} %broadcast_in_dim.61), calls=%async_computation.2 | async-start | bytes 98304 | tf_op jit(solution)/shard_map/all_to_all | solution.py:89
  103.1 16.4 %copy-start.2 = (f32[1,6,16,8,128]{4,2,3,1,0:T(8,128)S(1)}, f32[1,6,16,8,128]{4,2,3,1,0:T(8,128)}, u32[]{:S(2)}) copy-start(f32[1,6,16,8,128]{4,2,3,1,0:T(8,128)} %copy-done.1) | copy-start | bytes 1179652
  103.1 16.4 %copy-start.4 = (f32[1,6,16,8,128]{4,2,3,1,0:T(8,128)S(1)}, f32[1,6,16,8,128]{4,2,3,1,0:T(8,128)}, u32[]{:S(2)}) copy-start(f32[1,6,16,8,128]{4,2,3,1,0:T(8,128)} %copy-done.3) | copy-start | bytes 1179652
  114.4 9.2 %all-to-all-start.3 = ((bf16[4,192,128]{2,1,0:T(8,128)(2,1)}), bf16[4,192,128]{2,1,0:T(8,128)(2,1)}, u32[]{:S(2)}, u32[]{:S(2)}) async-start(bf16[4,192,128]{2,1,0:T(8,128)(2,1)} %broadcast_in_dim.63), calls=%async_computation.3 | async-start | bytes 393216 | tf_op jit(solution)/shard_map/all_to_all | solution.py:89
  120.7 6.7 %copy-start.8 = (bf16[1,4,16,8,128]{4,3,2,1,0:T(8,128)(2,1)S(1)}, bf16[1,4,16,8,128]{4,3,2,1,0:T(8,128)(2,1)}, u32[]{:S(2)}) copy-start(bf16[1,4,16,8,128]{4,3,2,1,0:T(8,128)(2,1)} %copy-done.7) | copy-start | bytes 393220
  129.8 2.2 %copy-start.6 = (bf16[1,4,16,8,128]{4,3,2,1,0:T(8,128)(2,1)S(1)}, bf16[1,4,16,8,128]{4,3,2,1,0:T(8,128)(2,1)}, u32[]{:S(2)}) copy-start(bf16[1,4,16,8,128]{4,3,2,1,0:T(8,128)(2,1)} %copy-done.5) | copy-start | bytes 393220
  132.1 0.7 copy-start.20
  132.4 20.1 %copy-start.23 = (pred[16]{0:T(512)(128)(4,1)S(1)}, pred[16]{0:T(512)(128)(4,1)}, u32[]{:S(2)}) copy-start(pred[16]{0:T(512)(128)(4,1)} %iota_compare_fusion.3) | copy-start | bytes 52
  132.4 20.1 %copy-start.24 = (pred[16]{0:T(512)(128)(4,1)S(1)}, pred[16]{0:T(512)(128)(4,1)}, u32[]{:S(2)}) copy-start(pred[16]{0:T(512)(128)(4,1)} %iota_compare_fusion.1) | copy-start | bytes 52
  132.4 20.6 %copy-start.21 = (f32[4]{0:T(128)S(1)}, f32[4]{0:T(128)}, u32[]{:S(2)}) copy-start(f32[4]{0:T(128)} %get-tuple-element.121) | copy-start | bytes 52
  132.4 20.6 %copy-start.22 = (f32[4]{0:T(128)S(1)}, f32[4]{0:T(128)}, u32[]{:S(2)}) copy-start(f32[4]{0:T(128)} %get-tuple-element.122) | copy-start | bytes 52
  132.4 20.6 %copy-start.25 = (f32[4]{0:T(128)S(1)}, f32[4]{0:T(128)}, u32[]{:S(2)}) copy-start(f32[4]{0:T(128)} %get-tuple-element.119) | copy-start | bytes 52
  132.5 20.6 %copy-start.26 = (f32[4]{0:T(128)S(1)}, f32[4]{0:T(128)}, u32[]{:S(2)}) copy-start(f32[4]{0:T(128)} %get-tuple-element.120) | copy-start | bytes 52
  132.5 20.6 %copy-start.12 = (f32[4,16,8]{1,2,0:T(8,128)S(1)}, f32[4,16,8]{1,2,0:T(8,128)}, u32[]{:S(2)}) copy-start(f32[4,16,8]{1,2,0:T(8,128)} %copy.142) | copy-start | bytes 6148
  133.8 18.7 %all-to-all-start.4 = ((f32[16,4,128]{2,1,0:T(4,128)}), f32[16,4,128]{2,1,0:T(4,128)S(1)}, u32[]{:S(2)}, u32[]{:S(2)}) async-start(f32[16,4,128]{2,1,0:T(4,128)} %broadcast_in_dim.67), calls=%async_computation.4 | async-start | bytes 65536 | tf_op jit(solution)/shard_map/all_to_all | solution.py:219
  146.7 7.9 %copy-start.14 = (f32[1,4,128]{2,1,0:T(4,128)S(1)}, f32[1,4,128]{2,1,0:T(4,128)}, u32[]{:S(2)}) copy-start(f32[1,4,128]{2,1,0:T(4,128)} %param.11) | copy-start | bytes 6148

commit v3 on v0

v3 whole, which is shorter than its diff:
```python
import jax
import jax.numpy as jnp
from jax import lax
from jax.experimental import pallas as pl
from jax.experimental.pallas import tpu as pltpu
from jax.sharding import PartitionSpec as P

TAYLOR = 4
BUF = 4

time_step = 0.4
half_step = 0.2
xc_factor = 0.9847450218426965


def neighbour_pair(value, axis):
    devices = lax.axis_size(axis)
    up = [(i, i + 1) for i in range(devices - 1)]
    down = [(i + 1, i) for i in range(devices - 1)]
    return lax.ppermute(value, axis, up), lax.ppermute(value, axis, down)


def rounded(value):
    return value.astype(jnp.bfloat16).astype(jnp.float32)


def spread_column(row):
    return jnp.broadcast_to(row, (row.shape[-1], row.shape[-1])).T


def laplace(ref, part, plane):
    center = ref[part, plane]
    side = center.shape[1]
    zero = jnp.zeros((1,) + center.shape[1:], jnp.float32)
    total = ref[part, plane - 1] + ref[part, plane + 1]
    total = total + jnp.concatenate([center[1:], zero]) + jnp.concatenate([zero, center[:-1]])
    level = lax.broadcasted_iota(jnp.int32, center.shape, 1)
    total = total + jnp.where(level == side - 1, 0.0, pltpu.roll(center, side - 1, 1))
    total = total + jnp.where(level == 0, 0.0, pltpu.roll(center, 1, 1))
    return total - 6.0 * center


def kinetic(edge, running, even, odd, slab, grid):
    planes = 3 * slab
    cells = grid[0] * grid[1]
    now, after = even, odd
    for order in range(1, TAYLOR + 1):
        factor = time_step / (2.0 * order)

        def one(plane, carry, now=now, after=after, factor=factor, last=order == TAYLOR):
            inside = jnp.where(plane < slab, edge[0], jnp.where(plane >= 2 * slab, edge[1], 1.0))
            keep = inside * factor
            real = -keep * laplace(now, 1, plane)
            imag = keep * laplace(now, 0, plane)
            for part, update in enumerate((real, imag)):
                running[part, plane] = running[part, plane] + update
                if not last:
                    flat = update.reshape(cells, update.shape[-1])
                    after[part, plane] = rounded(flat).reshape(update.shape)
            return carry

        lax.fori_loop(order, planes - order, one, 0)
        now, after = after, now


def fill_phase(potential, row, place, cos_ref, sin_ref, slab):
    cosv = jnp.cos(half_step * potential)
    sinv = jnp.sin(half_step * potential)
    for plane in range(slab):
        cos_ref[place + plane] = spread_column(cosv[row + plane : row + plane + 1])
        sin_ref[place + plane] = spread_column(sinv[row + plane : row + plane + 1])


def front_kernel(slab, grid, scale, edge, low_i, own_i, high_i, low_o, own_o, high_o, pot,
                 partial_ref, moved_ref, sent_ref, turned_ref,
                 even, odd, running, cos_ref, sin_ref, part_ref, adjoint_ref, right):
    cells = grid[0] * grid[1]
    half = slab * cells
    lanes = own_i.shape[-1]
    tail = 2 * half
    box = grid + (lanes,)
    for group, ref in ((0, low_i), (2, high_i)):
        extra = ref[tail : tail + 32].astype(jnp.float32)
        whole = extra[0:8] + extra[8:16] + extra[16:24]
        fill_phase(whole, 0, group * slab, cos_ref, sin_ref, slab)
    fill_phase(pot[...], 0, slab, cos_ref, sin_ref, slab)

    def start_at(plane, real, imag):
        for part, value in enumerate((real, imag)):
            running[part, plane] = value.reshape(box)
            even[part, plane] = rounded(value).reshape(box)

    def load(ref, part, plane):
        at = pl.multiple_of((part * slab + plane) * cells, cells)
        return ref[pl.ds(at, cells), :].astype(jnp.float32)

    def finish(plane):
        real = running[0, slab + plane].reshape(cells, lanes)
        imag = running[1, slab + plane].reshape(cells, lanes)
        cosv = cos_ref[slab + plane]
        sinv = sin_ref[slab + plane]
        return cosv * real + sinv * imag, cosv * imag - sinv * real

    for part in range(2):
        for group, ref in enumerate((low_i, own_i, high_i)):

            def begin(plane, carry, ref=ref, group=group, part=part):
                value = load(ref, part, plane)
                at = group * slab + plane
                start_at(at, cos_ref[at] * value, -sin_ref[at] * value)
                return carry

            lax.fori_loop(0, slab, begin, 0)
        kinetic(edge, running, even, odd, slab, grid)
        for plane in range(slab):
            real, imag = finish(plane)
            low = plane * cells
            if part == 0:
                part_ref[0, plane] = real
                part_ref[1, plane] = imag
            else:
                kept_real = part_ref[0, plane]
                kept_imag = part_ref[1, plane]
                moved_real = (kept_real - imag).astype(jnp.bfloat16)
                moved_imag = (kept_imag + real).astype(jnp.bfloat16)
                moved_ref[low : low + cells] = moved_real
                moved_ref[half + low : half + low + cells] = moved_imag
                right[low : low + cells, 2 * lanes : 3 * lanes] = moved_real
                right[low : low + cells, 3 * lanes :] = moved_imag
                right[half + low : half + low + cells, 2 * lanes : 3 * lanes] = moved_imag
                right[half + low : half + low + cells, 3 * lanes :] = -moved_real
                adjoint_ref[low : low + cells] = (kept_real + imag).astype(jnp.bfloat16)
                adjoint_ref[half + low : half + low + cells] = (real - kept_imag).astype(jnp.bfloat16)

    for group, ref in enumerate((low_o, own_o, high_o)):

        def begin_field(plane, carry, ref=ref, group=group):
            real = load(ref, 0, plane)
            imag = load(ref, 1, plane)
            at = group * slab + plane
            cosv = cos_ref[at]
            sinv = sin_ref[at]
            start_at(at, cosv * real + sinv * imag, cosv * imag - sinv * real)
            return carry

        lax.fori_loop(0, slab, begin_field, 0)
    kinetic(edge, running, even, odd, slab, grid)
    for plane in range(slab):
        real, imag = finish(plane)
        low = plane * cells
        cosv = cos_ref[slab + plane]
        sinv = sin_ref[slab + plane]
        turned_real = cosv * real + sinv * imag
        turned_imag = cosv * imag - sinv * real
        turned_ref[low : low + cells] = turned_real
        turned_ref[half + low : half + low + cells] = turned_imag
        sent_ref[low : low + cells] = turned_real.astype(jnp.bfloat16)
        sent_ref[half + low : half + low + cells] = turned_imag.astype(jnp.bfloat16)
        first_real = real.astype(jnp.bfloat16)
        first_imag = imag.astype(jnp.bfloat16)
        right[low : low + cells, :lanes] = first_real
        right[low : low + cells, lanes : 2 * lanes] = first_imag
        right[half + low : half + low + cells, :lanes] = first_imag
        right[half + low : half + low + cells, lanes : 2 * lanes] = -first_real

    over = contract(own_i[...], right[...]) * scale
    cross = contract(adjoint_ref[...], right[:, : 2 * lanes]) * scale
    for index in range(2):
        piece = slice(index * lanes, (index + 1) * lanes)
        partial_ref[index * lanes : (index + 1) * lanes] = over[:, piece].astype(jnp.bfloat16)
        partial_ref[(2 + index) * lanes : (3 + index) * lanes] = cross[:, piece].astype(jnp.bfloat16)
        piece = slice((2 + index) * lanes, (3 + index) * lanes)
        partial_ref[(4 + index) * lanes : (5 + index) * lanes] = over[:, piece].astype(jnp.bfloat16)


def second_kernel(slab, grid, edge, low, own, high, turned, pot, second_ref,
                  even, odd, running, cos_ref, sin_ref):
    cells = grid[0] * grid[1]
    half = slab * cells
    lanes = own.shape[-1]
    box = grid + (lanes,)
    fill_phase(pot[...], 0, 0, cos_ref, sin_ref, slab)
    for part in range(2):
        for group, ref in enumerate((low, own, high)):

            def begin(plane, carry, ref=ref, group=group, part=part):
                at = pl.multiple_of((part * slab + plane) * cells, cells)
                value = ref[pl.ds(at, cells), :].astype(jnp.float32).reshape(box)
                even[part, group * slab + plane] = value
                if group == 1:
                    running[part, slab + plane] = turned[pl.ds(at, cells), :].reshape(box)
                return carry

            lax.fori_loop(0, slab, begin, 0)
    kinetic(edge, running, even, odd, slab, grid)
    for plane in range(slab):
        real = running[0, slab + plane].reshape(cells, lanes)
        imag = running[1, slab + plane].reshape(cells, lanes)
        cosv = cos_ref[plane]
        sinv = sin_ref[plane]
        at = plane * cells
        second_ref[at : at + cells] = cosv * real + sinv * imag
        second_ref[half + at : half + at + cells] = cosv * imag - sinv * real


def sum_kernel(parts_ref, out_ref):
    total = parts_ref[0].astype(jnp.float32)
    for index in range(1, parts_ref.shape[0]):
        total = total + parts_ref[index].astype(jnp.float32)
    total = total.astype(jnp.bfloat16)
    for index in range(out_ref.shape[0]):
        out_ref[index] = total


def back_kernel(slab, sums, coupling, moved, start, second, occupation,
                inter_ref, field_ref, density_ref):
    lanes = coupling.shape[-1]
    half = start.shape[0] // 2
    cells = half // slab
    strength = coupling[...]

    def matrix(index):
        return sums[index * lanes : (index + 1) * lanes]

    def mixed(real, imag):
        return (
            high_dot(strength, real).astype(jnp.bfloat16),
            high_dot(strength, imag).astype(jnp.bfloat16),
        )

    mix1_real, mix1_imag = mixed(
        matrix(0).astype(jnp.float32), matrix(1).astype(jnp.float32)
    )
    gram_real, gram_imag = matrix(4), matrix(5)
    over_real = matrix(2).astype(jnp.float32) + time_step * (
        half_dot(gram_real, mix1_imag) + half_dot(gram_imag, mix1_real)
    )
    over_imag = matrix(3).astype(jnp.float32) - time_step * (
        half_dot(gram_real, mix1_real) - half_dot(gram_imag, mix1_imag)
    )
    inter_ref[:lanes] = over_real
    inter_ref[lanes:] = over_imag
    mix2_real, mix2_imag = mixed(over_real, over_imag)
    mix1_real_imag = jnp.concatenate([mix1_real, mix1_imag], axis=1)
    mix1_turned = jnp.concatenate([-mix1_imag, mix1_real], axis=1)
    mix2_real_imag = jnp.concatenate([mix2_real, mix2_imag], axis=1)
    mix2_turned = jnp.concatenate([-mix2_imag, mix2_real], axis=1)
    weight = jnp.broadcast_to(occupation[...], (8, lanes))
    for plane in range(slab):
        low = plane * cells
        real_rows = slice(low, low + cells)
        imag_rows = slice(half + low, half + low + cells)
        corr = (
            half_dot(moved[real_rows], mix1_real_imag)
            + half_dot(moved[imag_rows], mix1_turned)
            + half_dot(start[real_rows], mix2_real_imag)
            + half_dot(start[imag_rows], mix2_turned)
        )
        real = second[real_rows] + time_step * corr[:, lanes:]
        imag = second[imag_rows] - time_step * corr[:, :lanes]
        field_ref[real_rows] = real
        field_ref[imag_rows] = imag
        square = real * real + imag * imag
        dense = lax.dot_general(
            weight,
            square,
            (((1,), (1,)), ((), ())),
            precision=lax.Precision.HIGHEST,
            preferred_element_type=jnp.float32,
        )
        for owner in range(density_ref.shape[0]):
            density_ref[owner, plane : plane + 1] = dense[:1]


def tail_kernel(slab, grid, place, gathered, external, field, grid_ref, evolved_ref):
    lanes = external.shape[-1]
    half = field.shape[0] // 2
    cells = half // slab
    side = grid[1]
    own = gathered[place[4]]
    lower = gathered[place[0]]
    upper = gathered[place[1]]
    lower = pltpu.roll(lower, (lanes - place[2] * side) % lanes, 1)
    upper = pltpu.roll(upper, (2 * lanes - BUF * side - place[3] * side) % lanes, 1)
    level = lax.broadcasted_iota(jnp.int32, own.shape, 1) // side
    step = level.astype(jnp.float32)
    weight_low = (step + 1.0) / (BUF + 1.0)
    weight_high = (grid[0] - step) / (BUF + 1.0)
    low = own * weight_low + lower * (1.0 - weight_low)
    high = own * weight_high + upper * (1.0 - weight_high)
    blended = jnp.where(level < BUF, low, jnp.where(level >= grid[0] - BUF, high, own))
    root = jnp.exp(jnp.log(blended + 1e-06) * (1.0 / 3.0))
    new_grid = external[...] - xc_factor * root
    grid_ref[...] = new_grid
    cosv = jnp.cos(half_step * new_grid)
    sinv = jnp.sin(half_step * new_grid)
    for plane in range(slab):
        low_row = plane * cells
        real = field[low_row : low_row + cells]
        imag = field[half + low_row : half + low_row + cells]
        cos_b = spread_column(cosv[plane : plane + 1])
        sin_b = spread_column(sinv[plane : plane + 1])
        evolved_ref[low_row : low_row + cells] = (cos_b * real + sin_b * imag).astype(jnp.bfloat16)
        evolved_ref[half + low_row : half + low_row + cells] = (
            cos_b * imag - sin_b * real
        ).astype(jnp.bfloat16)


def contract(left, right):
    return lax.dot_general(
        left, right, (((0,), (0,)), ((), ())), preferred_element_type=jnp.float32
    )


def high_dot(left, right):
    return jnp.dot(
        left, right, precision=lax.Precision.HIGHEST, preferred_element_type=jnp.float32
    )


def half_dot(left, right):
    return jnp.dot(left, right, preferred_element_type=jnp.float32)


def pieces(value):
    high = lax.reduce_precision(value, 8, 7)
    rest = value - high
    middle = lax.reduce_precision(rest, 8, 7)
    low = rest - middle
    rows = value.shape[0]
    pad = jnp.zeros((8 - rows,) + value.shape[1:], value.dtype)
    stacked = jnp.concatenate([high, pad, middle, pad, low, pad, jnp.zeros((8,) + value.shape[1:])])
    return stacked.astype(jnp.bfloat16)


def scalars(count):
    return [pl.BlockSpec(memory_space=pltpu.SMEM)] + [
        pl.BlockSpec(memory_space=pltpu.VMEM) for _ in range(count)
    ]


def shards(orbitals, initial, potential, external, occupation, coupling, neighbours, offsets):
    slab, rows_y, cols_z, orbits = initial.shape[2:]
    grid = (rows_y, cols_z)
    cells = rows_y * cols_z
    rows = 2 * slab * cells
    start = initial.reshape(rows, orbits)
    devices = lax.axis_size("space")
    place = lax.axis_index("space")
    f32, bf16 = jnp.float32, jnp.bfloat16
    edge = jnp.stack([place > 0, place < devices - 1]).astype(f32)
    planes = (2, 3 * slab) + grid + (orbits,)
    stencil = [pltpu.VMEM(planes, f32) for _ in range(3)]
    message = jnp.concatenate([start, pieces(potential[0])])
    orbs = orbitals.reshape(rows, orbits)
    low_i, high_i = neighbour_pair(message, "space")
    low_o, high_o = neighbour_pair(orbs, "space")
    scale = 1.0 / (slab * devices * cells)
    shape = jax.ShapeDtypeStruct
    partial, moved, sent, turned = pl.pallas_call(
        lambda *refs: front_kernel(slab, grid, scale, *refs),
        out_shape=(
            shape((6 * orbits, orbits), bf16),
            shape((rows, orbits), bf16),
            shape((rows, orbits), bf16),
            shape((rows, orbits), f32),
        ),
        in_specs=scalars(7),
        scratch_shapes=stencil
        + [pltpu.VMEM((3 * slab, cells, orbits), f32) for _ in range(2)]
        + [
            pltpu.VMEM((2, slab, cells, orbits), f32),
            pltpu.VMEM((rows, orbits), bf16),
            pltpu.VMEM((rows, 4 * orbits), bf16),
        ],
        compiler_params=pltpu.CompilerParams(vmem_limit_bytes=20 << 20),
        name="front",
    )(edge, low_i, start, high_i, low_o, orbs, high_o, potential[0])

    share = 6 * orbits // devices
    parts = lax.all_to_all(partial.reshape(devices, share, orbits), "space", 0, 0, tiled=True)
    low_s, high_s = neighbour_pair(sent, "space")
    spread = pl.pallas_call(
        sum_kernel,
        out_shape=shape((devices, share, orbits), bf16),
        compiler_params=pltpu.CompilerParams(vmem_limit_bytes=6 << 20),
        name="total",
    )(parts)
    sums = lax.all_to_all(spread, "space", 0, 0, tiled=True).reshape(6 * orbits, orbits)
    second = pl.pallas_call(
        lambda *refs: second_kernel(slab, grid, *refs),
        out_shape=shape((rows, orbits), f32),
        in_specs=scalars(5),
        scratch_shapes=stencil + [pltpu.VMEM((slab, cells, orbits), f32) for _ in range(2)],
        compiler_params=pltpu.CompilerParams(vmem_limit_bytes=14 << 20),
        name="second",
    )(edge, low_s, sent, high_s, turned, potential[0])

    domain_count = neighbours.shape[0]
    intersection, field, density = pl.pallas_call(
        lambda *refs: back_kernel(slab, *refs),
        out_shape=(
            shape((2 * orbits, orbits), f32),
            shape((rows, orbits), f32),
            shape((domain_count, slab, cells), f32),
        ),
        compiler_params=pltpu.CompilerParams(vmem_limit_bytes=14 << 20),
        name="back",
    )(sums, coupling, moved, start, second, occupation.reshape(1, orbits))
    gathered = lax.all_to_all(density, "dom", 0, 0, tiled=True)
    own_index = lax.axis_index("dom")
    mine = lax.dynamic_index_in_dim(neighbours, own_index, 0, keepdims=False)
    shift = lax.dynamic_index_in_dim(offsets, own_index, 0, keepdims=False)
    where = jnp.concatenate([mine, shift, own_index.reshape(1).astype(jnp.int32)])
    new_grid, evolved = pl.pallas_call(
        lambda *refs: tail_kernel(slab, grid, *refs),
        out_shape=(shape((slab, cells), f32), shape((rows, orbits), bf16)),
        in_specs=scalars(3),
        compiler_params=pltpu.CompilerParams(vmem_limit_bytes=8 << 20),
        name="tail",
    )(where, gathered, external[0], field)
    return (
        evolved.reshape(orbitals.shape),
        intersection.reshape(1, 2, orbits, orbits),
        new_grid[None],
    )


def solution(mesh):
    return jax.shard_map(
        shards,
        mesh=mesh,
        in_specs=(
            P("dom", None, "space", None, None, None),
            P("dom", None, "space", None, None, None),
            P("dom", "space", None),
            P("dom", "space", None),
            P(),
            P(),
            P(),
            P(),
        ),
        out_specs=(
            P("dom", None, "space", None, None, None),
            P("dom", None, None, None),
            P("dom", "space", None),
        ),
        check_vma=False,
    )
```

time: 694 us -> 111 us (0.16)
  waiting for transfers between devices: 580 us -> 19 us
  between operations: 18.8 us -> 0.81 us
  Pallas kernels: 0 us -> 16.1 us
  other arithmetic: 11 us -> 0.84 us
  matrix products: 7.38 us -> 0 us
    psum x2 -> x0, waiting for transfers between devices: 549 us -> none  [shards(): intersection = lax.psum(partial_sum, 'space')]
    all_to_all x0 -> x1, blocking collectives: none -> 38.2 us  [shards(): lax.all_to_all(partial.reshape(devices, share, orbits), 'space', 0, 0, ti...]
    all_gather x1 -> x0, blocking collectives: 36 us -> none  [shards(): lax.all_gather(density.reshape(1, slab, rows_y * cols_z), 'dom', axis=0,...]
    ppermute x16 -> x6, starting transfers between devices: 37.5 us -> 17 us  [neighbour_pair(): return (lax.ppermute(value, axis, up), lax.ppermute(value, axis, down))]
    ppermute x16 -> x6, waiting for transfers between devices: 30.6 us -> 13.3 us  [neighbour_pair(): return (lax.ppermute(value, axis, up), lax.ppermute(value, axis, down))]
    pallas_call x0 -> x5, Pallas kernels: none -> 16.1 us  [the longest x1 8.37 us: shards(): pl.pallas_call(lambda *refs: front_kernel(slab, grid, scale, *refs), out_...]
    all_to_all x0 -> x2, starting transfers between devices: none -> 15.2 us  [the longest x1 10.7 us: shards(): gathered = lax.all_to_all(density, 'dom', 0, 0, tiled=True)]
    dot_general x18 -> x0, matrix products: 7.38 us -> none  [the longest x2 2.21 us: shards(): jnp.dot(coupling, intersection[0], precision=lax.Precision.HIGHEST)]
  transfers between devices with their start and end apart: 18 -> 8, of which waited for: 10 -> 5; matrix products, arithmetic and copies ran while one was open for 0% -> 0% of each run, Pallas kernels for 0% -> 3%
where the time goes in v3:
time: 111 us; the launch traced here: 110 us
  blocking collectives  38.2 us (34%)
  starting transfers between devices  32.2 us (29%)
  waiting for transfers between devices  19 us (17%)
  Pallas kernels  16.1 us (15%)
  local copies, waits for them, and re-layouts  2.72 us (2%)
    all_to_all x1, blocking collectives, shards(): lax.all_to_all(partial.reshape(devices, share, orbits), 'space', 0, 0, ti...  38.2 us
    ppermute x6, starting transfers between devices, neighbour_pair(): return (lax.ppermute(value, axis, up), lax.ppermute(value, axis, down))  17 us
    ppermute x6, waiting for transfers between devices, neighbour_pair(): return (lax.ppermute(value, axis, up), lax.ppermute(value, axis, down))  13.3 us
    all_to_all x1, starting transfers between devices, shards(): gathered = lax.all_to_all(density, 'dom', 0, 0, tiled=True)  10.7 us
    pallas_call x1, Pallas kernels, shards(): pl.pallas_call(lambda *refs: front_kernel(slab, grid, scale, *refs), out_...  8.37 us
    all_to_all x1, waiting for transfers between devices, shards(): gathered = lax.all_to_all(density, 'dom', 0, 0, tiled=True)  5.72 us
    all_to_all x1, starting transfers between devices, shards(): lax.all_to_all(spread, 'space', 0, 0, tiled=True)  4.47 us
    pallas_call x1, Pallas kernels, shards(): pl.pallas_call(lambda *refs: second_kernel(slab, grid, *refs), out_shape=...  2.92 us
  transfers between devices with their start and end apart: 8, of which 5 were waited for; matrix products, arithmetic and copies ran while one was open for 0% of the time, Pallas kernels for 3%

profile of v3, /device:TPU:1, one launch (start us, length us, event | category | flops | bytes accessed | tf_op | source)
XLA Modules:
  0.0 109.9 jit_solution(2477731742440948912)
XLA Ops:
  0.6 0.7 fusion
  1.3 0.0 copy-start.1
  1.3 0.0 copy-start
  1.4 1.2 %concatenate.10 = bf16[1056,128]{1,0:T(8,128)(2,1)S(1)} concatenate(bf16[1024,128]{1,0:T(8,128)(2,1)} %bitcast.16, bf16[4,128]{1,0:T(4,128)(2,1)S(1)} %get-tuple-element.22, bf16[4,128]{1,0:T(4,128)(2,1)S(1)} %broadcast_in_dim.9, bf16[4,128]{1,0:T(4,128)(2,1)S(1)} %get-tuple-element.23, bf16[4,128]{1,0:T(4,128)(2,1)S(1)} %broadcast_in_dim.9, ...), dimensions={0} | concatenate | bytes 540672 | tf_op jit(solution)/shard_map/concatenate | solution.py:354
  2.5 1.3 %collective-permute-start.1 = (bf16[1056,128]{1,0:T(8,128)(2,1)S(1)}, bf16[1056,128]{1,0:T(8,128)(2,1)S(1)}, u32[]{:S(2)}, u32[]{:S(2)}) collective-permute-start(bf16[1056,128]{1,0:T(8,128)(2,1)S(1)} %concatenate.10), channel_id=1, source_target_pairs={{1,0},{2,1},{3,2},{4,3},{5,4},{6,5},{7,6},{8,7},{9,8},{10,9},{11,1... | collective-permute-start | bytes 811016 | tf_op jit(solution)/shard_map/ppermute | solution.py:20
  3.8 5.0 %collective-permute-start = (bf16[1056,128]{1,0:T(8,128)(2,1)S(1)}, bf16[1056,128]{1,0:T(8,128)(2,1)S(1)}, u32[]{:S(2)}, u32[]{:S(2)}) collective-permute-start(bf16[1056,128]{1,0:T(8,128)(2,1)S(1)} %concatenate.10), channel_id=1, source_target_pairs={{0,1},{1,2},{2,3},{3,4},{4,5},{5,6},{6,7},{7,8},{8,9},{9,10},{10,1... | collective-permute-start | bytes 811016 | tf_op jit(solution)/shard_map/ppermute | solution.py:20
  8.8 0.0 copy-done.1
  8.8 1.3 %collective-permute-start.3 = (bf16[1024,128]{1,0:T(8,128)(2,1)S(1)}, bf16[1024,128]{1,0:T(8,128)(2,1)S(1)}, u32[]{:S(2)}, u32[]{:S(2)}) collective-permute-start(bf16[1024,128]{1,0:T(8,128)(2,1)S(1)} %bitcast.20), channel_id=1, source_target_pairs={{1,0},{2,1},{3,2},{4,3},{5,4},{6,5},{7,6},{8,7},{9,8},{10,9},{11,1... | collective-permute-start | bytes 786440 | tf_op jit(solution)/shard_map/ppermute | solution.py:20
  10.1 4.2 %collective-permute-start.2 = (bf16[1024,128]{1,0:T(8,128)(2,1)S(1)}, bf16[1024,128]{1,0:T(8,128)(2,1)S(1)}, u32[]{:S(2)}, u32[]{:S(2)}) collective-permute-start(bf16[1024,128]{1,0:T(8,128)(2,1)S(1)} %bitcast.21), channel_id=1, source_target_pairs={{0,1},{1,2},{2,3},{3,4},{4,5},{5,6},{6,7},{7,8},{8,9},{9,10},{10,1... | collective-permute-start | bytes 786440 | tf_op jit(solution)/shard_map/ppermute | solution.py:20
  14.3 0.0 copy-start.3
  14.3 0.1 add_convert_fusion.refs_0_
  14.4 4.0 %collective-permute-done.3.refs_6_ = bf16[1024,128]{1,0:T(8,128)(2,1)S(1)} collective-permute-done((bf16[1024,128]{1,0:T(8,128)(2,1)S(1)}, bf16[1024,128]{1,0:T(8,128)(2,1)S(1)}, u32[]{:S(2)}, u32[]{:S(2)}) %collective-permute-start.3) | collective-permute-done | bytes 262176 | tf_op jit(solution)/shard_map/ppermute | solution.py:20
  18.4 0.9 collective-permute-done.2.refs_4_
  19.3 0.0 collective-permute-done.1.refs_3_
  19.3 0.0 collective-permute-done.refs_1_
  19.3 0.0 copy-done
  19.3 0.0 copy-done.3
  19.3 8.4 %front.1 = (bf16[768,128]{1,0:T(8,128)(2,1)S(1)}, bf16[1024,128]{1,0:T(8,128)(2,1)S(1)}, bf16[1024,128]{1,0:T(8,128)(2,1)S(1)}, f32[1024,128]{1,0:T(8,128)S(1)}) custom-call(f32[2]{0:T(128)S(1)} %add_convert_fusion.refs_0_, bf16[1056,128]{1,0:T(8,128)(2,1)S(1)} %collective-permute-done.refs_1_, bf16[1024,128]{1,0:T(8,128)(2,1)S(1)} %bitcast.17, ...), custom_call_target="tpu_custom_call" | custom-call | tf_op jit(solution)/shard_map/front/pallas_call | solution.py:360
  27.7 38.2 %all_to_all.15.parts_ref = bf16[32,24,128]{2,1,0:T(8,128)(2,1)S(1)} all-to-all(bf16[32,24,128]{2,1,0:T(8,128)(2,1)S(1)} %bitcast.23), channel_id=1, replica_groups=mesh['dom'=16,'space'=32] {'space'}, dimensions={0} | all-to-all | bytes 393216 | tf_op jit(solution)/shard_map/all_to_all | solution.py:381
  65.9 0.7 total.1
  66.6 4.5 %all-to-all-start.1 = ((bf16[32,24,128]{2,1,0:T(8,128)(2,1)}), bf16[32,24,128]{2,1,0:T(8,128)(2,1)S(1)}, u32[]{:S(2)}, u32[]{:S(2)}) async-start(bf16[32,24,128]{2,1,0:T(8,128)(2,1)} %total.1), calls=%async_computation.1 | async-start | bytes 393216 | tf_op jit(solution)/shard_map/all_to_all | solution.py:389
  71.1 1.3 %collective-permute-start.5 = (bf16[1024,128]{1,0:T(8,128)(2,1)S(1)}, bf16[1024,128]{1,0:T(8,128)(2,1)S(1)}, u32[]{:S(2)}, u32[]{:S(2)}) collective-permute-start(bf16[1024,128]{1,0:T(8,128)(2,1)S(1)} %get-tuple-element.14.refs_2_), channel_id=1, source_target_pairs={{1,0},{2,1},{3,2},{4,3},{5,4},{6,5},{7,6},{8,7},{9,8},{10,9},{11,1... | collective-permute-start | bytes 786440 | tf_op jit(solution)/shard_map/ppermute | solution.py:20
  72.4 4.0 %collective-permute-start.4 = (bf16[1024,128]{1,0:T(8,128)(2,1)S(1)}, bf16[1024,128]{1,0:T(8,128)(2,1)S(1)}, u32[]{:S(2)}, u32[]{:S(2)}) collective-permute-start(bf16[1024,128]{1,0:T(8,128)(2,1)S(1)} %get-tuple-element.14.refs_2_), channel_id=1, source_target_pairs={{0,1},{1,2},{2,3},{3,4},{4,5},{5,6},{6,7},{7,8},{8,9},{9,10},{10,1... | collective-permute-start | bytes 786440 | tf_op jit(solution)/shard_map/ppermute | solution.py:20
  76.4 0.0 copy-start.6
  76.4 0.0 copy-start.7
  76.4 0.7 copy-done.6
  77.1 0.0 copy-done.7
  77.1 0.2 dynamic-slice_reduce_fusion
  77.3 7.6 %collective-permute-done.5.refs_3_ = bf16[1024,128]{1,0:T(8,128)(2,1)S(1)} collective-permute-done((bf16[1024,128]{1,0:T(8,128)(2,1)S(1)}, bf16[1024,128]{1,0:T(8,128)(2,1)S(1)}, u32[]{:S(2)}, u32[]{:S(2)}) %collective-permute-start.5) | collective-permute-done | bytes 262176 | tf_op jit(solution)/shard_map/ppermute | solution.py:20
  84.9 0.8 collective-permute-done.4.refs_1_
  85.7 0.0 copy-start.2
  85.7 2.9 %second.1.refs_4_ = f32[1024,128]{1,0:T(8,128)S(1)} custom-call(f32[2]{0:T(128)S(1)} %add_convert_fusion.refs_0_, bf16[1024,128]{1,0:T(8,128)(2,1)S(1)} %collective-permute-done.4.refs_1_, bf16[1024,128]{1,0:T(8,128)(2,1)S(1)} %get-tuple-element.14.refs_2_, bf16[1024,128]{1,0:T(8,128)(2,1)S(1)} %collective-permute-done.5.refs_3_, ...), custom_call_target="tpu_custom_call" | custom-call | tf_op jit(solution)/shard_map/second/pallas_call | solution.py:390
  88.6 0.0 all-to-all-done.1
  88.6 0.0 copy-start.5
  88.7 0.0 copy-done.2
  88.7 0.6 copy-done.5
  89.3 2.5 %back.1 = (f32[256,128]{1,0:T(8,128)}, f32[1024,128]{1,0:T(8,128)S(1)}, f32[16,4,128]{2,1,0:T(4,128)}) custom-call(bf16[768,128]{1,0:T(8,128)(2,1)S(1)} %bitcast.19, f32[128,128]{1,0:T(8,128)S(1)} %copy-done.2, bf16[1024,128]{1,0:T(8,128)(2,1)S(1)} %get-tuple-element.13.refs_2_, bf16[1024,128]{1,0:T(8,128)(2,1)S(1)} %bitcast.18, ...), custom_call_target="tpu_custom_call" | custom-call | tf_op jit(solution)/shard_map/back/pallas_call | solution.py:400
  91.8 10.7 %all-to-all-start.2 = ((f32[16,4,128]{2,1,0:T(4,128)}), f32[16,4,128]{2,1,0:T(4,128)S(1)}, u32[]{:S(2)}, u32[]{:S(2)}) async-start(f32[16,4,128]{2,1,0:T(4,128)} %get-tuple-element.16), calls=%async_computation.2 | async-start | bytes 65536 | tf_op jit(solution)/shard_map/all_to_all | solution.py:410
  102.5 0.1 pad_add_fusion.refs_0_
  102.6 0.0 copy-start.4
  102.6 5.7 %all-to-all-done.2.refs_1_ = f32[16,4,128]{2,1,0:T(4,128)S(1)} async-done(((f32[16,4,128]{2,1,0:T(4,128)}), f32[16,4,128]{2,1,0:T(4,128)S(1)}, u32[]{:S(2)}, u32[]{:S(2)}) %all-to-all-start.2) | async-done | bytes 32800 | tf_op jit(solution)/shard_map/all_to_all | solution.py:410
  108.3 0.0 copy-done.4
  108.3 1.6 %tail.1 = (f32[4,128]{1,0:T(4,128)}, bf16[1024,128]{1,0:T(8,128)(2,1)}) custom-call(s32[5]{0:T(128)S(1)} %pad_add_fusion.refs_0_, f32[16,4,128]{2,1,0:T(4,128)S(1)} %all-to-all-done.2.refs_1_, f32[4,128]{1,0:T(4,128)S(1)} %bitcast.26, f32[1024,128]{1,0:T(8,128)S(1)} %get-tuple-element.17.refs_3_), custom_call_target="tpu_custom_call" | custom-call | tf_op jit(solution)/shard_map/tail/pallas_call | solution.py:415
  (2 shorter events, 0.0 us)
Async XLA Ops:
  1.3 7.5 %copy-start.1 = (bf16[1,2,4,16,8,128]{5,4,3,2,1,0:T(8,128)(2,1)S(1)}, bf16[1,2,4,16,8,128]{5,4,3,2,1,0:T(8,128)(2,1)}, u32[]{:S(2)}) copy-start(bf16[1,2,4,16,8,128]{5,4,3,2,1,0:T(8,128)(2,1)} %param.8) | copy-start | bytes 786436
  1.3 18.0 %copy-start = (bf16[1,2,4,16,8,128]{5,4,3,2,1,0:T(8,128)(2,1)S(1)}, bf16[1,2,4,16,8,128]{5,4,3,2,1,0:T(8,128)(2,1)}, u32[]{:S(2)}) copy-start(bf16[1,2,4,16,8,128]{5,4,3,2,1,0:T(8,128)(2,1)} %param.9) | copy-start | bytes 786436
  2.5 16.8 %collective-permute-start.1 = (bf16[1056,128]{1,0:T(8,128)(2,1)S(1)}, bf16[1056,128]{1,0:T(8,128)(2,1)S(1)}, u32[]{:S(2)}, u32[]{:S(2)}) collective-permute-start(bf16[1056,128]{1,0:T(8,128)(2,1)S(1)} %concatenate.10), channel_id=1, source_target_pairs={{1,0},{2,1},{3,2},{4,3},{5,4},{6,5},{7,6},{8,7},{9,8},{10,9},{11,1... | collective-permute-start | bytes 811016 | tf_op jit(solution)/shard_map/ppermute | solution.py:20
  3.8 15.5 %collective-permute-start = (bf16[1056,128]{1,0:T(8,128)(2,1)S(1)}, bf16[1056,128]{1,0:T(8,128)(2,1)S(1)}, u32[]{:S(2)}, u32[]{:S(2)}) collective-permute-start(bf16[1056,128]{1,0:T(8,128)(2,1)S(1)} %concatenate.10), channel_id=1, source_target_pairs={{0,1},{1,2},{2,3},{3,4},{4,5},{5,6},{6,7},{7,8},{8,9},{9,10},{10,1... | collective-permute-start | bytes 811016 | tf_op jit(solution)/shard_map/ppermute | solution.py:20
  8.8 9.6 %collective-permute-start.3 = (bf16[1024,128]{1,0:T(8,128)(2,1)S(1)}, bf16[1024,128]{1,0:T(8,128)(2,1)S(1)}, u32[]{:S(2)}, u32[]{:S(2)}) collective-permute-start(bf16[1024,128]{1,0:T(8,128)(2,1)S(1)} %bitcast.20), channel_id=1, source_target_pairs={{1,0},{2,1},{3,2},{4,3},{5,4},{6,5},{7,6},{8,7},{9,8},{10,9},{11,1... | collective-permute-start | bytes 786440 | tf_op jit(solution)/shard_map/ppermute | solution.py:20
  10.1 9.2 %collective-permute-start.2 = (bf16[1024,128]{1,0:T(8,128)(2,1)S(1)}, bf16[1024,128]{1,0:T(8,128)(2,1)S(1)}, u32[]{:S(2)}, u32[]{:S(2)}) collective-permute-start(bf16[1024,128]{1,0:T(8,128)(2,1)S(1)} %bitcast.21), channel_id=1, source_target_pairs={{0,1},{1,2},{2,3},{3,4},{4,5},{5,6},{6,7},{7,8},{8,9},{9,10},{10,1... | collective-permute-start | bytes 786440 | tf_op jit(solution)/shard_map/ppermute | solution.py:20
  14.3 5.0 %copy-start.3 = (f32[1,4,128]{2,1,0:T(4,128)S(1)}, f32[1,4,128]{2,1,0:T(4,128)}, u32[]{:S(2)}) copy-start(f32[1,4,128]{2,1,0:T(4,128)} %param.10) | copy-start | bytes 6148
  66.6 22.0 %all-to-all-start.1 = ((bf16[32,24,128]{2,1,0:T(8,128)(2,1)}), bf16[32,24,128]{2,1,0:T(8,128)(2,1)S(1)}, u32[]{:S(2)}, u32[]{:S(2)}) async-start(bf16[32,24,128]{2,1,0:T(8,128)(2,1)} %total.1), calls=%async_computation.1 | async-start | bytes 393216 | tf_op jit(solution)/shard_map/all_to_all | solution.py:389
  71.1 13.8 %collective-permute-start.5 = (bf16[1024,128]{1,0:T(8,128)(2,1)S(1)}, bf16[1024,128]{1,0:T(8,128)(2,1)S(1)}, u32[]{:S(2)}, u32[]{:S(2)}) collective-permute-start(bf16[1024,128]{1,0:T(8,128)(2,1)S(1)} %get-tuple-element.14.refs_2_), channel_id=1, source_target_pairs={{1,0},{2,1},{3,2},{4,3},{5,4},{6,5},{7,6},{8,7},{9,8},{10,9},{11,1... | collective-permute-start | bytes 786440 | tf_op jit(solution)/shard_map/ppermute | solution.py:20
  72.4 13.3 %collective-permute-start.4 = (bf16[1024,128]{1,0:T(8,128)(2,1)S(1)}, bf16[1024,128]{1,0:T(8,128)(2,1)S(1)}, u32[]{:S(2)}, u32[]{:S(2)}) collective-permute-start(bf16[1024,128]{1,0:T(8,128)(2,1)S(1)} %get-tuple-element.14.refs_2_), channel_id=1, source_target_pairs={{0,1},{1,2},{2,3},{3,4},{4,5},{5,6},{6,7},{7,8},{8,9},{9,10},{10,1... | collective-permute-start | bytes 786440 | tf_op jit(solution)/shard_map/ppermute | solution.py:20
  76.4 0.7 copy-start.6
  76.4 0.7 copy-start.7
  85.7 3.0 %copy-start.2 = (f32[128,128]{1,0:T(8,128)S(1)}, f32[128,128]{1,0:T(8,128)}, u32[]{:S(2)}) copy-start(f32[128,128]{1,0:T(8,128)} %refs_1_.1) | copy-start | bytes 196612
  88.6 0.7 copy-start.5
  91.8 16.5 %all-to-all-start.2 = ((f32[16,4,128]{2,1,0:T(4,128)}), f32[16,4,128]{2,1,0:T(4,128)S(1)}, u32[]{:S(2)}, u32[]{:S(2)}) async-start(f32[16,4,128]{2,1,0:T(4,128)} %get-tuple-element.16), calls=%async_computation.2 | async-start | bytes 65536 | tf_op jit(solution)/shard_map/all_to_all | solution.py:410
  102.6 5.7 %copy-start.4 = (f32[1,4,128]{2,1,0:T(4,128)S(1)}, f32[1,4,128]{2,1,0:T(4,128)}, u32[]{:S(2)}) copy-start(f32[1,4,128]{2,1,0:T(4,128)} %param.11) | copy-start | bytes 6148

commit v4 on v3

--- a/solution.py
+++ b/solution.py
@@ -4,6 +4,7 @@
 from jax.experimental import pallas as pl
 from jax.experimental.pallas import tpu as pltpu
 from jax.sharding import PartitionSpec as P
+
 
 TAYLOR = 4
 BUF = 4
@@ -71,15 +72,15 @@
         sin_ref[place + plane] = spread_column(sinv[row + plane : row + plane + 1])
 
 
-def front_kernel(slab, grid, scale, edge, low_i, own_i, high_i, low_o, own_o, high_o, pot,
+def front_kernel(slab, grid, scale, edge, low_ref, own_ref, high_ref, pot,
                  partial_ref, moved_ref, sent_ref, turned_ref,
                  even, odd, running, cos_ref, sin_ref, part_ref, adjoint_ref, right):
     cells = grid[0] * grid[1]
     half = slab * cells
-    lanes = own_i.shape[-1]
-    tail = 2 * half
+    lanes = own_ref.shape[-1]
+    tail = 4 * half
     box = grid + (lanes,)
-    for group, ref in ((0, low_i), (2, high_i)):
+    for group, ref in ((0, low_ref), (2, high_ref)):
         extra = ref[tail : tail + 32].astype(jnp.float32)
         whole = extra[0:8] + extra[8:16] + extra[16:24]
         fill_phase(whole, 0, group * slab, cos_ref, sin_ref, slab)
@@ -102,7 +103,7 @@
         return cosv * real + sinv * imag, cosv * imag - sinv * real
 
     for part in range(2):
-        for group, ref in enumerate((low_i, own_i, high_i)):
+        for group, ref in enumerate((low_ref, own_ref, high_ref)):
 
             def begin(plane, carry, ref=ref, group=group, part=part):
                 value = load(ref, part, plane)
@@ -132,11 +133,11 @@
                 adjoint_ref[low : low + cells] = (kept_real + imag).astype(jnp.bfloat16)
                 adjoint_ref[half + low : half + low + cells] = (real - kept_imag).astype(jnp.bfloat16)
 
-    for group, ref in enumerate((low_o, own_o, high_o)):
+    for group, ref in enumerate((low_ref, own_ref, high_ref)):
 
         def begin_field(plane, carry, ref=ref, group=group):
-            real = load(ref, 0, plane)
-            imag = load(ref, 1, plane)
+            real = load(ref, 2, plane)
+            imag = load(ref, 3, plane)
             at = group * slab + plane
             cosv = cos_ref[at]
             sinv = sin_ref[at]
@@ -163,7 +164,7 @@
         right[half + low : half + low + cells, :lanes] = first_imag
         right[half + low : half + low + cells, lanes : 2 * lanes] = -first_real
 
-    over = contract(own_i[...], right[...]) * scale
+    over = contract(own_ref[: 2 * half], right[...]) * scale
     cross = contract(adjoint_ref[...], right[:, : 2 * lanes]) * scale
     for index in range(2):
         piece = slice(index * lanes, (index + 1) * lanes)
@@ -351,10 +352,9 @@
     edge = jnp.stack([place > 0, place < devices - 1]).astype(f32)
     planes = (2, 3 * slab) + grid + (orbits,)
     stencil = [pltpu.VMEM(planes, f32) for _ in range(3)]
-    message = jnp.concatenate([start, pieces(potential[0])])
     orbs = orbitals.reshape(rows, orbits)
-    low_i, high_i = neighbour_pair(message, "space")
-    low_o, high_o = neighbour_pair(orbs, "space")
+    message = jnp.concatenate([start, orbs, pieces(potential[0])])
+    low_m, high_m = neighbour_pair(message, "space")
     scale = 1.0 / (slab * devices * cells)
     shape = jax.ShapeDtypeStruct
     partial, moved, sent, turned = pl.pallas_call(
@@ -365,7 +365,7 @@
             shape((rows, orbits), bf16),
             shape((rows, orbits), f32),
         ),
-        in_specs=scalars(7),
+        in_specs=scalars(4),
         scratch_shapes=stencil
         + [pltpu.VMEM((3 * slab, cells, orbits), f32) for _ in range(2)]
         + [
@@ -375,7 +375,7 @@
         ],
         compiler_params=pltpu.CompilerParams(vmem_limit_bytes=20 << 20),
         name="front",
-    )(edge, low_i, start, high_i, low_o, orbs, high_o, potential[0])
+    )(edge, low_m, message, high_m, potential[0])
 
     share = 6 * orbits // devices
     parts = lax.all_to_all(partial.reshape(devices, share, orbits), "space", 0, 0, tiled=True)

time: 111 us -> 110 us (level)
  starting transfers between devices: 32.2 us -> 25.4 us
  blocking collectives: 38.2 us -> 42.1 us
  waiting for transfers between devices: 19 us -> 21 us
    ppermute x6 -> x4, starting transfers between devices: 17 us -> 11.6 us  [neighbour_pair(): return (lax.ppermute(value, axis, up), lax.ppermute(value, axis, down))]
    all_to_all x1, blocking collectives: 38.2 us -> 42.1 us  [shards(): lax.all_to_all(partial.reshape(devices, share, orbits), 'space', 0, 0, ti...]
    ppermute x6 -> x4, waiting for transfers between devices: 13.3 us -> 15.3 us  [neighbour_pair(): return (lax.ppermute(value, axis, up), lax.ppermute(value, axis, down))]
    all_to_all x1, starting transfers between devices: 10.7 us -> 9.05 us  [shards(): gathered = lax.all_to_all(density, 'dom', 0, 0, tiled=True)]
  transfers between devices with their start and end apart: 8 -> 6, of which waited for: 5 -> 5; matrix products, arithmetic and copies ran while one was open for 0% -> 0% of each run, Pallas kernels for 3% -> 3%
where the time goes in v4:
time: 110 us
  blocking collectives  42.1 us (38%)
  starting transfers between devices  25.4 us (23%)
  waiting for transfers between devices  21 us (19%)
  Pallas kernels  16.1 us (15%)
  local copies, waits for them, and re-layouts  3.66 us (3%)
    all_to_all x1, blocking collectives, shards(): lax.all_to_all(partial.reshape(devices, share, orbits), 'space', 0, 0, ti...  42.1 us
    ppermute x4, waiting for transfers between devices, neighbour_pair(): return (lax.ppermute(value, axis, up), lax.ppermute(value, axis, down))  15.3 us
    ppermute x4, starting transfers between devices, neighbour_pair(): return (lax.ppermute(value, axis, up), lax.ppermute(value, axis, down))  11.6 us
    all_to_all x1, starting transfers between devices, shards(): gathered = lax.all_to_all(density, 'dom', 0, 0, tiled=True)  9.05 us
    pallas_call x1, Pallas kernels, shards(): pl.pallas_call(lambda *refs: front_kernel(slab, grid, scale, *refs), out_...  8.38 us
    all_to_all x1, waiting for transfers between devices, shards(): gathered = lax.all_to_all(density, 'dom', 0, 0, tiled=True)  5.72 us
    all_to_all x1, starting transfers between devices, shards(): lax.all_to_all(spread, 'space', 0, 0, tiled=True)  4.75 us
    pallas_call x1, Pallas kernels, shards(): pl.pallas_call(lambda *refs: second_kernel(slab, grid, *refs), out_shape=...  2.92 us
  transfers between devices with their start and end apart: 6, of which 5 were waited for; matrix products, arithmetic and copies ran while one was open for 0% of the time, Pallas kernels for 3%

profile of v4, /device:TPU:1, one launch (start us, length us, event | category | flops | bytes accessed | tf_op | source)
XLA Modules:
  0.0 109.9 jit_solution(8411316668055444140)
XLA Ops:
  0.6 0.7 fusion
  1.3 2.1 %concatenate.10.refs_2_ = bf16[2080,128]{1,0:T(8,128)(2,1)S(1)} concatenate(bf16[1024,128]{1,0:T(8,128)(2,1)} %bitcast.16, bf16[1024,128]{1,0:T(8,128)(2,1)} %bitcast.24, bf16[4,128]{1,0:T(4,128)(2,1)S(1)} %get-tuple-element.22, bf16[4,128]{1,0:T(4,128)(2,1)S(1)} %broadcast_in_dim.9, bf16[4,128]{1,0:T(4,128)(2,1)S(1)} %get-tuple-element.23, bf16[4,128]{1,0:T(4,128)(2,1)S(1)} %broadcast_in_dim.9, ...), dimensions={0} | concatenate | bytes 1064960 | tf_op jit(solution)/shard_map/concatenate | solution.py:356
  3.4 1.3 %collective-permute-start.1 = (bf16[2080,128]{1,0:T(8,128)(2,1)S(1)}, bf16[2080,128]{1,0:T(8,128)(2,1)S(1)}, u32[]{:S(2)}, u32[]{:S(2)}) collective-permute-start(bf16[2080,128]{1,0:T(8,128)(2,1)S(1)} %concatenate.10.refs_2_), channel_id=1, source_target_pairs={{1,0},{2,1},{3,2},{4,3},{5,4},{6,5},{7,6},{8,7},{9,8},{10,9},{11,1... | collective-permute-start | bytes 1597448 | tf_op jit(solution)/shard_map/ppermute | solution.py:21
  4.7 5.0 %collective-permute-start = (bf16[2080,128]{1,0:T(8,128)(2,1)S(1)}, bf16[2080,128]{1,0:T(8,128)(2,1)S(1)}, u32[]{:S(2)}, u32[]{:S(2)}) collective-permute-start(bf16[2080,128]{1,0:T(8,128)(2,1)S(1)} %concatenate.10.refs_2_), channel_id=1, source_target_pairs={{0,1},{1,2},{2,3},{3,4},{4,5},{5,6},{6,7},{7,8},{8,9},{9,10},{10,1... | collective-permute-start | bytes 1597448 | tf_op jit(solution)/shard_map/ppermute | solution.py:21
  9.8 0.0 copy-start.2
  9.8 0.1 add_convert_fusion.refs_0_
  9.9 4.6 %collective-permute-done.1.refs_3_ = bf16[2080,128]{1,0:T(8,128)(2,1)S(1)} collective-permute-done((bf16[2080,128]{1,0:T(8,128)(2,1)S(1)}, bf16[2080,128]{1,0:T(8,128)(2,1)S(1)}, u32[]{:S(2)}, u32[]{:S(2)}) %collective-permute-start.1) | collective-permute-done | bytes 532512 | tf_op jit(solution)/shard_map/ppermute | solution.py:21
  14.4 1.5 %collective-permute-done.refs_1_ = bf16[2080,128]{1,0:T(8,128)(2,1)S(1)} collective-permute-done((bf16[2080,128]{1,0:T(8,128)(2,1)S(1)}, bf16[2080,128]{1,0:T(8,128)(2,1)S(1)}, u32[]{:S(2)}, u32[]{:S(2)}) %collective-permute-start) | collective-permute-done | bytes 532512 | tf_op jit(solution)/shard_map/ppermute | solution.py:21
  15.9 0.0 copy-done.2
  15.9 8.4 %front.1 = (bf16[768,128]{1,0:T(8,128)(2,1)S(1)}, bf16[1024,128]{1,0:T(8,128)(2,1)S(1)}, bf16[1024,128]{1,0:T(8,128)(2,1)S(1)}, f32[1024,128]{1,0:T(8,128)S(1)}) custom-call(f32[2]{0:T(128)S(1)} %add_convert_fusion.refs_0_, bf16[2080,128]{1,0:T(8,128)(2,1)S(1)} %collective-permute-done.refs_1_, bf16[2080,128]{1,0:T(8,128)(2,1)S(1)} %concatenate.10.refs_2_, ...), custom_call_target="tpu_custom_call" | custom-call | tf_op jit(solution)/shard_map/front/pallas_call | solution.py:360
  24.3 42.1 %all_to_all.15.parts_ref = bf16[32,24,128]{2,1,0:T(8,128)(2,1)S(1)} all-to-all(bf16[32,24,128]{2,1,0:T(8,128)(2,1)S(1)} %bitcast.19), channel_id=1, replica_groups=mesh['dom'=16,'space'=32] {'space'}, dimensions={0} | all-to-all | bytes 393216 | tf_op jit(solution)/shard_map/all_to_all | solution.py:381
  66.5 0.7 total.1
  67.2 4.8 %all-to-all-start.1 = ((bf16[32,24,128]{2,1,0:T(8,128)(2,1)}), bf16[32,24,128]{2,1,0:T(8,128)(2,1)S(1)}, u32[]{:S(2)}, u32[]{:S(2)}) async-start(bf16[32,24,128]{2,1,0:T(8,128)(2,1)} %total.1), calls=%async_computation.1 | async-start | bytes 393216 | tf_op jit(solution)/shard_map/all_to_all | solution.py:389
  72.0 1.3 %collective-permute-start.3 = (bf16[1024,128]{1,0:T(8,128)(2,1)S(1)}, bf16[1024,128]{1,0:T(8,128)(2,1)S(1)}, u32[]{:S(2)}, u32[]{:S(2)}) collective-permute-start(bf16[1024,128]{1,0:T(8,128)(2,1)S(1)} %get-tuple-element.14.refs_2_), channel_id=1, source_target_pairs={{1,0},{2,1},{3,2},{4,3},{5,4},{6,5},{7,6},{8,7},{9,8},{10,9},{11,1... | collective-permute-start | bytes 786440 | tf_op jit(solution)/shard_map/ppermute | solution.py:21
  73.3 4.0 %collective-permute-start.2 = (bf16[1024,128]{1,0:T(8,128)(2,1)S(1)}, bf16[1024,128]{1,0:T(8,128)(2,1)S(1)}, u32[]{:S(2)}, u32[]{:S(2)}) collective-permute-start(bf16[1024,128]{1,0:T(8,128)(2,1)S(1)} %get-tuple-element.14.refs_2_), channel_id=1, source_target_pairs={{0,1},{1,2},{2,3},{3,4},{4,5},{5,6},{6,7},{7,8},{8,9},{9,10},{10,1... | collective-permute-start | bytes 786440 | tf_op jit(solution)/shard_map/ppermute | solution.py:21
  77.3 0.0 copy-start.5
  77.3 0.0 copy-start.6
  77.3 0.7 copy-done.5
  77.9 0.0 copy-done.6
  78.0 0.2 dynamic-slice_reduce_fusion
  78.2 8.5 %collective-permute-done.3.refs_3_ = bf16[1024,128]{1,0:T(8,128)(2,1)S(1)} collective-permute-done((bf16[1024,128]{1,0:T(8,128)(2,1)S(1)}, bf16[1024,128]{1,0:T(8,128)(2,1)S(1)}, u32[]{:S(2)}, u32[]{:S(2)}) %collective-permute-start.3) | collective-permute-done | bytes 262176 | tf_op jit(solution)/shard_map/ppermute | solution.py:21
  86.7 0.7 collective-permute-done.2.refs_1_
  87.4 0.0 copy-start
  87.4 0.0 copy-start.1
  87.4 2.9 %second.1.refs_4_ = f32[1024,128]{1,0:T(8,128)S(1)} custom-call(f32[2]{0:T(128)S(1)} %add_convert_fusion.refs_0_, bf16[1024,128]{1,0:T(8,128)(2,1)S(1)} %collective-permute-done.2.refs_1_, bf16[1024,128]{1,0:T(8,128)(2,1)S(1)} %get-tuple-element.14.refs_2_, bf16[1024,128]{1,0:T(8,128)(2,1)S(1)} %collective-permute-done.3.refs_3_, ...), custom_call_target="tpu_custom_call" | custom-call | tf_op jit(solution)/shard_map/second/pallas_call | solution.py:390
  90.3 0.0 all-to-all-done.1
  90.3 0.0 copy-start.4
  90.3 0.0 copy-done
  90.3 0.0 copy-done.1
  90.4 0.6 copy-done.4
  91.0 2.5 %back.1 = (f32[256,128]{1,0:T(8,128)}, f32[1024,128]{1,0:T(8,128)S(1)}, f32[16,4,128]{2,1,0:T(4,128)}) custom-call(bf16[768,128]{1,0:T(8,128)(2,1)S(1)} %bitcast.18, f32[128,128]{1,0:T(8,128)S(1)} %copy-done.1, bf16[1024,128]{1,0:T(8,128)(2,1)S(1)} %get-tuple-element.13.refs_2_, bf16[1024,128]{1,0:T(8,128)(2,1)S(1)} %bitcast.17, ...), custom_call_target="tpu_custom_call" | custom-call | tf_op jit(solution)/shard_map/back/pallas_call | solution.py:400
  93.5 9.1 %all-to-all-start.2 = ((f32[16,4,128]{2,1,0:T(4,128)}), f32[16,4,128]{2,1,0:T(4,128)S(1)}, u32[]{:S(2)}, u32[]{:S(2)}) async-start(f32[16,4,128]{2,1,0:T(4,128)} %get-tuple-element.16), calls=%async_computation.2 | async-start | bytes 65536 | tf_op jit(solution)/shard_map/all_to_all | solution.py:410
  102.5 0.1 pad_add_fusion.refs_0_
  102.6 0.0 copy-start.3
  102.6 5.7 %all-to-all-done.2.refs_1_ = f32[16,4,128]{2,1,0:T(4,128)S(1)} async-done(((f32[16,4,128]{2,1,0:T(4,128)}), f32[16,4,128]{2,1,0:T(4,128)S(1)}, u32[]{:S(2)}, u32[]{:S(2)}) %all-to-all-start.2) | async-done | bytes 32800 | tf_op jit(solution)/shard_map/all_to_all | solution.py:410
  108.3 0.0 copy-done.3
  108.4 1.6 %tail.1 = (f32[4,128]{1,0:T(4,128)}, bf16[1024,128]{1,0:T(8,128)(2,1)}) custom-call(s32[5]{0:T(128)S(1)} %pad_add_fusion.refs_0_, f32[16,4,128]{2,1,0:T(4,128)S(1)} %all-to-all-done.2.refs_1_, f32[4,128]{1,0:T(4,128)S(1)} %bitcast.22, f32[1024,128]{1,0:T(8,128)S(1)} %get-tuple-element.17.refs_3_), custom_call_target="tpu_custom_call" | custom-call | tf_op jit(solution)/shard_map/tail/pallas_call | solution.py:415
  (2 shorter events, 0.0 us)
Async XLA Ops:
  3.4 11.0 %collective-permute-start.1 = (bf16[2080,128]{1,0:T(8,128)(2,1)S(1)}, bf16[2080,128]{1,0:T(8,128)(2,1)S(1)}, u32[]{:S(2)}, u32[]{:S(2)}) collective-permute-start(bf16[2080,128]{1,0:T(8,128)(2,1)S(1)} %concatenate.10.refs_2_), channel_id=1, source_target_pairs={{1,0},{2,1},{3,2},{4,3},{5,4},{6,5},{7,6},{8,7},{9,8},{10,9},{11,1... | collective-permute-start | bytes 1597448 | tf_op jit(solution)/shard_map/ppermute | solution.py:21
  4.7 11.2 %collective-permute-start = (bf16[2080,128]{1,0:T(8,128)(2,1)S(1)}, bf16[2080,128]{1,0:T(8,128)(2,1)S(1)}, u32[]{:S(2)}, u32[]{:S(2)}) collective-permute-start(bf16[2080,128]{1,0:T(8,128)(2,1)S(1)} %concatenate.10.refs_2_), channel_id=1, source_target_pairs={{0,1},{1,2},{2,3},{3,4},{4,5},{5,6},{6,7},{7,8},{8,9},{9,10},{10,1... | collective-permute-start | bytes 1597448 | tf_op jit(solution)/shard_map/ppermute | solution.py:21
  9.8 6.2 %copy-start.2 = (f32[1,4,128]{2,1,0:T(4,128)S(1)}, f32[1,4,128]{2,1,0:T(4,128)}, u32[]{:S(2)}) copy-start(f32[1,4,128]{2,1,0:T(4,128)} %param.10) | copy-start | bytes 6148
  67.2 23.1 %all-to-all-start.1 = ((bf16[32,24,128]{2,1,0:T(8,128)(2,1)}), bf16[32,24,128]{2,1,0:T(8,128)(2,1)S(1)}, u32[]{:S(2)}, u32[]{:S(2)}) async-start(bf16[32,24,128]{2,1,0:T(8,128)(2,1)} %total.1), calls=%async_computation.1 | async-start | bytes 393216 | tf_op jit(solution)/shard_map/all_to_all | solution.py:389
  72.0 14.7 %collective-permute-start.3 = (bf16[1024,128]{1,0:T(8,128)(2,1)S(1)}, bf16[1024,128]{1,0:T(8,128)(2,1)S(1)}, u32[]{:S(2)}, u32[]{:S(2)}) collective-permute-start(bf16[1024,128]{1,0:T(8,128)(2,1)S(1)} %get-tuple-element.14.refs_2_), channel_id=1, source_target_pairs={{1,0},{2,1},{3,2},{4,3},{5,4},{6,5},{7,6},{8,7},{9,8},{10,9},{11,1... | collective-permute-start | bytes 786440 | tf_op jit(solution)/shard_map/ppermute | solution.py:21
  73.3 14.1 %collective-permute-start.2 = (bf16[1024,128]{1,0:T(8,128)(2,1)S(1)}, bf16[1024,128]{1,0:T(8,128)(2,1)S(1)}, u32[]{:S(2)}, u32[]{:S(2)}) collective-permute-start(bf16[1024,128]{1,0:T(8,128)(2,1)S(1)} %get-tuple-element.14.refs_2_), channel_id=1, source_target_pairs={{0,1},{1,2},{2,3},{3,4},{4,5},{5,6},{6,7},{7,8},{8,9},{9,10},{10,1... | collective-permute-start | bytes 786440 | tf_op jit(solution)/shard_map/ppermute | solution.py:21
  77.3 0.7 copy-start.5
  77.3 0.7 copy-start.6
  87.4 3.0 %copy-start = (bf16[1,2,4,16,8,128]{5,4,3,2,1,0:T(8,128)(2,1)S(1)}, bf16[1,2,4,16,8,128]{5,4,3,2,1,0:T(8,128)(2,1)}, u32[]{:S(2)}) copy-start(bf16[1,2,4,16,8,128]{5,4,3,2,1,0:T(8,128)(2,1)} %param.9) | copy-start | bytes 786436
  87.4 3.0 %copy-start.1 = (f32[128,128]{1,0:T(8,128)S(1)}, f32[128,128]{1,0:T(8,128)}, u32[]{:S(2)}) copy-start(f32[128,128]{1,0:T(8,128)} %refs_1_.1) | copy-start | bytes 196612
  90.3 0.7 copy-start.4
  93.5 14.9 %all-to-all-start.2 = ((f32[16,4,128]{2,1,0:T(4,128)}), f32[16,4,128]{2,1,0:T(4,128)S(1)}, u32[]{:S(2)}, u32[]{:S(2)}) async-start(f32[16,4,128]{2,1,0:T(4,128)} %get-tuple-element.16), calls=%async_computation.2 | async-start | bytes 65536 | tf_op jit(solution)/shard_map/all_to_all | solution.py:410
  102.6 5.7 %copy-start.3 = (f32[1,4,128]{2,1,0:T(4,128)S(1)}, f32[1,4,128]{2,1,0:T(4,128)}, u32[]{:S(2)}) copy-start(f32[1,4,128]{2,1,0:T(4,128)} %param.11) | copy-start | bytes 6148

commit v5 on v4

v5 whole, which is shorter than its diff:
```python
import jax
import jax.numpy as jnp
from jax import lax
from jax.experimental import pallas as pl
from jax.experimental.pallas import tpu as pltpu
from jax.sharding import PartitionSpec as P


TAYLOR = 4
BUF = 4

time_step = 0.4
half_step = 0.2
xc_factor = 0.9847450218426965


def neighbour_pair(value, axis):
    devices = lax.axis_size(axis)
    up = [(i, i + 1) for i in range(devices - 1)]
    down = [(i + 1, i) for i in range(devices - 1)]
    return lax.ppermute(value, axis, up), lax.ppermute(value, axis, down)


def rounded(value):
    return value.astype(jnp.bfloat16).astype(jnp.float32)


def spread_column(row):
    return jnp.broadcast_to(row, (row.shape[-1], row.shape[-1])).T


def laplace(ref, part, plane):
    center = ref[part, plane]
    side = center.shape[1]
    zero = jnp.zeros((1,) + center.shape[1:], jnp.float32)
    total = ref[part, plane - 1] + ref[part, plane + 1]
    total = total + jnp.concatenate([center[1:], zero]) + jnp.concatenate([zero, center[:-1]])
    level = lax.broadcasted_iota(jnp.int32, center.shape, 1)
    total = total + jnp.where(level == side - 1, 0.0, pltpu.roll(center, side - 1, 1))
    total = total + jnp.where(level == 0, 0.0, pltpu.roll(center, 1, 1))
    return total - 6.0 * center


def kinetic(edge, running, even, odd, slab, grid, exact):
    planes = 3 * slab
    cells = grid[0] * grid[1]
    now, after = even, odd
    for order in range(1, TAYLOR + 1):
        factor = time_step / (2.0 * order)
        spans = ((order, slab, 0), (slab, 2 * slab, None), (2 * slab, planes - order, 1))
        for begin, end, side in spans:
            keep = factor if side is None else edge[side] * factor

            def one(plane, carry, now=now, after=after, keep=keep, side=side, order=order):
                real = -keep * laplace(now, 1, plane)
                imag = keep * laplace(now, 0, plane)
                for part, update in enumerate((real, imag)):
                    if side is None:
                        running[part, plane - slab] = running[part, plane - slab] + update
                    if order < TAYLOR:
                        if not exact:
                            flat = update.reshape(cells, update.shape[-1])
                            update = rounded(flat).reshape(update.shape)
                        after[part, plane] = update
                return carry

            if begin < end:
                lax.fori_loop(begin, end, one, 0)
        now, after = after, now


def fill_phase(potential, row, place, cos_ref, sin_ref, slab):
    cosv = jnp.cos(half_step * potential)
    sinv = jnp.sin(half_step * potential)
    for plane in range(slab):
        cos_ref[place + plane] = spread_column(cosv[row + plane : row + plane + 1])
        sin_ref[place + plane] = spread_column(sinv[row + plane : row + plane + 1])


def start_kernel(slab, grid, scale, edge, low_ref, own_ref, high_ref, field_ref, pot,
                 partial_ref, moved_ref, adjoint_ref, cos_ref, sin_ref,
                 even, odd, running, part_ref, right):
    cells = grid[0] * grid[1]
    half = slab * cells
    lanes = own_ref.shape[-1]
    tail = 2 * half
    box = grid + (lanes,)
    for group, ref in ((0, low_ref), (2, high_ref)):
        extra = ref[tail : tail + 32].astype(jnp.float32)
        whole = extra[0:8] + extra[8:16] + extra[16:24]
        fill_phase(whole, 0, group * slab, cos_ref, sin_ref, slab)
    fill_phase(pot[...], 0, slab, cos_ref, sin_ref, slab)

    for part in range(2):
        for group, ref in enumerate((low_ref, own_ref, high_ref)):

            def begin(plane, carry, ref=ref, group=group, part=part):
                rows = pl.multiple_of((part * slab + plane) * cells, cells)
                value = ref[pl.ds(rows, cells), :].astype(jnp.float32)
                at = group * slab + plane
                real = (cos_ref[at] * value).reshape(box)
                imag = (-sin_ref[at] * value).reshape(box)
                even[0, at] = real
                even[1, at] = imag
                if group == 1:
                    running[0, plane] = real
                    running[1, plane] = imag
                return carry

            lax.fori_loop(0, slab, begin, 0)
        kinetic(edge, running, even, odd, slab, grid, True)
        for plane in range(slab):
            real, imag = turned_back(running, plane, cos_ref, sin_ref, slab)
            low = slice(plane * cells, (plane + 1) * cells)
            high = slice(half + plane * cells, half + (plane + 1) * cells)
            if part == 0:
                part_ref[0, plane] = real
                part_ref[1, plane] = imag
            else:
                kept_real = part_ref[0, plane]
                kept_imag = part_ref[1, plane]
                moved_ref[low] = (kept_real - imag).astype(jnp.bfloat16)
                moved_ref[high] = (kept_imag + real).astype(jnp.bfloat16)
                adjoint_ref[low] = (kept_real + imag).astype(jnp.bfloat16)
                adjoint_ref[high] = (real - kept_imag).astype(jnp.bfloat16)
    for place, ref in ((0, field_ref), (2, own_ref)):
        right[:half, place * lanes : (place + 1) * lanes] = ref[:half]
        right[half:, place * lanes : (place + 1) * lanes] = ref[half : 2 * half]
        right[:half, (place + 1) * lanes : (place + 2) * lanes] = ref[half : 2 * half]
        right[half:, (place + 1) * lanes : (place + 2) * lanes] = -ref[:half]
    over = contract(adjoint_ref[...], right[...]) * scale
    for index in range(4):
        piece = slice(index * lanes, (index + 1) * lanes)
        partial_ref[piece] = over[:, piece].astype(jnp.bfloat16)


def turned_back(running, plane, cos_ref, sin_ref, slab):
    shape = cos_ref.shape[1:]
    real = running[0, plane].reshape(shape)
    imag = running[1, plane].reshape(shape)
    cosv = cos_ref[slab + plane]
    sinv = sin_ref[slab + plane]
    return cosv * real + sinv * imag, cosv * imag - sinv * real


def first_kernel(slab, grid, scale, edge, low_ref, own_ref, high_ref, adjoint, cos_ref, sin_ref,
                 partial_ref, sent_ref, turned_ref, even, odd, running, right):
    cells = grid[0] * grid[1]
    half = slab * cells
    lanes = own_ref.shape[-1]
    box = grid + (lanes,)
    for group, ref in enumerate((low_ref, own_ref, high_ref)):

        def begin(plane, carry, ref=ref, group=group):
            rows = pl.multiple_of(plane * cells, cells)
            real = ref[pl.ds(rows, cells), :].astype(jnp.float32)
            imag = ref[pl.ds(half + rows, cells), :].astype(jnp.float32)
            at = group * slab + plane
            cosv = cos_ref[at]
            sinv = sin_ref[at]
            for part, value in enumerate((cosv * real + sinv * imag, cosv * imag - sinv * real)):
                even[part, at] = rounded(value).reshape(box)
                if group == 1:
                    running[part, plane] = value.reshape(box)
            return carry

        lax.fori_loop(0, slab, begin, 0)
    kinetic(edge, running, even, odd, slab, grid, False)
    for plane in range(slab):
        real, imag = turned_back(running, plane, cos_ref, sin_ref, slab)
        low = slice(plane * cells, (plane + 1) * cells)
        high = slice(half + plane * cells, half + (plane + 1) * cells)
        cosv = cos_ref[slab + plane]
        sinv = sin_ref[slab + plane]
        turned_real = cosv * real + sinv * imag
        turned_imag = cosv * imag - sinv * real
        turned_ref[low] = turned_real
        turned_ref[high] = turned_imag
        sent_ref[low] = turned_real.astype(jnp.bfloat16)
        sent_ref[high] = turned_imag.astype(jnp.bfloat16)
        first_real = real.astype(jnp.bfloat16)
        first_imag = imag.astype(jnp.bfloat16)
        right[low, :lanes] = first_real
        right[low, lanes:] = first_imag
        right[high, :lanes] = first_imag
        right[high, lanes:] = -first_real
    cross = contract(adjoint[...], right[...]) * scale
    partial_ref[:lanes] = cross[:, :lanes].astype(jnp.bfloat16)
    partial_ref[lanes:] = cross[:, lanes:].astype(jnp.bfloat16)


def second_kernel(slab, grid, edge, low, own, high, turned, cos_ref, sin_ref, second_ref,
                  even, odd, running):
    cells = grid[0] * grid[1]
    half = slab * cells
    lanes = own.shape[-1]
    box = grid + (lanes,)
    for part in range(2):
        for group, ref in enumerate((low, own, high)):

            def begin(plane, carry, ref=ref, group=group, part=part):
                at = pl.multiple_of((part * slab + plane) * cells, cells)
                value = ref[pl.ds(at, cells), :].astype(jnp.float32).reshape(box)
                even[part, group * slab + plane] = value
                if group == 1:
                    running[part, plane] = turned[pl.ds(at, cells), :].reshape(box)
                return carry

            lax.fori_loop(0, slab, begin, 0)
    kinetic(edge, running, even, odd, slab, grid, False)
    for plane in range(slab):
        real, imag = turned_back(running, plane, cos_ref, sin_ref, slab)
        at = plane * cells
        second_ref[at : at + cells] = real
        second_ref[half + at : half + at + cells] = imag


def sum_kernel(main_ref, cross_ref, out_ref):
    split = main_ref.shape[1]
    for rows, ref in ((slice(0, split), main_ref), (slice(split, None), cross_ref)):
        total = ref[0].astype(jnp.float32)
        for index in range(1, ref.shape[0]):
            total = total + ref[index].astype(jnp.float32)
        total = total.astype(jnp.bfloat16)
        for index in range(out_ref.shape[0]):
            out_ref[index, rows] = total


def back_kernel(slab, gathered, coupling, moved, start, second, occupation,
                inter_ref, field_ref, density_ref):
    lanes = coupling.shape[-1]
    half = start.shape[0] // 2
    cells = half // slab
    strength = coupling[...]
    share = 4 * lanes // gathered.shape[0]
    sums = gathered[:, :share].astype(jnp.float32).reshape(4 * lanes, lanes)
    cross = gathered[:, share:].astype(jnp.float32).reshape(2 * lanes, lanes)

    def matrix(index):
        return sums[index * lanes : (index + 1) * lanes]

    def mixed(real, imag):
        return (
            high_dot(strength, real).astype(jnp.bfloat16),
            high_dot(strength, imag).astype(jnp.bfloat16),
        )

    mix1_real, mix1_imag = mixed(matrix(0), matrix(1))
    gram_real, gram_imag = matrix(2).astype(jnp.bfloat16), matrix(3).astype(jnp.bfloat16)
    over_real = cross[:lanes] + time_step * (
        half_dot(gram_real, mix1_imag) + half_dot(gram_imag, mix1_real)
    )
    over_imag = cross[lanes:] - time_step * (
        half_dot(gram_real, mix1_real) - half_dot(gram_imag, mix1_imag)
    )
    inter_ref[:lanes] = over_real
    inter_ref[lanes:] = over_imag
    mix2_real, mix2_imag = mixed(over_real, over_imag)
    mix1_real_imag = jnp.concatenate([mix1_real, mix1_imag], axis=1)
    mix1_turned = jnp.concatenate([-mix1_imag, mix1_real], axis=1)
    mix2_real_imag = jnp.concatenate([mix2_real, mix2_imag], axis=1)
    mix2_turned = jnp.concatenate([-mix2_imag, mix2_real], axis=1)
    weight = jnp.broadcast_to(occupation[...], (8, lanes))
    for plane in range(slab):
        low = plane * cells
        real_rows = slice(low, low + cells)
        imag_rows = slice(half + low, half + low + cells)
        corr = (
            half_dot(moved[real_rows], mix1_real_imag)
            + half_dot(moved[imag_rows], mix1_turned)
            + half_dot(start[real_rows], mix2_real_imag)
            + half_dot(start[imag_rows], mix2_turned)
        )
        real = second[real_rows] + time_step * corr[:, lanes:]
        imag = second[imag_rows] - time_step * corr[:, :lanes]
        field_ref[real_rows] = real
        field_ref[imag_rows] = imag
        square = real * real + imag * imag
        dense = lax.dot_general(
            weight,
            square,
            (((1,), (1,)), ((), ())),
            precision=lax.Precision.HIGHEST,
            preferred_element_type=jnp.float32,
        )
        for owner in range(density_ref.shape[0]):
            density_ref[owner, plane : plane + 1] = dense[:1]


def tail_kernel(slab, grid, place, gathered, external, field, grid_ref, evolved_ref):
    lanes = external.shape[-1]
    half = field.shape[0] // 2
    cells = half // slab
    side = grid[1]
    own = gathered[place[4]]
    lower = gathered[place[0]]
    upper = gathered[place[1]]
    lower = pltpu.roll(lower, (lanes - place[2] * side) % lanes, 1)
    upper = pltpu.roll(upper, (2 * lanes - BUF * side - place[3] * side) % lanes, 1)
    level = lax.broadcasted_iota(jnp.int32, own.shape, 1) // side
    step = level.astype(jnp.float32)
    weight_low = (step + 1.0) / (BUF + 1.0)
    weight_high = (grid[0] - step) / (BUF + 1.0)
    low = own * weight_low + lower * (1.0 - weight_low)
    high = own * weight_high + upper * (1.0 - weight_high)
    blended = jnp.where(level < BUF, low, jnp.where(level >= grid[0] - BUF, high, own))
    root = jnp.exp(jnp.log(blended + 1e-06) * (1.0 / 3.0))
    new_grid = external[...] - xc_factor * root
    grid_ref[...] = new_grid
    cosv = jnp.cos(half_step * new_grid)
    sinv = jnp.sin(half_step * new_grid)
    for plane in range(slab):
        low_row = plane * cells
        real = field[low_row : low_row + cells]
        imag = field[half + low_row : half + low_row + cells]
        cos_b = spread_column(cosv[plane : plane + 1])
        sin_b = spread_column(sinv[plane : plane + 1])
        evolved_ref[low_row : low_row + cells] = (cos_b * real + sin_b * imag).astype(jnp.bfloat16)
        evolved_ref[half + low_row : half + low_row + cells] = (
            cos_b * imag - sin_b * real
        ).astype(jnp.bfloat16)


def contract(left, right):
    return lax.dot_general(
        left, right, (((0,), (0,)), ((), ())), preferred_element_type=jnp.float32
    )


def high_dot(left, right):
    return jnp.dot(
        left, right, precision=lax.Precision.HIGHEST, preferred_element_type=jnp.float32
    )


def half_dot(left, right):
    return jnp.dot(left, right, preferred_element_type=jnp.float32)


def pieces(value):
    high = lax.reduce_precision(value, 8, 7)
    rest = value - high
    middle = lax.reduce_precision(rest, 8, 7)
    low = rest - middle
    rows = value.shape[0]
    pad = jnp.zeros((8 - rows,) + value.shape[1:], value.dtype)
    stacked = jnp.concatenate([high, pad, middle, pad, low, pad, jnp.zeros((8,) + value.shape[1:])])
    return stacked.astype(jnp.bfloat16)


def scalars(count):
    return [pl.BlockSpec(memory_space=pltpu.SMEM)] + [
        pl.BlockSpec(memory_space=pltpu.VMEM) for _ in range(count)
    ]


def shards(orbitals, initial, potential, external, occupation, coupling, neighbours, offsets):
    slab, rows_y, cols_z, orbits = initial.shape[2:]
    grid = (rows_y, cols_z)
    cells = rows_y * cols_z
    rows = 2 * slab * cells
    start = initial.reshape(rows, orbits)
    devices = lax.axis_size("space")
    place = lax.axis_index("space")
    f32, bf16 = jnp.float32, jnp.bfloat16
    edge = jnp.stack([place > 0, place < devices - 1]).astype(f32)
    planes = (2, 3 * slab) + grid + (orbits,)
    stencil = [pltpu.VMEM(planes, f32), pltpu.VMEM(planes, f32)]
    stencil = stencil + [pltpu.VMEM((2, slab) + grid + (orbits,), f32)]
    shape = jax.ShapeDtypeStruct
    orbs = orbitals.reshape(rows, orbits)
    message = jnp.concatenate([start, pieces(potential[0])])
    low_m, high_m = neighbour_pair(message, "space")
    low_o, high_o = neighbour_pair(orbs, "space")
    scale = 1.0 / (slab * devices * cells)
    turn = shape((3 * slab, cells, orbits), f32)

    def limit(mib):
        return pltpu.CompilerParams(vmem_limit_bytes=mib << 20)

    def shared(value):
        share = value.shape[0] // devices
        parts = lax.all_to_all(
            value.reshape(devices, share, orbits), "space", 0, 0, tiled=True
        )
        return parts

    partial, moved, adjoint, cosv, sinv = pl.pallas_call(
        lambda *refs: start_kernel(slab, grid, scale, *refs),
        out_shape=(
            shape((4 * orbits, orbits), bf16),
            shape((rows, orbits), bf16),
            shape((rows, orbits), bf16),
            turn,
            turn,
        ),
        in_specs=scalars(5),
        scratch_shapes=stencil
        + [
            pltpu.VMEM((2, slab, cells, orbits), f32),
            pltpu.VMEM((rows, 4 * orbits), bf16),
        ],
        compiler_params=limit(16),
        name="start",
    )(edge, low_m, start, high_m, orbs, potential[0])
    parts = shared(partial)
    partial, sent, turned = pl.pallas_call(
        lambda *refs: first_kernel(slab, grid, scale, *refs),
        out_shape=(
            shape((2 * orbits, orbits), bf16),
            shape((rows, orbits), bf16),
            shape((rows, orbits), f32),
        ),
        in_specs=scalars(6),
        scratch_shapes=stencil + [pltpu.VMEM((rows, 2 * orbits), bf16)],
        compiler_params=limit(14),
        name="first",
    )(edge, low_o, orbs, high_o, adjoint, cosv, sinv)
    cross_parts = shared(partial)
    low_s, high_s = neighbour_pair(sent, "space")
    spread = pl.pallas_call(
        sum_kernel,
        out_shape=shape((devices, 6 * orbits // devices, orbits), bf16),
        compiler_params=limit(6),
        name="total",
    )(parts, cross_parts)
    sums = lax.all_to_all(spread, "space", 0, 0, tiled=True)
    second = pl.pallas_call(
        lambda *refs: second_kernel(slab, grid, *refs),
        out_shape=shape((rows, orbits), f32),
        in_specs=scalars(6),
        scratch_shapes=stencil,
        compiler_params=limit(12),
        name="second",
    )(edge, low_s, sent, high_s, turned, cosv, sinv)

    domain_count = neighbours.shape[0]
    intersection, field, density = pl.pallas_call(
        lambda *refs: back_kernel(slab, *refs),
        out_shape=(
            shape((2 * orbits, orbits), f32),
            shape((rows, orbits), f32),
            shape((domain_count, slab, cells), f32),
        ),
        compiler_params=limit(14),
        name="back",
    )(sums, coupling, moved, start, second, occupation.reshape(1, orbits))
    gathered = lax.all_to_all(density, "dom", 0, 0, tiled=True)
    own_index = lax.axis_index("dom")
    mine = lax.dynamic_index_in_dim(neighbours, own_index, 0, keepdims=False)
    shift = lax.dynamic_index_in_dim(offsets, own_index, 0, keepdims=False)
    where = jnp.concatenate([mine, shift, own_index.reshape(1).astype(jnp.int32)])
    new_grid, evolved = pl.pallas_call(
        lambda *refs: tail_kernel(slab, grid, *refs),
        out_shape=(shape((slab, cells), f32), shape((rows, orbits), bf16)),
        in_specs=scalars(3),
        compiler_params=limit(8),
        name="tail",
    )(where, gathered, external[0], field)
    return (
        evolved.reshape(orbitals.shape),
        intersection.reshape(1, 2, orbits, orbits),
        new_grid[None],
    )


def solution(mesh):
    return jax.shard_map(
        shards,
        mesh=mesh,
        in_specs=(
            P("dom", None, "space", None, None, None),
            P("dom", None, "space", None, None, None),
            P("dom", "space", None),
            P("dom", "space", None),
            P(),
            P(),
            P(),
            P(),
        ),
        out_specs=(
            P("dom", None, "space", None, None, None),
            P("dom", None, None, None),
            P("dom", "space", None),
        ),
        check_vma=False,
    )
```

time: 110 us -> 125 us (1.14)
  the two profiles are of different devices: /device:TPU:1 before, /device:TPU:5 now
where the time goes in v5:
time: 125 us
  starting transfers between devices  45.1 us (36%)
  blocking collectives  35.3 us (28%)
  waiting for transfers between devices  18.7 us (15%)
  Pallas kernels  16.9 us (14%)
  local copies, waits for them, and re-layouts  6.98 us (6%)
    all_to_all x2, blocking collectives, shared(): lax.all_to_all(value.reshape(devices, share, orbits), 'space', 0, 0, tile...  35.3 us
    ppermute x6, starting transfers between devices, neighbour_pair(): return (lax.ppermute(value, axis, up), lax.ppermute(value, axis, down))  28.1 us
    ppermute x6, waiting for transfers between devices, neighbour_pair(): return (lax.ppermute(value, axis, up), lax.ppermute(value, axis, down))  13 us
    all_to_all x1, starting transfers between devices, shards(): gathered = lax.all_to_all(density, 'dom', 0, 0, tiled=True)  10.7 us
    all_to_all x1, starting transfers between devices, shards(): sums = lax.all_to_all(spread, 'space', 0, 0, tiled=True)  6.31 us
    all_to_all x1, waiting for transfers between devices, shards(): gathered = lax.all_to_all(density, 'dom', 0, 0, tiled=True)  5.72 us
    unnamed x28, local copies, waits for them, and re-layouts  5.61 us
    pallas_call x1, Pallas kernels, shards(): pl.pallas_call(lambda *refs: start_kernel(slab, grid, scale, *refs), out_...  5.46 us
  transfers between devices with their start and end apart: 8, of which 5 were waited for; matrix products, arithmetic and copies ran while one was open for 0% of the time, Pallas kernels for 7%

profile of v5, /device:TPU:5, one launch (start us, length us, event | category | flops | bytes accessed | tf_op | source)
XLA Modules:
  0.0 124.7 jit_solution(12429714698139052662)
XLA Ops:
  0.6 0.7 fusion
  1.3 0.0 copy-start.1
  1.3 0.0 copy-start
  1.4 1.2 concatenate.10
  2.5 11.1 %collective-permute-start.1 = (bf16[1056,128]{1,0:T(8,128)(2,1)S(1)}, bf16[1056,128]{1,0:T(8,128)(2,1)S(1)}, u32[]{:S(2)}, u32[]{:S(2)}) collective-permute-start(bf16[1056,128]{1,0:T(8,128)(2,1)S(1)} %concatenate.10), channel_id=1, source_target_pairs={{1,0},{2,1},{3,2},{4,3},{5,4},{6,5},{7,6},{8,7},{9,8},{10,9},{11,1... | collective-permute-start | bytes 811016 | tf_op jit(solution)/shard_map/ppermute | solution.py:21
  13.6 1.9 %collective-permute-start = (bf16[1056,128]{1,0:T(8,128)(2,1)S(1)}, bf16[1056,128]{1,0:T(8,128)(2,1)S(1)}, u32[]{:S(2)}, u32[]{:S(2)}) collective-permute-start(bf16[1056,128]{1,0:T(8,128)(2,1)S(1)} %concatenate.10), channel_id=1, source_target_pairs={{0,1},{1,2},{2,3},{3,4},{4,5},{5,6},{6,7},{7,8},{8,9},{9,10},{10,1... | collective-permute-start | bytes 811016 | tf_op jit(solution)/shard_map/ppermute | solution.py:21
  15.5 0.0 copy-done.1
  15.5 7.0 %collective-permute-start.3 = (bf16[1024,128]{1,0:T(8,128)(2,1)S(1)}, bf16[1024,128]{1,0:T(8,128)(2,1)S(1)}, u32[]{:S(2)}, u32[]{:S(2)}) collective-permute-start(bf16[1024,128]{1,0:T(8,128)(2,1)S(1)} %bitcast.19), channel_id=1, source_target_pairs={{1,0},{2,1},{3,2},{4,3},{5,4},{6,5},{7,6},{8,7},{9,8},{10,9},{11,1... | collective-permute-start | bytes 786440 | tf_op jit(solution)/shard_map/ppermute | solution.py:21
  22.5 1.9 %collective-permute-start.2 = (bf16[1024,128]{1,0:T(8,128)(2,1)S(1)}, bf16[1024,128]{1,0:T(8,128)(2,1)}, u32[]{:S(2)}, u32[]{:S(2)}) collective-permute-start(bf16[1024,128]{1,0:T(8,128)(2,1)S(1)} %bitcast.20), channel_id=1, source_target_pairs={{0,1},{1,2},{2,3},{3,4},{4,5},{5,6},{6,7},{7,8},{8,9},{9,10},{10,1... | collective-permute-start | bytes 786440 | tf_op jit(solution)/shard_map/ppermute | solution.py:21
  24.4 0.0 copy-start.9
  24.4 0.1 add_convert_fusion.refs_0_
  24.5 0.0 collective-permute-done.1.refs_3_
  24.5 1.6 %collective-permute-done.refs_1_ = bf16[1056,128]{1,0:T(8,128)(2,1)S(1)} collective-permute-done((bf16[1056,128]{1,0:T(8,128)(2,1)S(1)}, bf16[1056,128]{1,0:T(8,128)(2,1)S(1)}, u32[]{:S(2)}, u32[]{:S(2)}) %collective-permute-start) | collective-permute-done | bytes 270368 | tf_op jit(solution)/shard_map/ppermute | solution.py:21
  26.2 0.0 copy-done
  26.2 0.0 copy-done.9
  26.2 5.5 %start.1 = (bf16[512,128]{1,0:T(8,128)(2,1)S(1)}, bf16[1024,128]{1,0:T(8,128)(2,1)S(1)}, bf16[1024,128]{1,0:T(8,128)(2,1)S(1)}, f32[12,128,128]{2,1,0:T(8,128)S(1)}, f32[12,128,128]{2,1,0:T(8,128)S(1)}) custom-call(f32[2]{0:T(128)S(1)} %add_convert_fusion.refs_0_, bf16[1056,128]{1,0:T(8,128)(2,1)S(1)} %collective-permute-done.refs_1_, ...), custom_call_target="tpu_custom_call" | custom-call | tf_op jit(solution)/shard_map/start/pallas_call | solution.py:388
  31.6 0.0 collective-permute-done.3.refs_3_
  31.6 0.0 copy-start.6
  31.7 0.7 copy-done.6
  32.3 2.1 %collective-permute-done.2.refs_1_ = bf16[1024,128]{1,0:T(8,128)(2,1)} collective-permute-done((bf16[1024,128]{1,0:T(8,128)(2,1)S(1)}, bf16[1024,128]{1,0:T(8,128)(2,1)}, u32[]{:S(2)}, u32[]{:S(2)}) %collective-permute-start.2) | collective-permute-done | bytes 262176 | tf_op jit(solution)/shard_map/ppermute | solution.py:21
  34.5 0.0 copy-start.7
  34.5 0.9 copy-done.7
  35.4 3.6 %first.1 = (bf16[256,128]{1,0:T(8,128)(2,1)S(1)}, bf16[1024,128]{1,0:T(8,128)(2,1)S(1)}, f32[1024,128]{1,0:T(8,128)S(1)}) custom-call(f32[2]{0:T(128)S(1)} %add_convert_fusion.refs_0_, bf16[1024,128]{1,0:T(8,128)(2,1)} %collective-permute-done.2.refs_1_, bf16[1024,128]{1,0:T(8,128)(2,1)S(1)} %bitcast.22, bf16[1024,128]{1,0:T(8,128)(2,1)S(1)} %copy-done.7, ...), custom_call_target="tpu_custom_call" | custom-call | tf_op jit(solution)/shard_map/first/pallas_call | solution.py:407
  39.0 0.0 copy-start.2
  39.0 16.4 %all_to_all.20.cross_ref = bf16[32,8,128]{2,1,0:T(8,128)(2,1)S(1)} all-to-all(bf16[32,8,128]{2,1,0:T(8,128)(2,1)S(1)} %bitcast.24), channel_id=1, replica_groups=mesh['dom'=16,'space'=32] {'space'}, dimensions={0} | all-to-all | bytes 131072 | tf_op jit(solution)/shard_map/all_to_all | solution.py:383
  55.4 18.9 %all_to_all.21.main_ref = bf16[32,16,128]{2,1,0:T(8,128)(2,1)S(1)} all-to-all(bf16[32,16,128]{2,1,0:T(8,128)(2,1)S(1)} %bitcast.23), channel_id=1, replica_groups=mesh['dom'=16,'space'=32] {'space'}, dimensions={0} | all-to-all | bytes 262144 | tf_op jit(solution)/shard_map/all_to_all | solution.py:383
  74.3 0.7 total.1
  75.1 6.3 %all-to-all-start.2 = ((bf16[32,24,128]{2,1,0:T(8,128)(2,1)}), bf16[32,24,128]{2,1,0:T(8,128)(2,1)S(1)}, u32[]{:S(2)}, u32[]{:S(2)}) async-start(bf16[32,24,128]{2,1,0:T(8,128)(2,1)} %total.1), calls=%async_computation.2 | async-start | bytes 393216 | tf_op jit(solution)/shard_map/all_to_all | solution.py:427
  81.4 4.3 %collective-permute-start.5 = (bf16[1024,128]{1,0:T(8,128)(2,1)S(1)}, bf16[1024,128]{1,0:T(8,128)(2,1)S(1)}, u32[]{:S(2)}, u32[]{:S(2)}) collective-permute-start(bf16[1024,128]{1,0:T(8,128)(2,1)S(1)} %get-tuple-element.22.refs_2_), channel_id=1, source_target_pairs={{1,0},{2,1},{3,2},{4,3},{5,4},{6,5},{7,6},{8,7},{9,8},{10,9},{11,1... | collective-permute-start | bytes 786440 | tf_op jit(solution)/shard_map/ppermute | solution.py:21
  85.7 0.0 copy-done.2
  85.7 1.9 %collective-permute-start.4 = (bf16[1024,128]{1,0:T(8,128)(2,1)S(1)}, bf16[1024,128]{1,0:T(8,128)(2,1)}, u32[]{:S(2)}, u32[]{:S(2)}) collective-permute-start(bf16[1024,128]{1,0:T(8,128)(2,1)S(1)} %get-tuple-element.22.refs_2_), channel_id=1, source_target_pairs={{0,1},{1,2},{2,3},{3,4},{4,5},{5,6},{6,7},{7,8},{8,9},{9,10},{10,1... | collective-permute-start | bytes 786440 | tf_op jit(solution)/shard_map/ppermute | solution.py:21
  87.6 0.0 copy-start.12
  87.6 0.0 copy-start.13
  87.7 0.7 copy-done.12
  88.3 0.0 copy-done.13
  88.3 0.2 dynamic-slice_reduce_fusion
  88.5 5.8 %collective-permute-done.5.refs_3_ = bf16[1024,128]{1,0:T(8,128)(2,1)S(1)} collective-permute-done((bf16[1024,128]{1,0:T(8,128)(2,1)S(1)}, bf16[1024,128]{1,0:T(8,128)(2,1)S(1)}, u32[]{:S(2)}, u32[]{:S(2)}) %collective-permute-start.5) | collective-permute-done | bytes 262176 | tf_op jit(solution)/shard_map/ppermute | solution.py:21
  94.4 0.0 copy-start.4
  94.4 0.7 copy-done.4
  95.1 3.4 %collective-permute-done.4.refs_1_ = bf16[1024,128]{1,0:T(8,128)(2,1)} collective-permute-done((bf16[1024,128]{1,0:T(8,128)(2,1)S(1)}, bf16[1024,128]{1,0:T(8,128)(2,1)}, u32[]{:S(2)}, u32[]{:S(2)}) %collective-permute-start.4) | collective-permute-done | bytes 262176 | tf_op jit(solution)/shard_map/ppermute | solution.py:21
  98.5 0.0 copy-start.3
  98.5 0.9 copy-done.3
  99.4 0.0 copy-start.5
  99.4 0.9 copy-done.5
  100.4 0.0 copy-start.8
  100.4 3.1 %second.1.refs_4_ = f32[1024,128]{1,0:T(8,128)S(1)} custom-call(f32[2]{0:T(128)S(1)} %add_convert_fusion.refs_0_, bf16[1024,128]{1,0:T(8,128)(2,1)} %collective-permute-done.4.refs_1_, bf16[1024,128]{1,0:T(8,128)(2,1)S(1)} %copy-done.3, bf16[1024,128]{1,0:T(8,128)(2,1)S(1)} %copy-done.5, f32[1024,128]{1,0:T(8,128)S(1)} %get-tuple-element.23.refs_4_, ...), custom_call_target="tpu_custom_call" | custom-call | tf_op jit(solution)/shard_map/second/pallas_call | solution.py:428
  103.5 0.0 all-to-all-done.2.refs_0_
  103.5 0.0 copy-start.11
  103.5 0.0 copy-done.8
  103.5 0.6 copy-done.11
  104.1 2.5 %back.1 = (f32[256,128]{1,0:T(8,128)}, f32[1024,128]{1,0:T(8,128)S(1)}, f32[16,4,128]{2,1,0:T(4,128)}) custom-call(bf16[32,24,128]{2,1,0:T(8,128)(2,1)S(1)} %all-to-all-done.2.refs_0_, f32[128,128]{1,0:T(8,128)S(1)} %copy-done.8, bf16[1024,128]{1,0:T(8,128)(2,1)S(1)} %get-tuple-element.21.refs_2_, bf16[1024,128]{1,0:T(8,128)(2,1)S(1)} %bitcast.18, ...), custom_call_target="tpu_custom_call" | custom-call | tf_op jit(solution)/shard_map/back/pallas_call | solution.py:438
  106.6 10.7 %all-to-all-start.3 = ((f32[16,4,128]{2,1,0:T(4,128)}), f32[16,4,128]{2,1,0:T(4,128)S(1)}, u32[]{:S(2)}, u32[]{:S(2)}) async-start(f32[16,4,128]{2,1,0:T(4,128)} %get-tuple-element.24), calls=%async_computation.3 | async-start | bytes 65536 | tf_op jit(solution)/shard_map/all_to_all | solution.py:448
  117.3 0.1 pad_add_fusion.refs_0_
  117.4 0.0 copy-start.10
  117.4 5.7 %all-to-all-done.3.refs_1_ = f32[16,4,128]{2,1,0:T(4,128)S(1)} async-done(((f32[16,4,128]{2,1,0:T(4,128)}), f32[16,4,128]{2,1,0:T(4,128)S(1)}, u32[]{:S(2)}, u32[]{:S(2)}) %all-to-all-start.3) | async-done | bytes 32800 | tf_op jit(solution)/shard_map/all_to_all | solution.py:448
  123.1 0.0 copy-done.10
  123.2 1.6 %tail.1 = (f32[4,128]{1,0:T(4,128)}, bf16[1024,128]{1,0:T(8,128)(2,1)}) custom-call(s32[5]{0:T(128)S(1)} %pad_add_fusion.refs_0_, f32[16,4,128]{2,1,0:T(4,128)S(1)} %all-to-all-done.3.refs_1_, f32[4,128]{1,0:T(4,128)S(1)} %bitcast.26, f32[1024,128]{1,0:T(8,128)S(1)} %get-tuple-element.25.refs_3_), custom_call_target="tpu_custom_call" | custom-call | tf_op jit(solution)/shard_map/tail/pallas_call | solution.py:453
  (2 shorter events, 0.0 us)
Async XLA Ops:
  1.3 14.2 %copy-start.1 = (bf16[1,2,4,16,8,128]{5,4,3,2,1,0:T(8,128)(2,1)S(1)}, bf16[1,2,4,16,8,128]{5,4,3,2,1,0:T(8,128)(2,1)}, u32[]{:S(2)}) copy-start(bf16[1,2,4,16,8,128]{5,4,3,2,1,0:T(8,128)(2,1)} %param.8) | copy-start | bytes 786436
  1.3 24.8 %copy-start = (bf16[1,2,4,16,8,128]{5,4,3,2,1,0:T(8,128)(2,1)S(1)}, bf16[1,2,4,16,8,128]{5,4,3,2,1,0:T(8,128)(2,1)}, u32[]{:S(2)}) copy-start(bf16[1,2,4,16,8,128]{5,4,3,2,1,0:T(8,128)(2,1)} %param.9) | copy-start | bytes 786436
  2.5 22.0 %collective-permute-start.1 = (bf16[1056,128]{1,0:T(8,128)(2,1)S(1)}, bf16[1056,128]{1,0:T(8,128)(2,1)S(1)}, u32[]{:S(2)}, u32[]{:S(2)}) collective-permute-start(bf16[1056,128]{1,0:T(8,128)(2,1)S(1)} %concatenate.10), channel_id=1, source_target_pairs={{1,0},{2,1},{3,2},{4,3},{5,4},{6,5},{7,6},{8,7},{9,8},{10,9},{11,1... | collective-permute-start | bytes 811016 | tf_op jit(solution)/shard_map/ppermute | solution.py:21
  13.6 12.6 %collective-permute-start = (bf16[1056,128]{1,0:T(8,128)(2,1)S(1)}, bf16[1056,128]{1,0:T(8,128)(2,1)S(1)}, u32[]{:S(2)}, u32[]{:S(2)}) collective-permute-start(bf16[1056,128]{1,0:T(8,128)(2,1)S(1)} %concatenate.10), channel_id=1, source_target_pairs={{0,1},{1,2},{2,3},{3,4},{4,5},{5,6},{6,7},{7,8},{8,9},{9,10},{10,1... | collective-permute-start | bytes 811016 | tf_op jit(solution)/shard_map/ppermute | solution.py:21
  15.5 16.1 %collective-permute-start.3 = (bf16[1024,128]{1,0:T(8,128)(2,1)S(1)}, bf16[1024,128]{1,0:T(8,128)(2,1)S(1)}, u32[]{:S(2)}, u32[]{:S(2)}) collective-permute-start(bf16[1024,128]{1,0:T(8,128)(2,1)S(1)} %bitcast.19), channel_id=1, source_target_pairs={{1,0},{2,1},{3,2},{4,3},{5,4},{6,5},{7,6},{8,7},{9,8},{10,9},{11,1... | collective-permute-start | bytes 786440 | tf_op jit(solution)/shard_map/ppermute | solution.py:21
  22.5 12.0 %collective-permute-start.2 = (bf16[1024,128]{1,0:T(8,128)(2,1)S(1)}, bf16[1024,128]{1,0:T(8,128)(2,1)}, u32[]{:S(2)}, u32[]{:S(2)}) collective-permute-start(bf16[1024,128]{1,0:T(8,128)(2,1)S(1)} %bitcast.20), channel_id=1, source_target_pairs={{0,1},{1,2},{2,3},{3,4},{4,5},{5,6},{6,7},{7,8},{8,9},{9,10},{10,1... | collective-permute-start | bytes 786440 | tf_op jit(solution)/shard_map/ppermute | solution.py:21
  24.4 1.7 %copy-start.9 = (f32[1,4,128]{2,1,0:T(4,128)S(1)}, f32[1,4,128]{2,1,0:T(4,128)}, u32[]{:S(2)}) copy-start(f32[1,4,128]{2,1,0:T(4,128)} %param.10) | copy-start | bytes 6148
  31.6 0.7 copy-start.6
  34.5 1.0 copy-start.7
  39.0 46.7 %copy-start.2 = (bf16[1024,128]{1,0:T(8,128)(2,1)}, bf16[1024,128]{1,0:T(8,128)(2,1)S(1)}, u32[]{:S(2)}) copy-start(bf16[1024,128]{1,0:T(8,128)(2,1)S(1)} %get-tuple-element.22.refs_2_) | copy-start | bytes 786436
  75.1 28.4 %all-to-all-start.2 = ((bf16[32,24,128]{2,1,0:T(8,128)(2,1)}), bf16[32,24,128]{2,1,0:T(8,128)(2,1)S(1)}, u32[]{:S(2)}, u32[]{:S(2)}) async-start(bf16[32,24,128]{2,1,0:T(8,128)(2,1)} %total.1), calls=%async_computation.2 | async-start | bytes 393216 | tf_op jit(solution)/shard_map/all_to_all | solution.py:427
  81.4 13.0 %collective-permute-start.5 = (bf16[1024,128]{1,0:T(8,128)(2,1)S(1)}, bf16[1024,128]{1,0:T(8,128)(2,1)S(1)}, u32[]{:S(2)}, u32[]{:S(2)}) collective-permute-start(bf16[1024,128]{1,0:T(8,128)(2,1)S(1)} %get-tuple-element.22.refs_2_), channel_id=1, source_target_pairs={{1,0},{2,1},{3,2},{4,3},{5,4},{6,5},{7,6},{8,7},{9,8},{10,9},{11,1... | collective-permute-start | bytes 786440 | tf_op jit(solution)/shard_map/ppermute | solution.py:21
  85.7 12.8 %collective-permute-start.4 = (bf16[1024,128]{1,0:T(8,128)(2,1)S(1)}, bf16[1024,128]{1,0:T(8,128)(2,1)}, u32[]{:S(2)}, u32[]{:S(2)}) collective-permute-start(bf16[1024,128]{1,0:T(8,128)(2,1)S(1)} %get-tuple-element.22.refs_2_), channel_id=1, source_target_pairs={{0,1},{1,2},{2,3},{3,4},{4,5},{5,6},{6,7},{7,8},{8,9},{9,10},{10,1... | collective-permute-start | bytes 786440 | tf_op jit(solution)/shard_map/ppermute | solution.py:21
  87.6 0.7 copy-start.12
  87.6 0.7 copy-start.13
  94.4 0.7 copy-start.4
  98.5 1.0 copy-start.3
  99.4 0.9 copy-start.5
  100.4 3.1 %copy-start.8 = (f32[128,128]{1,0:T(8,128)S(1)}, f32[128,128]{1,0:T(8,128)}, u32[]{:S(2)}) copy-start(f32[128,128]{1,0:T(8,128)} %refs_1_.1) | copy-start | bytes 196612
  103.5 0.7 copy-start.11
  106.6 16.5 %all-to-all-start.3 = ((f32[16,4,128]{2,1,0:T(4,128)}), f32[16,4,128]{2,1,0:T(4,128)S(1)}, u32[]{:S(2)}, u32[]{:S(2)}) async-start(f32[16,4,128]{2,1,0:T(4,128)} %get-tuple-element.24), calls=%async_computation.3 | async-start | bytes 65536 | tf_op jit(solution)/shard_map/all_to_all | solution.py:448
  117.4 5.7 %copy-start.10 = (f32[1,4,128]{2,1,0:T(4,128)S(1)}, f32[1,4,128]{2,1,0:T(4,128)}, u32[]{:S(2)}) copy-start(f32[1,4,128]{2,1,0:T(4,128)} %param.11) | copy-start | bytes 6148

commit v6 on v5

--- a/solution.py
+++ b/solution.py
@@ -143,7 +143,7 @@
     return cosv * real + sinv * imag, cosv * imag - sinv * real
 
 
-def first_kernel(slab, grid, scale, edge, low_ref, own_ref, high_ref, adjoint, cos_ref, sin_ref,
+def first_kernel(slab, grid, scale, edge, low_ref, own_ref, high_ref, adjoint, cos_ref, sin_ref, over,
                  partial_ref, sent_ref, turned_ref, even, odd, running, right):
     cells = grid[0] * grid[1]
     half = slab * cells
@@ -185,8 +185,10 @@
         right[high, :lanes] = first_imag
         right[high, lanes:] = -first_real
     cross = contract(adjoint[...], right[...]) * scale
-    partial_ref[:lanes] = cross[:, :lanes].astype(jnp.bfloat16)
-    partial_ref[lanes:] = cross[:, lanes:].astype(jnp.bfloat16)
+    partial_ref[: 2 * lanes] = over[: 2 * lanes]
+    partial_ref[2 * lanes : 3 * lanes] = cross[:, :lanes].astype(jnp.bfloat16)
+    partial_ref[3 * lanes : 4 * lanes] = cross[:, lanes:].astype(jnp.bfloat16)
+    partial_ref[4 * lanes :] = over[2 * lanes :]
 
 
 def second_kernel(slab, grid, edge, low, own, high, turned, cos_ref, sin_ref, second_ref,
@@ -215,26 +217,21 @@
         second_ref[half + at : half + at + cells] = imag
 
 
-def sum_kernel(main_ref, cross_ref, out_ref):
-    split = main_ref.shape[1]
-    for rows, ref in ((slice(0, split), main_ref), (slice(split, None), cross_ref)):
-        total = ref[0].astype(jnp.float32)
-        for index in range(1, ref.shape[0]):
-            total = total + ref[index].astype(jnp.float32)
-        total = total.astype(jnp.bfloat16)
-        for index in range(out_ref.shape[0]):
-            out_ref[index, rows] = total
-
-
-def back_kernel(slab, gathered, coupling, moved, start, second, occupation,
+def sum_kernel(parts_ref, out_ref):
+    total = parts_ref[0].astype(jnp.float32)
+    for index in range(1, parts_ref.shape[0]):
+        total = total + parts_ref[index].astype(jnp.float32)
+    total = total.astype(jnp.bfloat16)
+    for index in range(out_ref.shape[0]):
+        out_ref[index] = total
+
+
+def back_kernel(slab, sums, coupling, moved, start, second, occupation,
                 inter_ref, field_ref, density_ref):
     lanes = coupling.shape[-1]
     half = start.shape[0] // 2
     cells = half // slab
     strength = coupling[...]
-    share = 4 * lanes // gathered.shape[0]
-    sums = gathered[:, :share].astype(jnp.float32).reshape(4 * lanes, lanes)
-    cross = gathered[:, share:].astype(jnp.float32).reshape(2 * lanes, lanes)
 
     def matrix(index):
         return sums[index * lanes : (index + 1) * lanes]
@@ -245,12 +242,14 @@
             high_dot(strength, imag).astype(jnp.bfloat16),
         )
 
-    mix1_real, mix1_imag = mixed(matrix(0), matrix(1))
-    gram_real, gram_imag = matrix(2).astype(jnp.bfloat16), matrix(3).astype(jnp.bfloat16)
-    over_real = cross[:lanes] + time_step * (
+    mix1_real, mix1_imag = mixed(
+        matrix(0).astype(jnp.float32), matrix(1).astype(jnp.float32)
+    )
+    gram_real, gram_imag = matrix(4), matrix(5)
+    over_real = matrix(2).astype(jnp.float32) + time_step * (
         half_dot(gram_real, mix1_imag) + half_dot(gram_imag, mix1_real)
     )
-    over_imag = cross[lanes:] - time_step * (
+    over_imag = matrix(3).astype(jnp.float32) - time_step * (
         half_dot(gram_real, mix1_real) - half_dot(gram_imag, mix1_imag)
     )
     inter_ref[:lanes] = over_real
@@ -337,15 +336,16 @@
     return jnp.dot(left, right, preferred_element_type=jnp.float32)
 
 
-def pieces(value):
-    high = lax.reduce_precision(value, 8, 7)
-    rest = value - high
-    middle = lax.reduce_precision(rest, 8, 7)
-    low = rest - middle
-    rows = value.shape[0]
-    pad = jnp.zeros((8 - rows,) + value.shape[1:], value.dtype)
-    stacked = jnp.concatenate([high, pad, middle, pad, low, pad, jnp.zeros((8,) + value.shape[1:])])
-    return stacked.astype(jnp.bfloat16)
+def pack_kernel(start_ref, pot, out_ref):
+    rows = start_ref.shape[0]
+    value = pot[...]
+    high = rounded(value)
+    middle = rounded(value - high)
+    low = value - high - middle
+    pad = jnp.zeros((8 - value.shape[0], value.shape[1]), value.dtype)
+    none = jnp.zeros((8, value.shape[1]), value.dtype)
+    out_ref[:rows] = start_ref[...]
+    out_ref[rows:] = jnp.concatenate([high, pad, middle, pad, low, pad, none]).astype(jnp.bfloat16)
 
 
 def scalars(count):
@@ -369,7 +369,12 @@
     stencil = stencil + [pltpu.VMEM((2, slab) + grid + (orbits,), f32)]
     shape = jax.ShapeDtypeStruct
     orbs = orbitals.reshape(rows, orbits)
-    message = jnp.concatenate([start, pieces(potential[0])])
+    message = pl.pallas_call(
+        pack_kernel,
+        out_shape=shape((rows + 32, orbits), bf16),
+        compiler_params=pltpu.CompilerParams(vmem_limit_bytes=3 << 20),
+        name="pack",
+    )(start, potential[0])
     low_m, high_m = neighbour_pair(message, "space")
     low_o, high_o = neighbour_pair(orbs, "space")
     scale = 1.0 / (slab * devices * cells)
@@ -378,14 +383,7 @@
     def limit(mib):
         return pltpu.CompilerParams(vmem_limit_bytes=mib << 20)
 
-    def shared(value):
-        share = value.shape[0] // devices
-        parts = lax.all_to_all(
-            value.reshape(devices, share, orbits), "space", 0, 0, tiled=True
-        )
-        return parts
-
-    partial, moved, adjoint, cosv, sinv = pl.pallas_call(
+    over, moved, adjoint, cosv, sinv = pl.pallas_call(
         lambda *refs: start_kernel(slab, grid, scale, *refs),
         out_shape=(
             shape((4 * orbits, orbits), bf16),
@@ -402,29 +400,30 @@
         ],
         compiler_params=limit(16),
         name="start",
-    )(edge, low_m, start, high_m, orbs, potential[0])
-    parts = shared(partial)
+    )(edge, low_m, message, high_m, orbs, potential[0])
     partial, sent, turned = pl.pallas_call(
         lambda *refs: first_kernel(slab, grid, scale, *refs),
         out_shape=(
-            shape((2 * orbits, orbits), bf16),
+            shape((6 * orbits, orbits), bf16),
             shape((rows, orbits), bf16),
             shape((rows, orbits), f32),
         ),
-        in_specs=scalars(6),
+        in_specs=scalars(7),
         scratch_shapes=stencil + [pltpu.VMEM((rows, 2 * orbits), bf16)],
         compiler_params=limit(14),
         name="first",
-    )(edge, low_o, orbs, high_o, adjoint, cosv, sinv)
-    cross_parts = shared(partial)
+    )(edge, low_o, orbs, high_o, adjoint, cosv, sinv, over)
+    share = 6 * orbits // devices
+    parts = lax.all_to_all(partial.reshape(devices, share, orbits), "space", 0, 0, tiled=True)
     low_s, high_s = neighbour_pair(sent, "space")
     spread = pl.pallas_call(
         sum_kernel,
-        out_shape=shape((devices, 6 * orbits // devices, orbits), bf16),
+        out_shape=shape((devices, share, orbits), bf16),
         compiler_params=limit(6),
         name="total",
-    )(parts, cross_parts)
+    )(parts)
     sums = lax.all_to_all(spread, "space", 0, 0, tiled=True)
+    sums = sums.reshape(6 * orbits, orbits)
     second = pl.pallas_call(
         lambda *refs: second_kernel(slab, grid, *refs),
         out_shape=shape((rows, orbits), f32),

time: 125 us -> 110 us (0.88)
  blocking collectives: 35.3 us -> 19.9 us
  local copies, waits for them, and re-layouts: 6.98 us -> 9.06 us
    all_to_all x2 -> x1, blocking collectives: 35.3 us -> 19.9 us  [shards(): lax.all_to_all(partial.reshape(devices, share, orbits), 'space', 0, 0, ti...]
    unnamed x28 -> x34, local copies, waits for them, and re-layouts: 5.61 us -> 8.84 us
where the time goes in v6:
time: 110 us; the launch traced here: 109 us
  starting transfers between devices  44.9 us (41%)
  blocking collectives  19.9 us (18%)
  waiting for transfers between devices  18.1 us (16%)
  Pallas kernels  16.5 us (15%)
  local copies, waits for them, and re-layouts  9.06 us (8%)
    ppermute x6, starting transfers between devices, neighbour_pair(): return (lax.ppermute(value, axis, up), lax.ppermute(value, axis, down))  28.2 us
    all_to_all x1, blocking collectives, shards(): lax.all_to_all(partial.reshape(devices, share, orbits), 'space', 0, 0, ti...  19.9 us
    ppermute x6, waiting for transfers between devices, neighbour_pair(): return (lax.ppermute(value, axis, up), lax.ppermute(value, axis, down))  12.4 us
    all_to_all x1, starting transfers between devices, shards(): gathered = lax.all_to_all(density, 'dom', 0, 0, tiled=True)  9.77 us
    unnamed x34, local copies, waits for them, and re-layouts  8.84 us
    all_to_all x1, starting transfers between devices, shards(): sums = lax.all_to_all(spread, 'space', 0, 0, tiled=True)  6.92 us
    all_to_all x1, waiting for transfers between devices, shards(): gathered = lax.all_to_all(density, 'dom', 0, 0, tiled=True)  5.72 us
    pallas_call x1, Pallas kernels, shards(): pl.pallas_call(lambda *refs: start_kernel(slab, grid, scale, *refs), out_...  5.46 us
  transfers between devices with their start and end apart: 8, of which 5 were waited for; matrix products, arithmetic and copies ran while one was open for 0% of the time, Pallas kernels for 7%

profile of v6, /device:TPU:5, one launch (start us, length us, event | category | flops | bytes accessed | tf_op | source)
XLA Modules:
  0.0 109.5 jit_solution(17718532490291767772)
XLA Ops:
  0.6 0.0 copy-start.12
  0.6 0.7 copy-done.12
  1.3 0.0 copy-start
  1.3 0.9 copy-done
  2.3 0.0 copy-start.2
  2.3 11.2 %collective-permute-start.3 = (bf16[1056,128]{1,0:T(8,128)(2,1)S(1)}, bf16[1056,128]{1,0:T(8,128)(2,1)S(1)}, u32[]{:S(2)}, u32[]{:S(2)}) collective-permute-start(bf16[1056,128]{1,0:T(8,128)(2,1)S(1)} %pack.1.refs_2_), channel_id=1, source_target_pairs={{1,0},{2,1},{3,2},{4,3},{5,4},{6,5},{7,6},{8,7},{9,8},{10,9},{11,1... | collective-permute-start | bytes 811016 | tf_op jit(solution)/shard_map/ppermute | solution.py:21
  13.5 1.9 %collective-permute-start.2 = (bf16[1056,128]{1,0:T(8,128)(2,1)S(1)}, bf16[1056,128]{1,0:T(8,128)(2,1)S(1)}, u32[]{:S(2)}, u32[]{:S(2)}) collective-permute-start(bf16[1056,128]{1,0:T(8,128)(2,1)S(1)} %pack.1.refs_2_), channel_id=1, source_target_pairs={{0,1},{1,2},{2,3},{3,4},{4,5},{5,6},{6,7},{7,8},{8,9},{9,10},{10,1... | collective-permute-start | bytes 811016 | tf_op jit(solution)/shard_map/ppermute | solution.py:21
  15.4 0.0 copy-done.2
  15.4 7.0 %collective-permute-start.1 = (bf16[1024,128]{1,0:T(8,128)(2,1)S(1)}, bf16[1024,128]{1,0:T(8,128)(2,1)S(1)}, u32[]{:S(2)}, u32[]{:S(2)}) collective-permute-start(bf16[1024,128]{1,0:T(8,128)(2,1)S(1)} %bitcast.15), channel_id=1, source_target_pairs={{1,0},{2,1},{3,2},{4,3},{5,4},{6,5},{7,6},{8,7},{9,8},{10,9},{11,1... | collective-permute-start | bytes 786440 | tf_op jit(solution)/shard_map/ppermute | solution.py:21
  22.4 1.9 %collective-permute-start = (bf16[1024,128]{1,0:T(8,128)(2,1)S(1)}, bf16[1024,128]{1,0:T(8,128)(2,1)}, u32[]{:S(2)}, u32[]{:S(2)}) collective-permute-start(bf16[1024,128]{1,0:T(8,128)(2,1)S(1)} %bitcast.16), channel_id=1, source_target_pairs={{0,1},{1,2},{2,3},{3,4},{4,5},{5,6},{6,7},{7,8},{8,9},{9,10},{10,1... | collective-permute-start | bytes 786440 | tf_op jit(solution)/shard_map/ppermute | solution.py:21
  24.4 0.1 add_convert_fusion.refs_0_
  24.4 0.0 collective-permute-done.3.refs_3_
  24.4 1.7 %collective-permute-done.2.refs_1_ = bf16[1056,128]{1,0:T(8,128)(2,1)S(1)} collective-permute-done((bf16[1056,128]{1,0:T(8,128)(2,1)S(1)}, bf16[1056,128]{1,0:T(8,128)(2,1)S(1)}, u32[]{:S(2)}, u32[]{:S(2)}) %collective-permute-start.2) | collective-permute-done | bytes 270368 | tf_op jit(solution)/shard_map/ppermute | solution.py:21
  26.1 5.5 %start.1 = (bf16[512,128]{1,0:T(8,128)(2,1)S(1)}, bf16[1024,128]{1,0:T(8,128)(2,1)S(1)}, bf16[1024,128]{1,0:T(8,128)(2,1)S(1)}, f32[12,128,128]{2,1,0:T(8,128)S(1)}, f32[12,128,128]{2,1,0:T(8,128)S(1)}) custom-call(f32[2]{0:T(128)S(1)} %add_convert_fusion.refs_0_, bf16[1056,128]{1,0:T(8,128)(2,1)S(1)} %collective-permute-done.2.refs_1_, ...), custom_call_target="tpu_custom_call" | custom-call | tf_op jit(solution)/shard_map/start/pallas_call | solution.py:386
  31.6 0.0 collective-permute-done.1.refs_3_
  31.6 0.0 copy-start.5
  31.6 0.7 copy-done.5
  32.3 2.1 %collective-permute-done.refs_1_ = bf16[1024,128]{1,0:T(8,128)(2,1)} collective-permute-done((bf16[1024,128]{1,0:T(8,128)(2,1)S(1)}, bf16[1024,128]{1,0:T(8,128)(2,1)}, u32[]{:S(2)}, u32[]{:S(2)}) %collective-permute-start) | collective-permute-done | bytes 262176 | tf_op jit(solution)/shard_map/ppermute | solution.py:21
  34.4 0.0 copy-start.6
  34.4 0.9 copy-done.6
  35.3 3.6 %first.1 = (bf16[768,128]{1,0:T(8,128)(2,1)S(1)}, bf16[1024,128]{1,0:T(8,128)(2,1)S(1)}, f32[1024,128]{1,0:T(8,128)S(1)}) custom-call(f32[2]{0:T(128)S(1)} %add_convert_fusion.refs_0_, bf16[1024,128]{1,0:T(8,128)(2,1)} %collective-permute-done.refs_1_, bf16[1024,128]{1,0:T(8,128)(2,1)S(1)} %bitcast.18, bf16[1024,128]{1,0:T(8,128)(2,1)S(1)} %copy-done.6, ...), custom_call_target="tpu_custom_call" | custom-call | tf_op jit(solution)/shard_map/first/pallas_call | solution.py:404
  38.9 0.0 copy-start.3
  38.9 19.9 %all_to_all.15.parts_ref = bf16[32,24,128]{2,1,0:T(8,128)(2,1)S(1)} all-to-all(bf16[32,24,128]{2,1,0:T(8,128)(2,1)S(1)} %bitcast.20), channel_id=1, replica_groups=mesh['dom'=16,'space'=32] {'space'}, dimensions={0} | all-to-all | bytes 393216 | tf_op jit(solution)/shard_map/all_to_all | solution.py:417
  58.8 0.7 total.1
  59.5 6.9 %all-to-all-start.1 = ((bf16[32,24,128]{2,1,0:T(8,128)(2,1)}), bf16[32,24,128]{2,1,0:T(8,128)(2,1)S(1)}, u32[]{:S(2)}, u32[]{:S(2)}) async-start(bf16[32,24,128]{2,1,0:T(8,128)(2,1)} %total.1), calls=%async_computation.1 | async-start | bytes 393216 | tf_op jit(solution)/shard_map/all_to_all | solution.py:425
  66.4 4.3 %collective-permute-start.5 = (bf16[1024,128]{1,0:T(8,128)(2,1)S(1)}, bf16[1024,128]{1,0:T(8,128)(2,1)S(1)}, u32[]{:S(2)}, u32[]{:S(2)}) collective-permute-start(bf16[1024,128]{1,0:T(8,128)(2,1)S(1)} %get-tuple-element.22.refs_2_), channel_id=1, source_target_pairs={{1,0},{2,1},{3,2},{4,3},{5,4},{6,5},{7,6},{8,7},{9,8},{10,9},{11,1... | collective-permute-start | bytes 786440 | tf_op jit(solution)/shard_map/ppermute | solution.py:21
  70.7 0.0 copy-done.3
  70.7 1.9 %collective-permute-start.4 = (bf16[1024,128]{1,0:T(8,128)(2,1)S(1)}, bf16[1024,128]{1,0:T(8,128)(2,1)S(1)}, u32[]{:S(2)}, u32[]{:S(2)}) collective-permute-start(bf16[1024,128]{1,0:T(8,128)(2,1)S(1)} %get-tuple-element.22.refs_2_), channel_id=1, source_target_pairs={{0,1},{1,2},{2,3},{3,4},{4,5},{5,6},{6,7},{7,8},{8,9},{9,10},{10,1... | collective-permute-start | bytes 786440 | tf_op jit(solution)/shard_map/ppermute | solution.py:21
  72.7 0.0 copy-start.15
  72.7 0.0 copy-start.16
  72.7 0.7 copy-done.15
  73.4 0.0 copy-done.16
  73.4 0.2 dynamic-slice_reduce_fusion
  73.6 6.6 %collective-permute-done.5.refs_3_ = bf16[1024,128]{1,0:T(8,128)(2,1)S(1)} collective-permute-done((bf16[1024,128]{1,0:T(8,128)(2,1)S(1)}, bf16[1024,128]{1,0:T(8,128)(2,1)S(1)}, u32[]{:S(2)}, u32[]{:S(2)}) %collective-permute-start.5) | collective-permute-done | bytes 262176 | tf_op jit(solution)/shard_map/ppermute | solution.py:21
  80.2 0.0 copy-start.7
  80.2 0.7 copy-done.7
  80.9 2.0 %collective-permute-done.4.refs_1_ = bf16[1024,128]{1,0:T(8,128)(2,1)S(1)} collective-permute-done((bf16[1024,128]{1,0:T(8,128)(2,1)S(1)}, bf16[1024,128]{1,0:T(8,128)(2,1)S(1)}, u32[]{:S(2)}, u32[]{:S(2)}) %collective-permute-start.4) | collective-permute-done | bytes 262176 | tf_op jit(solution)/shard_map/ppermute | solution.py:21
  82.9 0.0 copy-start.9
  82.9 0.7 copy-done.9
  83.6 0.0 copy-start.4
  83.6 0.9 copy-done.4
  84.6 0.0 copy-start.8
  84.6 0.9 copy-done.8
  85.5 0.0 copy-start.10
  85.5 0.9 copy-done.10
  86.5 0.0 copy-start.1
  86.5 0.0 copy-start.11
  86.5 2.6 %second.1.refs_4_ = f32[1024,128]{1,0:T(8,128)S(1)} custom-call(f32[2]{0:T(128)S(1)} %add_convert_fusion.refs_0_, bf16[1024,128]{1,0:T(8,128)(2,1)S(1)} %copy-done.10, bf16[1024,128]{1,0:T(8,128)(2,1)S(1)} %copy-done.4, bf16[1024,128]{1,0:T(8,128)(2,1)S(1)} %copy-done.8, f32[1024,128]{1,0:T(8,128)S(1)} %get-tuple-element.23.refs_4_, ...), custom_call_target="tpu_custom_call" | custom-call | tf_op jit(solution)/shard_map/second/pallas_call | solution.py:427
  89.1 0.0 all-to-all-done.1
  89.1 0.0 copy-start.14
  89.1 0.0 copy-done.1
  89.1 0.0 copy-done.11
  89.1 0.6 copy-done.14
  89.8 2.5 %back.1 = (f32[256,128]{1,0:T(8,128)}, f32[1024,128]{1,0:T(8,128)S(1)}, f32[16,4,128]{2,1,0:T(4,128)}) custom-call(bf16[768,128]{1,0:T(8,128)(2,1)S(1)} %bitcast.19, f32[128,128]{1,0:T(8,128)S(1)} %copy-done.11, bf16[1024,128]{1,0:T(8,128)(2,1)S(1)} %get-tuple-element.21.refs_2_, bf16[1024,128]{1,0:T(8,128)(2,1)S(1)} %bitcast.14, ...), custom_call_target="tpu_custom_call" | custom-call | tf_op jit(solution)/shard_map/back/pallas_call | solution.py:437
  92.3 9.8 %all-to-all-start.2 = ((f32[16,4,128]{2,1,0:T(4,128)}), f32[16,4,128]{2,1,0:T(4,128)S(1)}, u32[]{:S(2)}, u32[]{:S(2)}) async-start(f32[16,4,128]{2,1,0:T(4,128)} %get-tuple-element.24), calls=%async_computation.2 | async-start | bytes 65536 | tf_op jit(solution)/shard_map/all_to_all | solution.py:447
  102.1 0.1 pad_add_fusion.refs_0_
  102.1 0.0 copy-start.13
  102.1 5.7 %all-to-all-done.2.refs_1_ = f32[16,4,128]{2,1,0:T(4,128)S(1)} async-done(((f32[16,4,128]{2,1,0:T(4,128)}), f32[16,4,128]{2,1,0:T(4,128)S(1)}, u32[]{:S(2)}, u32[]{:S(2)}) %all-to-all-start.2) | async-done | bytes 32800 | tf_op jit(solution)/shard_map/all_to_all | solution.py:447
  107.9 0.0 copy-done.13
  107.9 1.6 %tail.1 = (f32[4,128]{1,0:T(4,128)}, bf16[1024,128]{1,0:T(8,128)(2,1)}) custom-call(s32[5]{0:T(128)S(1)} %pad_add_fusion.refs_0_, f32[16,4,128]{2,1,0:T(4,128)S(1)} %all-to-all-done.2.refs_1_, f32[4,128]{1,0:T(4,128)S(1)} %bitcast.23, f32[1024,128]{1,0:T(8,128)S(1)} %get-tuple-element.25.refs_3_), custom_call_target="tpu_custom_call" | custom-call | tf_op jit(solution)/shard_map/tail/pallas_call | solution.py:452
  (1 shorter events, 0.0 us)
Async XLA Ops:
  0.6 0.7 copy-start.12
  1.3 0.9 copy-start
  2.3 13.2 %copy-start.2 = (bf16[1,2,4,16,8,128]{5,4,3,2,1,0:T(8,128)(2,1)S(1)}, bf16[1,2,4,16,8,128]{5,4,3,2,1,0:T(8,128)(2,1)}, u32[]{:S(2)}) copy-start(bf16[1,2,4,16,8,128]{5,4,3,2,1,0:T(8,128)(2,1)} %param.8) | copy-start | bytes 786436
  2.3 22.1 %collective-permute-start.3 = (bf16[1056,128]{1,0:T(8,128)(2,1)S(1)}, bf16[1056,128]{1,0:T(8,128)(2,1)S(1)}, u32[]{:S(2)}, u32[]{:S(2)}) collective-permute-start(bf16[1056,128]{1,0:T(8,128)(2,1)S(1)} %pack.1.refs_2_), channel_id=1, source_target_pairs={{1,0},{2,1},{3,2},{4,3},{5,4},{6,5},{7,6},{8,7},{9,8},{10,9},{11,1... | collective-permute-start | bytes 811016 | tf_op jit(solution)/shard_map/ppermute | solution.py:21
  13.5 12.6 %collective-permute-start.2 = (bf16[1056,128]{1,0:T(8,128)(2,1)S(1)}, bf16[1056,128]{1,0:T(8,128)(2,1)S(1)}, u32[]{:S(2)}, u32[]{:S(2)}) collective-permute-start(bf16[1056,128]{1,0:T(8,128)(2,1)S(1)} %pack.1.refs_2_), channel_id=1, source_target_pairs={{0,1},{1,2},{2,3},{3,4},{4,5},{5,6},{6,7},{7,8},{8,9},{9,10},{10,1... | collective-permute-start | bytes 811016 | tf_op jit(solution)/shard_map/ppermute | solution.py:21
  15.4 16.1 %collective-permute-start.1 = (bf16[1024,128]{1,0:T(8,128)(2,1)S(1)}, bf16[1024,128]{1,0:T(8,128)(2,1)S(1)}, u32[]{:S(2)}, u32[]{:S(2)}) collective-permute-start(bf16[1024,128]{1,0:T(8,128)(2,1)S(1)} %bitcast.15), channel_id=1, source_target_pairs={{1,0},{2,1},{3,2},{4,3},{5,4},{6,5},{7,6},{8,7},{9,8},{10,9},{11,1... | collective-permute-start | bytes 786440 | tf_op jit(solution)/shard_map/ppermute | solution.py:21
  22.4 12.0 %collective-permute-start = (bf16[1024,128]{1,0:T(8,128)(2,1)S(1)}, bf16[1024,128]{1,0:T(8,128)(2,1)}, u32[]{:S(2)}, u32[]{:S(2)}) collective-permute-start(bf16[1024,128]{1,0:T(8,128)(2,1)S(1)} %bitcast.16), channel_id=1, source_target_pairs={{0,1},{1,2},{2,3},{3,4},{4,5},{5,6},{6,7},{7,8},{8,9},{9,10},{10,1... | collective-permute-start | bytes 786440 | tf_op jit(solution)/shard_map/ppermute | solution.py:21
  31.6 0.7 copy-start.5
  34.4 1.0 copy-start.6
  38.9 31.8 %copy-start.3 = (bf16[1024,128]{1,0:T(8,128)(2,1)}, bf16[1024,128]{1,0:T(8,128)(2,1)S(1)}, u32[]{:S(2)}) copy-start(bf16[1024,128]{1,0:T(8,128)(2,1)S(1)} %get-tuple-element.22.refs_2_) | copy-start | bytes 786436
  59.5 29.6 %all-to-all-start.1 = ((bf16[32,24,128]{2,1,0:T(8,128)(2,1)}), bf16[32,24,128]{2,1,0:T(8,128)(2,1)S(1)}, u32[]{:S(2)}, u32[]{:S(2)}) async-start(bf16[32,24,128]{2,1,0:T(8,128)(2,1)} %total.1), calls=%async_computation.1 | async-start | bytes 393216 | tf_op jit(solution)/shard_map/all_to_all | solution.py:425
  66.4 13.8 %collective-permute-start.5 = (bf16[1024,128]{1,0:T(8,128)(2,1)S(1)}, bf16[1024,128]{1,0:T(8,128)(2,1)S(1)}, u32[]{:S(2)}, u32[]{:S(2)}) collective-permute-start(bf16[1024,128]{1,0:T(8,128)(2,1)S(1)} %get-tuple-element.22.refs_2_), channel_id=1, source_target_pairs={{1,0},{2,1},{3,2},{4,3},{5,4},{6,5},{7,6},{8,7},{9,8},{10,9},{11,1... | collective-permute-start | bytes 786440 | tf_op jit(solution)/shard_map/ppermute | solution.py:21
  70.7 12.2 %collective-permute-start.4 = (bf16[1024,128]{1,0:T(8,128)(2,1)S(1)}, bf16[1024,128]{1,0:T(8,128)(2,1)S(1)}, u32[]{:S(2)}, u32[]{:S(2)}) collective-permute-start(bf16[1024,128]{1,0:T(8,128)(2,1)S(1)} %get-tuple-element.22.refs_2_), channel_id=1, source_target_pairs={{0,1},{1,2},{2,3},{3,4},{4,5},{5,6},{6,7},{7,8},{8,9},{9,10},{10,1... | collective-permute-start | bytes 786440 | tf_op jit(solution)/shard_map/ppermute | solution.py:21
  72.7 0.7 copy-start.15
  72.7 0.7 copy-start.16
  80.2 0.7 copy-start.7
  82.9 0.7 copy-start.9
  83.6 0.9 copy-start.4
  84.6 0.9 copy-start.8
  85.5 0.9 copy-start.10
  86.5 2.7 %copy-start.1 = (bf16[1,2,4,16,8,128]{5,4,3,2,1,0:T(8,128)(2,1)S(1)}, bf16[1,2,4,16,8,128]{5,4,3,2,1,0:T(8,128)(2,1)}, u32[]{:S(2)}) copy-start(bf16[1,2,4,16,8,128]{5,4,3,2,1,0:T(8,128)(2,1)} %param.9) | copy-start | bytes 786436
  86.5 2.7 %copy-start.11 = (f32[128,128]{1,0:T(8,128)S(1)}, f32[128,128]{1,0:T(8,128)}, u32[]{:S(2)}) copy-start(f32[128,128]{1,0:T(8,128)} %refs_1_.1) | copy-start | bytes 196612
  89.1 0.7 copy-start.14
  92.3 15.6 %all-to-all-start.2 = ((f32[16,4,128]{2,1,0:T(4,128)}), f32[16,4,128]{2,1,0:T(4,128)S(1)}, u32[]{:S(2)}, u32[]{:S(2)}) async-start(f32[16,4,128]{2,1,0:T(4,128)} %get-tuple-element.24), calls=%async_computation.2 | async-start | bytes 65536 | tf_op jit(solution)/shard_map/all_to_all | solution.py:447
  102.1 5.7 %copy-start.13 = (f32[1,4,128]{2,1,0:T(4,128)S(1)}, f32[1,4,128]{2,1,0:T(4,128)}, u32[]{:S(2)}) copy-start(f32[1,4,128]{2,1,0:T(4,128)} %param.11) | copy-start | bytes 6148

commit v7 on v6

--- a/solution.py
+++ b/solution.py
@@ -121,14 +121,14 @@
                 kept_imag = part_ref[1, plane]
                 moved_ref[low] = (kept_real - imag).astype(jnp.bfloat16)
                 moved_ref[high] = (kept_imag + real).astype(jnp.bfloat16)
-                adjoint_ref[low] = (kept_real + imag).astype(jnp.bfloat16)
-                adjoint_ref[high] = (real - kept_imag).astype(jnp.bfloat16)
+                adjoint_ref[:, low] = (kept_real + imag).T.astype(jnp.bfloat16)
+                adjoint_ref[:, high] = (real - kept_imag).T.astype(jnp.bfloat16)
     for place, ref in ((0, field_ref), (2, own_ref)):
         right[:half, place * lanes : (place + 1) * lanes] = ref[:half]
         right[half:, place * lanes : (place + 1) * lanes] = ref[half : 2 * half]
         right[:half, (place + 1) * lanes : (place + 2) * lanes] = ref[half : 2 * half]
         right[half:, (place + 1) * lanes : (place + 2) * lanes] = -ref[:half]
-    over = contract(adjoint_ref[...], right[...]) * scale
+    over = half_dot(adjoint_ref[...], right[...]) * scale
     for index in range(4):
         piece = slice(index * lanes, (index + 1) * lanes)
         partial_ref[piece] = over[:, piece].astype(jnp.bfloat16)
@@ -184,14 +184,15 @@
         right[low, lanes:] = first_imag
         right[high, :lanes] = first_imag
         right[high, lanes:] = -first_real
-    cross = contract(adjoint[...], right[...]) * scale
+    cross = half_dot(adjoint[...], right[...]) * scale
     partial_ref[: 2 * lanes] = over[: 2 * lanes]
     partial_ref[2 * lanes : 3 * lanes] = cross[:, :lanes].astype(jnp.bfloat16)
     partial_ref[3 * lanes : 4 * lanes] = cross[:, lanes:].astype(jnp.bfloat16)
     partial_ref[4 * lanes :] = over[2 * lanes :]
 
 
-def second_kernel(slab, grid, edge, low, own, high, turned, cos_ref, sin_ref, second_ref,
+def second_kernel(slab, grid, edge, low, own, high, turned, cos_ref, sin_ref, coupling,
+                  occupation, second_ref, coupling_ref, weight_ref,
                   even, odd, running):
     cells = grid[0] * grid[1]
     half = slab * cells
@@ -209,6 +210,8 @@
                 return carry
 
             lax.fori_loop(0, slab, begin, 0)
+    coupling_ref[...] = coupling[...]
+    weight_ref[...] = jnp.broadcast_to(occupation[...], weight_ref.shape)
     kinetic(edge, running, even, odd, slab, grid, False)
     for plane in range(slab):
         real, imag = turned_back(running, plane, cos_ref, sin_ref, slab)
@@ -237,10 +240,8 @@
         return sums[index * lanes : (index + 1) * lanes]
 
     def mixed(real, imag):
-        return (
-            high_dot(strength, real).astype(jnp.bfloat16),
-            high_dot(strength, imag).astype(jnp.bfloat16),
-        )
+        both = high_dot(strength, jnp.concatenate([real, imag], axis=1)).astype(jnp.bfloat16)
+        return both[:, :lanes], both[:, lanes:]
 
     mix1_real, mix1_imag = mixed(
         matrix(0).astype(jnp.float32), matrix(1).astype(jnp.float32)
@@ -259,7 +260,7 @@
     mix1_turned = jnp.concatenate([-mix1_imag, mix1_real], axis=1)
     mix2_real_imag = jnp.concatenate([mix2_real, mix2_imag], axis=1)
     mix2_turned = jnp.concatenate([-mix2_imag, mix2_real], axis=1)
-    weight = jnp.broadcast_to(occupation[...], (8, lanes))
+    weight = occupation[...]
     for plane in range(slab):
         low = plane * cells
         real_rows = slice(low, low + cells)
@@ -320,12 +321,6 @@
         ).astype(jnp.bfloat16)
 
 
-def contract(left, right):
-    return lax.dot_general(
-        left, right, (((0,), (0,)), ((), ())), preferred_element_type=jnp.float32
-    )
-
-
 def high_dot(left, right):
     return jnp.dot(
         left, right, precision=lax.Precision.HIGHEST, preferred_element_type=jnp.float32
@@ -388,7 +383,7 @@
         out_shape=(
             shape((4 * orbits, orbits), bf16),
             shape((rows, orbits), bf16),
-            shape((rows, orbits), bf16),
+            shape((orbits, rows), bf16),
             turn,
             turn,
         ),
@@ -424,14 +419,18 @@
     )(parts)
     sums = lax.all_to_all(spread, "space", 0, 0, tiled=True)
     sums = sums.reshape(6 * orbits, orbits)
-    second = pl.pallas_call(
+    second, strength, weight = pl.pallas_call(
         lambda *refs: second_kernel(slab, grid, *refs),
-        out_shape=shape((rows, orbits), f32),
-        in_specs=scalars(6),
+        out_shape=(
+            shape((rows, orbits), f32),
+            shape((orbits, orbits), f32),
+            shape((8, orbits), f32),
+        ),
+        in_specs=scalars(8),
         scratch_shapes=stencil,
         compiler_params=limit(12),
         name="second",
-    )(edge, low_s, sent, high_s, turned, cosv, sinv)
+    )(edge, low_s, sent, high_s, turned, cosv, sinv, coupling, occupation.reshape(1, orbits))
 
     domain_count = neighbours.shape[0]
     intersection, field, density = pl.pallas_call(
@@ -443,7 +442,7 @@
         ),
         compiler_params=limit(14),
         name="back",
-    )(sums, coupling, moved, start, second, occupation.reshape(1, orbits))
+    )(sums, strength, moved, start, second, weight)
     gathered = lax.all_to_all(density, "dom", 0, 0, tiled=True)
     own_index = lax.axis_index("dom")
     mine = lax.dynamic_index_in_dim(neighbours, own_index, 0, keepdims=False)

time: 110 us -> 110 us (level)
  no operation moved by 1% of the time
where the time goes in v7:
time: 110 us
  starting transfers between devices  45.1 us (41%)
  blocking collectives  19.9 us (18%)
  waiting for transfers between devices  18.2 us (17%)
  Pallas kernels  16.4 us (15%)
  local copies, waits for them, and re-layouts  9.09 us (8%)
    ppermute x6, starting transfers between devices, neighbour_pair(): return (lax.ppermute(value, axis, up), lax.ppermute(value, axis, down))  28.2 us
    all_to_all x1, blocking collectives, shards(): lax.all_to_all(partial.reshape(devices, share, orbits), 'space', 0, 0, ti...  19.9 us
    ppermute x6, waiting for transfers between devices, neighbour_pair(): return (lax.ppermute(value, axis, up), lax.ppermute(value, axis, down))  12.5 us
    all_to_all x1, starting transfers between devices, shards(): gathered = lax.all_to_all(density, 'dom', 0, 0, tiled=True)  9.77 us
    unnamed x34, local copies, waits for them, and re-layouts  8.88 us
    all_to_all x1, starting transfers between devices, shards(): sums = lax.all_to_all(spread, 'space', 0, 0, tiled=True)  7.05 us
    all_to_all x1, waiting for transfers between devices, shards(): gathered = lax.all_to_all(density, 'dom', 0, 0, tiled=True)  5.72 us
    pallas_call x1, Pallas kernels, shards(): pl.pallas_call(lambda *refs: start_kernel(slab, grid, scale, *refs), out_...  5.4 us
  transfers between devices with their start and end apart: 8, of which 5 were waited for; matrix products, arithmetic and copies ran while one was open for 0% of the time, Pallas kernels for 7%

profile of v7, /device:TPU:5, one launch (start us, length us, event | category | flops | bytes accessed | tf_op | source)
XLA Modules:
  0.0 109.5 jit_solution(1299237065263027104)
XLA Ops:
  0.6 0.0 copy-start.12
  0.6 0.7 copy-done.12
  1.3 0.0 copy-start
  1.3 0.9 copy-done
  2.3 0.0 copy-start.2
  2.3 11.2 %collective-permute-start.3 = (bf16[1056,128]{1,0:T(8,128)(2,1)S(1)}, bf16[1056,128]{1,0:T(8,128)(2,1)S(1)}, u32[]{:S(2)}, u32[]{:S(2)}) collective-permute-start(bf16[1056,128]{1,0:T(8,128)(2,1)S(1)} %pack.1.refs_2_), channel_id=1, source_target_pairs={{1,0},{2,1},{3,2},{4,3},{5,4},{6,5},{7,6},{8,7},{9,8},{10,9},{11,1... | collective-permute-start | bytes 811016 | tf_op jit(solution)/shard_map/ppermute | solution.py:21
  13.5 1.9 %collective-permute-start.2 = (bf16[1056,128]{1,0:T(8,128)(2,1)S(1)}, bf16[1056,128]{1,0:T(8,128)(2,1)S(1)}, u32[]{:S(2)}, u32[]{:S(2)}) collective-permute-start(bf16[1056,128]{1,0:T(8,128)(2,1)S(1)} %pack.1.refs_2_), channel_id=1, source_target_pairs={{0,1},{1,2},{2,3},{3,4},{4,5},{5,6},{6,7},{7,8},{8,9},{9,10},{10,1... | collective-permute-start | bytes 811016 | tf_op jit(solution)/shard_map/ppermute | solution.py:21
  15.4 0.0 copy-done.2
  15.4 7.0 %collective-permute-start.1 = (bf16[1024,128]{1,0:T(8,128)(2,1)S(1)}, bf16[1024,128]{1,0:T(8,128)(2,1)S(1)}, u32[]{:S(2)}, u32[]{:S(2)}) collective-permute-start(bf16[1024,128]{1,0:T(8,128)(2,1)S(1)} %bitcast.15), channel_id=1, source_target_pairs={{1,0},{2,1},{3,2},{4,3},{5,4},{6,5},{7,6},{8,7},{9,8},{10,9},{11,1... | collective-permute-start | bytes 786440 | tf_op jit(solution)/shard_map/ppermute | solution.py:21
  22.4 1.9 %collective-permute-start = (bf16[1024,128]{1,0:T(8,128)(2,1)S(1)}, bf16[1024,128]{1,0:T(8,128)(2,1)}, u32[]{:S(2)}, u32[]{:S(2)}) collective-permute-start(bf16[1024,128]{1,0:T(8,128)(2,1)S(1)} %bitcast.16), channel_id=1, source_target_pairs={{0,1},{1,2},{2,3},{3,4},{4,5},{5,6},{6,7},{7,8},{8,9},{9,10},{10,1... | collective-permute-start | bytes 786440 | tf_op jit(solution)/shard_map/ppermute | solution.py:21
  24.4 0.1 add_convert_fusion.refs_0_
  24.4 0.0 collective-permute-done.3.refs_3_
  24.4 1.7 %collective-permute-done.2.refs_1_ = bf16[1056,128]{1,0:T(8,128)(2,1)S(1)} collective-permute-done((bf16[1056,128]{1,0:T(8,128)(2,1)S(1)}, bf16[1056,128]{1,0:T(8,128)(2,1)S(1)}, u32[]{:S(2)}, u32[]{:S(2)}) %collective-permute-start.2) | collective-permute-done | bytes 270368 | tf_op jit(solution)/shard_map/ppermute | solution.py:21
  26.1 5.4 %start.1 = (bf16[512,128]{1,0:T(8,128)(2,1)S(1)}, bf16[1024,128]{1,0:T(8,128)(2,1)S(1)}, bf16[128,1024]{1,0:T(8,128)(2,1)S(1)}, f32[12,128,128]{2,1,0:T(8,128)S(1)}, f32[12,128,128]{2,1,0:T(8,128)S(1)}) custom-call(f32[2]{0:T(128)S(1)} %add_convert_fusion.refs_0_, bf16[1056,128]{1,0:T(8,128)(2,1)S(1)} %collective-permute-done.2.refs_1_, ...), custom_call_target="tpu_custom_call" | custom-call | tf_op jit(solution)/shard_map/start/pallas_call | solution.py:381
  31.5 0.0 collective-permute-done.1.refs_3_
  31.5 0.0 copy-start.3
  31.5 0.7 copy-done.3
  32.2 2.2 %collective-permute-done.refs_1_ = bf16[1024,128]{1,0:T(8,128)(2,1)} collective-permute-done((bf16[1024,128]{1,0:T(8,128)(2,1)S(1)}, bf16[1024,128]{1,0:T(8,128)(2,1)}, u32[]{:S(2)}, u32[]{:S(2)}) %collective-permute-start) | collective-permute-done | bytes 262176 | tf_op jit(solution)/shard_map/ppermute | solution.py:21
  34.4 0.0 copy-start.4
  34.4 0.9 copy-done.4
  35.3 3.5 %first.1 = (bf16[768,128]{1,0:T(8,128)(2,1)S(1)}, bf16[1024,128]{1,0:T(8,128)(2,1)S(1)}, f32[1024,128]{1,0:T(8,128)S(1)}) custom-call(f32[2]{0:T(128)S(1)} %add_convert_fusion.refs_0_, bf16[1024,128]{1,0:T(8,128)(2,1)} %collective-permute-done.refs_1_, bf16[1024,128]{1,0:T(8,128)(2,1)S(1)} %bitcast.18, bf16[1024,128]{1,0:T(8,128)(2,1)S(1)} %copy-done.4, ...), custom_call_target="tpu_custom_call" | custom-call | tf_op jit(solution)/shard_map/first/pallas_call | solution.py:399
  38.9 0.0 copy-start.5
  38.9 19.9 %all_to_all.15.parts_ref = bf16[32,24,128]{2,1,0:T(8,128)(2,1)S(1)} all-to-all(bf16[32,24,128]{2,1,0:T(8,128)(2,1)S(1)} %bitcast.20), channel_id=1, replica_groups=mesh['dom'=16,'space'=32] {'space'}, dimensions={0} | all-to-all | bytes 393216 | tf_op jit(solution)/shard_map/all_to_all | solution.py:412
  58.7 0.7 total.1
  59.5 0.0 copy-start.11
  59.5 7.1 %all-to-all-start.1 = ((bf16[32,24,128]{2,1,0:T(8,128)(2,1)}), bf16[32,24,128]{2,1,0:T(8,128)(2,1)S(1)}, u32[]{:S(2)}, u32[]{:S(2)}) async-start(bf16[32,24,128]{2,1,0:T(8,128)(2,1)} %total.1), calls=%async_computation.1 | async-start | bytes 393216 | tf_op jit(solution)/shard_map/all_to_all | solution.py:420
  66.5 4.3 %collective-permute-start.5 = (bf16[1024,128]{1,0:T(8,128)(2,1)S(1)}, bf16[1024,128]{1,0:T(8,128)(2,1)S(1)}, u32[]{:S(2)}, u32[]{:S(2)}) collective-permute-start(bf16[1024,128]{1,0:T(8,128)(2,1)S(1)} %get-tuple-element.24.refs_2_), channel_id=1, source_target_pairs={{1,0},{2,1},{3,2},{4,3},{5,4},{6,5},{7,6},{8,7},{9,8},{10,9},{11,1... | collective-permute-start | bytes 786440 | tf_op jit(solution)/shard_map/ppermute | solution.py:21
  70.8 0.0 copy-done.5
  70.9 1.9 %collective-permute-start.4 = (bf16[1024,128]{1,0:T(8,128)(2,1)S(1)}, bf16[1024,128]{1,0:T(8,128)(2,1)S(1)}, u32[]{:S(2)}, u32[]{:S(2)}) collective-permute-start(bf16[1024,128]{1,0:T(8,128)(2,1)S(1)} %get-tuple-element.24.refs_2_), channel_id=1, source_target_pairs={{0,1},{1,2},{2,3},{3,4},{4,5},{5,6},{6,7},{7,8},{8,9},{9,10},{10,1... | collective-permute-start | bytes 786440 | tf_op jit(solution)/shard_map/ppermute | solution.py:21
  72.8 0.0 copy-start.15
  72.8 0.0 copy-start.16
  72.8 0.7 copy-done.15
  73.5 0.0 copy-done.16
  73.5 0.2 dynamic-slice_reduce_fusion
  73.7 6.6 %collective-permute-done.5.refs_3_ = bf16[1024,128]{1,0:T(8,128)(2,1)S(1)} collective-permute-done((bf16[1024,128]{1,0:T(8,128)(2,1)S(1)}, bf16[1024,128]{1,0:T(8,128)(2,1)S(1)}, u32[]{:S(2)}, u32[]{:S(2)}) %collective-permute-start.5) | collective-permute-done | bytes 262176 | tf_op jit(solution)/shard_map/ppermute | solution.py:21
  80.3 0.0 copy-start.7
  80.3 0.7 copy-done.7
  81.0 2.0 %collective-permute-done.4.refs_1_ = bf16[1024,128]{1,0:T(8,128)(2,1)S(1)} collective-permute-done((bf16[1024,128]{1,0:T(8,128)(2,1)S(1)}, bf16[1024,128]{1,0:T(8,128)(2,1)S(1)}, u32[]{:S(2)}, u32[]{:S(2)}) %collective-permute-start.4) | collective-permute-done | bytes 262176 | tf_op jit(solution)/shard_map/ppermute | solution.py:21
  83.0 0.0 copy-start.9
  83.0 0.7 copy-done.9
  83.7 0.0 copy-start.14
  83.7 0.0 copy-done.11
  83.7 0.7 copy-done.14
  84.4 0.0 copy-start.6
  84.4 0.9 copy-done.6
  85.3 0.0 copy-start.8
  85.3 0.9 copy-done.8
  86.3 0.0 copy-start.10
  86.3 0.9 copy-done.10
  87.2 0.0 copy-start.1
  87.2 2.6 %second.1 = (f32[1024,128]{1,0:T(8,128)S(1)}, f32[128,128]{1,0:T(8,128)S(1)}, f32[8,128]{1,0:T(8,128)S(1)}) custom-call(f32[2]{0:T(128)S(1)} %add_convert_fusion.refs_0_, bf16[1024,128]{1,0:T(8,128)(2,1)S(1)} %copy-done.10, bf16[1024,128]{1,0:T(8,128)(2,1)S(1)} %copy-done.6, bf16[1024,128]{1,0:T(8,128)(2,1)S(1)} %copy-done.8, ...), custom_call_target="tpu_custom_call" | custom-call | tf_op jit(solution)/shard_map/second/pallas_call | solution.py:422
  89.9 0.0 all-to-all-done.1
  89.9 0.0 copy-done.1
  89.9 2.5 %back.1 = (f32[256,128]{1,0:T(8,128)}, f32[1024,128]{1,0:T(8,128)S(1)}, f32[16,4,128]{2,1,0:T(4,128)}) custom-call(bf16[768,128]{1,0:T(8,128)(2,1)S(1)} %bitcast.19, f32[128,128]{1,0:T(8,128)S(1)} %get-tuple-element.26.refs_1_, bf16[1024,128]{1,0:T(8,128)(2,1)S(1)} %get-tuple-element.27.refs_2_, bf16[1024,128]{1,0:T(8,128)(2,1)S(1)} %bitcast.14, ...), custom_call_target="tpu_custom_call" | custom-call | tf_op jit(solution)/shard_map/back/pallas_call | solution.py:436
  92.3 9.8 %all-to-all-start.2 = ((f32[16,4,128]{2,1,0:T(4,128)}), f32[16,4,128]{2,1,0:T(4,128)S(1)}, u32[]{:S(2)}, u32[]{:S(2)}) async-start(f32[16,4,128]{2,1,0:T(4,128)} %get-tuple-element.30), calls=%async_computation.2 | async-start | bytes 65536 | tf_op jit(solution)/shard_map/all_to_all | solution.py:446
  102.1 0.1 pad_add_fusion.refs_0_
  102.2 0.0 copy-start.13
  102.2 5.7 %all-to-all-done.2.refs_1_ = f32[16,4,128]{2,1,0:T(4,128)S(1)} async-done(((f32[16,4,128]{2,1,0:T(4,128)}), f32[16,4,128]{2,1,0:T(4,128)S(1)}, u32[]{:S(2)}, u32[]{:S(2)}) %all-to-all-start.2) | async-done | bytes 32800 | tf_op jit(solution)/shard_map/all_to_all | solution.py:446
  107.9 0.0 copy-done.13
  107.9 1.6 %tail.1 = (f32[4,128]{1,0:T(4,128)}, bf16[1024,128]{1,0:T(8,128)(2,1)}) custom-call(s32[5]{0:T(128)S(1)} %pad_add_fusion.refs_0_, f32[16,4,128]{2,1,0:T(4,128)S(1)} %all-to-all-done.2.refs_1_, f32[4,128]{1,0:T(4,128)S(1)} %bitcast.23, f32[1024,128]{1,0:T(8,128)S(1)} %get-tuple-element.31.refs_3_), custom_call_target="tpu_custom_call" | custom-call | tf_op jit(solution)/shard_map/tail/pallas_call | solution.py:451
  (1 shorter events, 0.0 us)
Async XLA Ops:
  0.6 0.7 copy-start.12
  1.3 0.9 copy-start
  2.3 13.2 %copy-start.2 = (bf16[1,2,4,16,8,128]{5,4,3,2,1,0:T(8,128)(2,1)S(1)}, bf16[1,2,4,16,8,128]{5,4,3,2,1,0:T(8,128)(2,1)}, u32[]{:S(2)}) copy-start(bf16[1,2,4,16,8,128]{5,4,3,2,1,0:T(8,128)(2,1)} %param.8) | copy-start | bytes 786436
  2.3 22.1 %collective-permute-start.3 = (bf16[1056,128]{1,0:T(8,128)(2,1)S(1)}, bf16[1056,128]{1,0:T(8,128)(2,1)S(1)}, u32[]{:S(2)}, u32[]{:S(2)}) collective-permute-start(bf16[1056,128]{1,0:T(8,128)(2,1)S(1)} %pack.1.refs_2_), channel_id=1, source_target_pairs={{1,0},{2,1},{3,2},{4,3},{5,4},{6,5},{7,6},{8,7},{9,8},{10,9},{11,1... | collective-permute-start | bytes 811016 | tf_op jit(solution)/shard_map/ppermute | solution.py:21
  13.5 12.6 %collective-permute-start.2 = (bf16[1056,128]{1,0:T(8,128)(2,1)S(1)}, bf16[1056,128]{1,0:T(8,128)(2,1)S(1)}, u32[]{:S(2)}, u32[]{:S(2)}) collective-permute-start(bf16[1056,128]{1,0:T(8,128)(2,1)S(1)} %pack.1.refs_2_), channel_id=1, source_target_pairs={{0,1},{1,2},{2,3},{3,4},{4,5},{5,6},{6,7},{7,8},{8,9},{9,10},{10,1... | collective-permute-start | bytes 811016 | tf_op jit(solution)/shard_map/ppermute | solution.py:21
  15.4 16.1 %collective-permute-start.1 = (bf16[1024,128]{1,0:T(8,128)(2,1)S(1)}, bf16[1024,128]{1,0:T(8,128)(2,1)S(1)}, u32[]{:S(2)}, u32[]{:S(2)}) collective-permute-start(bf16[1024,128]{1,0:T(8,128)(2,1)S(1)} %bitcast.15), channel_id=1, source_target_pairs={{1,0},{2,1},{3,2},{4,3},{5,4},{6,5},{7,6},{8,7},{9,8},{10,9},{11,1... | collective-permute-start | bytes 786440 | tf_op jit(solution)/shard_map/ppermute | solution.py:21
  22.4 12.0 %collective-permute-start = (bf16[1024,128]{1,0:T(8,128)(2,1)S(1)}, bf16[1024,128]{1,0:T(8,128)(2,1)}, u32[]{:S(2)}, u32[]{:S(2)}) collective-permute-start(bf16[1024,128]{1,0:T(8,128)(2,1)S(1)} %bitcast.16), channel_id=1, source_target_pairs={{0,1},{1,2},{2,3},{3,4},{4,5},{5,6},{6,7},{7,8},{8,9},{9,10},{10,1... | collective-permute-start | bytes 786440 | tf_op jit(solution)/shard_map/ppermute | solution.py:21
  31.5 0.7 copy-start.3
  34.4 1.0 copy-start.4
  38.9 32.0 %copy-start.5 = (bf16[1024,128]{1,0:T(8,128)(2,1)}, bf16[1024,128]{1,0:T(8,128)(2,1)S(1)}, u32[]{:S(2)}) copy-start(bf16[1024,128]{1,0:T(8,128)(2,1)S(1)} %get-tuple-element.24.refs_2_) | copy-start | bytes 786436
  59.5 24.3 %copy-start.11 = (f32[128,128]{1,0:T(8,128)S(1)}, f32[128,128]{1,0:T(8,128)}, u32[]{:S(2)}) copy-start(f32[128,128]{1,0:T(8,128)} %refs_7_.1) | copy-start | bytes 196612
  59.5 30.4 %all-to-all-start.1 = ((bf16[32,24,128]{2,1,0:T(8,128)(2,1)}), bf16[32,24,128]{2,1,0:T(8,128)(2,1)S(1)}, u32[]{:S(2)}, u32[]{:S(2)}) async-start(bf16[32,24,128]{2,1,0:T(8,128)(2,1)} %total.1), calls=%async_computation.1 | async-start | bytes 393216 | tf_op jit(solution)/shard_map/all_to_all | solution.py:420
  66.5 13.8 %collective-permute-start.5 = (bf16[1024,128]{1,0:T(8,128)(2,1)S(1)}, bf16[1024,128]{1,0:T(8,128)(2,1)S(1)}, u32[]{:S(2)}, u32[]{:S(2)}) collective-permute-start(bf16[1024,128]{1,0:T(8,128)(2,1)S(1)} %get-tuple-element.24.refs_2_), channel_id=1, source_target_pairs={{1,0},{2,1},{3,2},{4,3},{5,4},{6,5},{7,6},{8,7},{9,8},{10,9},{11,1... | collective-permute-start | bytes 786440 | tf_op jit(solution)/shard_map/ppermute | solution.py:21
  70.9 12.2 %collective-permute-start.4 = (bf16[1024,128]{1,0:T(8,128)(2,1)S(1)}, bf16[1024,128]{1,0:T(8,128)(2,1)S(1)}, u32[]{:S(2)}, u32[]{:S(2)}) collective-permute-start(bf16[1024,128]{1,0:T(8,128)(2,1)S(1)} %get-tuple-element.24.refs_2_), channel_id=1, source_target_pairs={{0,1},{1,2},{2,3},{3,4},{4,5},{5,6},{6,7},{7,8},{8,9},{9,10},{10,1... | collective-permute-start | bytes 786440 | tf_op jit(solution)/shard_map/ppermute | solution.py:21
  72.8 0.7 copy-start.15
  72.8 0.7 copy-start.16
  80.3 0.7 copy-start.7
  83.0 0.7 copy-start.9
  83.7 0.7 copy-start.14
  84.4 0.9 copy-start.6
  85.3 0.9 copy-start.8
  86.3 0.9 copy-start.10
  87.2 2.6 %copy-start.1 = (bf16[1,2,4,16,8,128]{5,4,3,2,1,0:T(8,128)(2,1)S(1)}, bf16[1,2,4,16,8,128]{5,4,3,2,1,0:T(8,128)(2,1)}, u32[]{:S(2)}) copy-start(bf16[1,2,4,16,8,128]{5,4,3,2,1,0:T(8,128)(2,1)} %param.9) | copy-start | bytes 786436
  92.3 15.6 %all-to-all-start.2 = ((f32[16,4,128]{2,1,0:T(4,128)}), f32[16,4,128]{2,1,0:T(4,128)S(1)}, u32[]{:S(2)}, u32[]{:S(2)}) async-start(f32[16,4,128]{2,1,0:T(4,128)} %get-tuple-element.30), calls=%async_computation.2 | async-start | bytes 65536 | tf_op jit(solution)/shard_map/all_to_all | solution.py:446
  102.2 5.7 %copy-start.13 = (f32[1,4,128]{2,1,0:T(4,128)S(1)}, f32[1,4,128]{2,1,0:T(4,128)}, u32[]{:S(2)}) copy-start(f32[1,4,128]{2,1,0:T(4,128)} %param.11) | copy-start | bytes 6148

commit v8 on v7

--- a/solution.py
+++ b/solution.py
@@ -65,7 +65,7 @@
                 return carry
 
             if begin < end:
-                lax.fori_loop(begin, end, one, 0)
+                lax.fori_loop(begin, end, one, 0, unroll=2 if (end - begin) % 2 == 0 else 1)
         now, after = after, now
 
 
@@ -287,7 +287,9 @@
             density_ref[owner, plane : plane + 1] = dense[:1]
 
 
-def tail_kernel(slab, grid, place, gathered, external, field, grid_ref, evolved_ref):
+def tail_kernel(slab, grid, place, gathered, external, field, inter, grid_ref, evolved_ref,
+                inter_ref):
+    inter_ref[...] = inter[...]
     lanes = external.shape[-1]
     half = field.shape[0] // 2
     cells = half // slab
@@ -448,13 +450,17 @@
     mine = lax.dynamic_index_in_dim(neighbours, own_index, 0, keepdims=False)
     shift = lax.dynamic_index_in_dim(offsets, own_index, 0, keepdims=False)
     where = jnp.concatenate([mine, shift, own_index.reshape(1).astype(jnp.int32)])
-    new_grid, evolved = pl.pallas_call(
+    new_grid, evolved, intersection = pl.pallas_call(
         lambda *refs: tail_kernel(slab, grid, *refs),
-        out_shape=(shape((slab, cells), f32), shape((rows, orbits), bf16)),
-        in_specs=scalars(3),
+        out_shape=(
+            shape((slab, cells), f32),
+            shape((rows, orbits), bf16),
+            shape((2 * orbits, orbits), f32),
+        ),
+        in_specs=scalars(4),
         compiler_params=limit(8),
         name="tail",
-    )(where, gathered, external[0], field)
+    )(where, gathered, external[0], field, intersection)
     return (
         evolved.reshape(orbitals.shape),
         intersection.reshape(1, 2, orbits, orbits),

time: 110 us -> 111 us (level)
  no operation moved by 1% of the time
where the time goes in v8:
time: 111 us; the launch traced here: 110 us
  starting transfers between devices  45.1 us (41%)
  blocking collectives  19.9 us (18%)
  waiting for transfers between devices  18.1 us (16%)
  Pallas kernels  16.6 us (15%)
  local copies, waits for them, and re-layouts  9.76 us (9%)
    ppermute x6, starting transfers between devices, neighbour_pair(): return (lax.ppermute(value, axis, up), lax.ppermute(value, axis, down))  28.2 us
    all_to_all x1, blocking collectives, shards(): lax.all_to_all(partial.reshape(devices, share, orbits), 'space', 0, 0, ti...  19.9 us
    ppermute x6, waiting for transfers between devices, neighbour_pair(): return (lax.ppermute(value, axis, up), lax.ppermute(value, axis, down))  12.3 us
    all_to_all x1, starting transfers between devices, shards(): gathered = lax.all_to_all(density, 'dom', 0, 0, tiled=True)  9.76 us
    unnamed x34, local copies, waits for them, and re-layouts  9.55 us
    all_to_all x1, starting transfers between devices, shards(): sums = lax.all_to_all(spread, 'space', 0, 0, tiled=True)  7.05 us
    all_to_all x1, waiting for transfers between devices, shards(): gathered = lax.all_to_all(density, 'dom', 0, 0, tiled=True)  5.73 us
    pallas_call x1, Pallas kernels, shards(): pl.pallas_call(lambda *refs: start_kernel(slab, grid, scale, *refs), out_...  5.52 us
  transfers between devices with their start and end apart: 8, of which 5 were waited for; matrix products, arithmetic and copies ran while one was open for 0% of the time, Pallas kernels for 7%

profile of v8, /device:TPU:5, one launch (start us, length us, event | category | flops | bytes accessed | tf_op | source)
XLA Modules:
  0.0 110.3 jit_solution(14648471992278134548)
XLA Ops:
  0.6 0.0 copy-start.12
  0.6 0.7 copy-done.12
  1.3 0.0 copy-start
  1.3 0.9 copy-done
  2.3 0.0 copy-start.2
  2.3 11.2 %collective-permute-start.3 = (bf16[1056,128]{1,0:T(8,128)(2,1)S(1)}, bf16[1056,128]{1,0:T(8,128)(2,1)S(1)}, u32[]{:S(2)}, u32[]{:S(2)}) collective-permute-start(bf16[1056,128]{1,0:T(8,128)(2,1)S(1)} %pack.1.refs_2_), channel_id=1, source_target_pairs={{1,0},{2,1},{3,2},{4,3},{5,4},{6,5},{7,6},{8,7},{9,8},{10,9},{11,1... | collective-permute-start | bytes 811016 | tf_op jit(solution)/shard_map/ppermute | solution.py:21
  13.5 1.9 %collective-permute-start.2 = (bf16[1056,128]{1,0:T(8,128)(2,1)S(1)}, bf16[1056,128]{1,0:T(8,128)(2,1)S(1)}, u32[]{:S(2)}, u32[]{:S(2)}) collective-permute-start(bf16[1056,128]{1,0:T(8,128)(2,1)S(1)} %pack.1.refs_2_), channel_id=1, source_target_pairs={{0,1},{1,2},{2,3},{3,4},{4,5},{5,6},{6,7},{7,8},{8,9},{9,10},{10,1... | collective-permute-start | bytes 811016 | tf_op jit(solution)/shard_map/ppermute | solution.py:21
  15.4 0.0 copy-done.2
  15.4 7.0 %collective-permute-start.1 = (bf16[1024,128]{1,0:T(8,128)(2,1)S(1)}, bf16[1024,128]{1,0:T(8,128)(2,1)S(1)}, u32[]{:S(2)}, u32[]{:S(2)}) collective-permute-start(bf16[1024,128]{1,0:T(8,128)(2,1)S(1)} %bitcast.15), channel_id=1, source_target_pairs={{1,0},{2,1},{3,2},{4,3},{5,4},{6,5},{7,6},{8,7},{9,8},{10,9},{11,1... | collective-permute-start | bytes 786440 | tf_op jit(solution)/shard_map/ppermute | solution.py:21
  22.4 1.9 %collective-permute-start = (bf16[1024,128]{1,0:T(8,128)(2,1)S(1)}, bf16[1024,128]{1,0:T(8,128)(2,1)}, u32[]{:S(2)}, u32[]{:S(2)}) collective-permute-start(bf16[1024,128]{1,0:T(8,128)(2,1)S(1)} %bitcast.16), channel_id=1, source_target_pairs={{0,1},{1,2},{2,3},{3,4},{4,5},{5,6},{6,7},{7,8},{8,9},{9,10},{10,1... | collective-permute-start | bytes 786440 | tf_op jit(solution)/shard_map/ppermute | solution.py:21
  24.4 0.1 add_convert_fusion.refs_0_
  24.4 0.0 collective-permute-done.3.refs_3_
  24.4 1.7 %collective-permute-done.2.refs_1_ = bf16[1056,128]{1,0:T(8,128)(2,1)S(1)} collective-permute-done((bf16[1056,128]{1,0:T(8,128)(2,1)S(1)}, bf16[1056,128]{1,0:T(8,128)(2,1)S(1)}, u32[]{:S(2)}, u32[]{:S(2)}) %collective-permute-start.2) | collective-permute-done | bytes 270368 | tf_op jit(solution)/shard_map/ppermute | solution.py:21
  26.1 5.5 %start.1 = (bf16[512,128]{1,0:T(8,128)(2,1)S(1)}, bf16[1024,128]{1,0:T(8,128)(2,1)S(1)}, bf16[128,1024]{1,0:T(8,128)(2,1)S(1)}, f32[12,128,128]{2,1,0:T(8,128)S(1)}, f32[12,128,128]{2,1,0:T(8,128)S(1)}) custom-call(f32[2]{0:T(128)S(1)} %add_convert_fusion.refs_0_, bf16[1056,128]{1,0:T(8,128)(2,1)S(1)} %collective-permute-done.2.refs_1_, ...), custom_call_target="tpu_custom_call" | custom-call | tf_op jit(solution)/shard_map/start/pallas_call | solution.py:383
  31.6 0.0 collective-permute-done.1.refs_3_
  31.6 0.0 copy-start.3
  31.6 0.7 copy-done.3
  32.3 2.0 %collective-permute-done.refs_1_ = bf16[1024,128]{1,0:T(8,128)(2,1)} collective-permute-done((bf16[1024,128]{1,0:T(8,128)(2,1)S(1)}, bf16[1024,128]{1,0:T(8,128)(2,1)}, u32[]{:S(2)}, u32[]{:S(2)}) %collective-permute-start) | collective-permute-done | bytes 262176 | tf_op jit(solution)/shard_map/ppermute | solution.py:21
  34.4 0.0 copy-start.4
  34.4 0.9 copy-done.4
  35.3 3.6 %first.1 = (bf16[768,128]{1,0:T(8,128)(2,1)S(1)}, bf16[1024,128]{1,0:T(8,128)(2,1)S(1)}, f32[1024,128]{1,0:T(8,128)S(1)}) custom-call(f32[2]{0:T(128)S(1)} %add_convert_fusion.refs_0_, bf16[1024,128]{1,0:T(8,128)(2,1)} %collective-permute-done.refs_1_, bf16[1024,128]{1,0:T(8,128)(2,1)S(1)} %bitcast.18, bf16[1024,128]{1,0:T(8,128)(2,1)S(1)} %copy-done.4, ...), custom_call_target="tpu_custom_call" | custom-call | tf_op jit(solution)/shard_map/first/pallas_call | solution.py:401
  38.9 0.0 copy-start.5
  38.9 19.9 %all_to_all.15.parts_ref = bf16[32,24,128]{2,1,0:T(8,128)(2,1)S(1)} all-to-all(bf16[32,24,128]{2,1,0:T(8,128)(2,1)S(1)} %bitcast.20), channel_id=1, replica_groups=mesh['dom'=16,'space'=32] {'space'}, dimensions={0} | all-to-all | bytes 393216 | tf_op jit(solution)/shard_map/all_to_all | solution.py:414
  58.8 0.7 total.1
  59.5 0.0 copy-start.11
  59.5 7.1 %all-to-all-start.1 = ((bf16[32,24,128]{2,1,0:T(8,128)(2,1)}), bf16[32,24,128]{2,1,0:T(8,128)(2,1)S(1)}, u32[]{:S(2)}, u32[]{:S(2)}) async-start(bf16[32,24,128]{2,1,0:T(8,128)(2,1)} %total.1), calls=%async_computation.1 | async-start | bytes 393216 | tf_op jit(solution)/shard_map/all_to_all | solution.py:422
  66.6 4.3 %collective-permute-start.5 = (bf16[1024,128]{1,0:T(8,128)(2,1)S(1)}, bf16[1024,128]{1,0:T(8,128)(2,1)S(1)}, u32[]{:S(2)}, u32[]{:S(2)}) collective-permute-start(bf16[1024,128]{1,0:T(8,128)(2,1)S(1)} %get-tuple-element.25.refs_2_), channel_id=1, source_target_pairs={{1,0},{2,1},{3,2},{4,3},{5,4},{6,5},{7,6},{8,7},{9,8},{10,9},{11,1... | collective-permute-start | bytes 786440 | tf_op jit(solution)/shard_map/ppermute | solution.py:21
  70.9 0.0 copy-done.5
  70.9 1.9 %collective-permute-start.4 = (bf16[1024,128]{1,0:T(8,128)(2,1)S(1)}, bf16[1024,128]{1,0:T(8,128)(2,1)S(1)}, u32[]{:S(2)}, u32[]{:S(2)}) collective-permute-start(bf16[1024,128]{1,0:T(8,128)(2,1)S(1)} %get-tuple-element.25.refs_2_), channel_id=1, source_target_pairs={{0,1},{1,2},{2,3},{3,4},{4,5},{5,6},{6,7},{7,8},{8,9},{9,10},{10,1... | collective-permute-start | bytes 786440 | tf_op jit(solution)/shard_map/ppermute | solution.py:21
  72.8 0.0 copy-start.15
  72.8 0.0 copy-start.16
  72.9 0.7 copy-done.15
  73.5 0.0 copy-done.16
  73.5 0.2 dynamic-slice_reduce_fusion
  73.7 6.6 %collective-permute-done.5.refs_3_ = bf16[1024,128]{1,0:T(8,128)(2,1)S(1)} collective-permute-done((bf16[1024,128]{1,0:T(8,128)(2,1)S(1)}, bf16[1024,128]{1,0:T(8,128)(2,1)S(1)}, u32[]{:S(2)}, u32[]{:S(2)}) %collective-permute-start.5) | collective-permute-done | bytes 262176 | tf_op jit(solution)/shard_map/ppermute | solution.py:21
  80.4 0.0 copy-start.7
  80.4 0.7 copy-done.7
  81.1 2.0 %collective-permute-done.4.refs_1_ = bf16[1024,128]{1,0:T(8,128)(2,1)S(1)} collective-permute-done((bf16[1024,128]{1,0:T(8,128)(2,1)S(1)}, bf16[1024,128]{1,0:T(8,128)(2,1)S(1)}, u32[]{:S(2)}, u32[]{:S(2)}) %collective-permute-start.4) | collective-permute-done | bytes 262176 | tf_op jit(solution)/shard_map/ppermute | solution.py:21
  83.1 0.0 copy-start.9
  83.1 0.7 copy-done.9
  83.8 0.0 copy-start.14
  83.8 0.0 copy-done.11
  83.8 0.7 copy-done.14
  84.4 0.0 copy-start.6
  84.4 0.9 copy-done.6
  85.4 0.0 copy-start.8
  85.4 0.9 copy-done.8
  86.3 0.0 copy-start.10
  86.3 0.9 copy-done.10
  87.3 0.0 copy-start.1
  87.3 2.7 %second.1 = (f32[1024,128]{1,0:T(8,128)S(1)}, f32[128,128]{1,0:T(8,128)S(1)}, f32[8,128]{1,0:T(8,128)S(1)}) custom-call(f32[2]{0:T(128)S(1)} %add_convert_fusion.refs_0_, bf16[1024,128]{1,0:T(8,128)(2,1)S(1)} %copy-done.10, bf16[1024,128]{1,0:T(8,128)(2,1)S(1)} %copy-done.6, bf16[1024,128]{1,0:T(8,128)(2,1)S(1)} %copy-done.8, ...), custom_call_target="tpu_custom_call" | custom-call | tf_op jit(solution)/shard_map/second/pallas_call | solution.py:424
  90.0 0.0 all-to-all-done.1
  90.0 0.0 copy-done.1
  90.0 2.5 %back.1 = (f32[256,128]{1,0:T(8,128)S(1)}, f32[1024,128]{1,0:T(8,128)S(1)}, f32[16,4,128]{2,1,0:T(4,128)}) custom-call(bf16[768,128]{1,0:T(8,128)(2,1)S(1)} %bitcast.19, f32[128,128]{1,0:T(8,128)S(1)} %get-tuple-element.27.refs_1_, bf16[1024,128]{1,0:T(8,128)(2,1)S(1)} %get-tuple-element.28.refs_2_, bf16[1024,128]{1,0:T(8,128)(2,1)S(1)} %bitcast.14, ...), custom_call_target="tpu_custom_call" | custom-call | tf_op jit(solution)/shard_map/back/pallas_call | solution.py:438
  92.4 9.8 %all-to-all-start.2 = ((f32[16,4,128]{2,1,0:T(4,128)}), f32[16,4,128]{2,1,0:T(4,128)S(1)}, u32[]{:S(2)}, u32[]{:S(2)}) async-start(f32[16,4,128]{2,1,0:T(4,128)} %get-tuple-element.31), calls=%async_computation.2 | async-start | bytes 65536 | tf_op jit(solution)/shard_map/all_to_all | solution.py:448
  102.2 0.1 pad_add_fusion.refs_0_
  102.3 5.7 %all-to-all-done.2.refs_1_ = f32[16,4,128]{2,1,0:T(4,128)S(1)} async-done(((f32[16,4,128]{2,1,0:T(4,128)}), f32[16,4,128]{2,1,0:T(4,128)S(1)}, u32[]{:S(2)}, u32[]{:S(2)}) %all-to-all-start.2) | async-done | bytes 32800 | tf_op jit(solution)/shard_map/all_to_all | solution.py:448
  108.0 0.0 copy-start.13
  108.0 0.7 copy-done.13
  108.7 1.6 %tail.1 = (f32[4,128]{1,0:T(4,128)}, bf16[1024,128]{1,0:T(8,128)(2,1)}, f32[256,128]{1,0:T(8,128)}) custom-call(s32[5]{0:T(128)S(1)} %pad_add_fusion.refs_0_, f32[16,4,128]{2,1,0:T(4,128)S(1)} %all-to-all-done.2.refs_1_, f32[4,128]{1,0:T(4,128)S(1)} %bitcast.23, f32[1024,128]{1,0:T(8,128)S(1)} %get-tuple-element.32.refs_3_, ...), custom_call_target="tpu_custom_call" | custom-call | tf_op jit(solution)/shard_map/tail/pallas_call | solution.py:453
  (1 shorter events, 0.0 us)
Async XLA Ops:
  0.6 0.7 copy-start.12
  1.3 0.9 copy-start
  2.3 13.2 %copy-start.2 = (bf16[1,2,4,16,8,128]{5,4,3,2,1,0:T(8,128)(2,1)S(1)}, bf16[1,2,4,16,8,128]{5,4,3,2,1,0:T(8,128)(2,1)}, u32[]{:S(2)}) copy-start(bf16[1,2,4,16,8,128]{5,4,3,2,1,0:T(8,128)(2,1)} %param.8) | copy-start | bytes 786436
  2.3 22.1 %collective-permute-start.3 = (bf16[1056,128]{1,0:T(8,128)(2,1)S(1)}, bf16[1056,128]{1,0:T(8,128)(2,1)S(1)}, u32[]{:S(2)}, u32[]{:S(2)}) collective-permute-start(bf16[1056,128]{1,0:T(8,128)(2,1)S(1)} %pack.1.refs_2_), channel_id=1, source_target_pairs={{1,0},{2,1},{3,2},{4,3},{5,4},{6,5},{7,6},{8,7},{9,8},{10,9},{11,1... | collective-permute-start | bytes 811016 | tf_op jit(solution)/shard_map/ppermute | solution.py:21
  13.5 12.6 %collective-permute-start.2 = (bf16[1056,128]{1,0:T(8,128)(2,1)S(1)}, bf16[1056,128]{1,0:T(8,128)(2,1)S(1)}, u32[]{:S(2)}, u32[]{:S(2)}) collective-permute-start(bf16[1056,128]{1,0:T(8,128)(2,1)S(1)} %pack.1.refs_2_), channel_id=1, source_target_pairs={{0,1},{1,2},{2,3},{3,4},{4,5},{5,6},{6,7},{7,8},{8,9},{9,10},{10,1... | collective-permute-start | bytes 811016 | tf_op jit(solution)/shard_map/ppermute | solution.py:21
  15.4 16.2 %collective-permute-start.1 = (bf16[1024,128]{1,0:T(8,128)(2,1)S(1)}, bf16[1024,128]{1,0:T(8,128)(2,1)S(1)}, u32[]{:S(2)}, u32[]{:S(2)}) collective-permute-start(bf16[1024,128]{1,0:T(8,128)(2,1)S(1)} %bitcast.15), channel_id=1, source_target_pairs={{1,0},{2,1},{3,2},{4,3},{5,4},{6,5},{7,6},{8,7},{9,8},{10,9},{11,1... | collective-permute-start | bytes 786440 | tf_op jit(solution)/shard_map/ppermute | solution.py:21
  22.4 12.0 %collective-permute-start = (bf16[1024,128]{1,0:T(8,128)(2,1)S(1)}, bf16[1024,128]{1,0:T(8,128)(2,1)}, u32[]{:S(2)}, u32[]{:S(2)}) collective-permute-start(bf16[1024,128]{1,0:T(8,128)(2,1)S(1)} %bitcast.16), channel_id=1, source_target_pairs={{0,1},{1,2},{2,3},{3,4},{4,5},{5,6},{6,7},{7,8},{8,9},{9,10},{10,1... | collective-permute-start | bytes 786440 | tf_op jit(solution)/shard_map/ppermute | solution.py:21
  31.6 0.7 copy-start.3
  34.4 1.0 copy-start.4
  38.9 32.0 %copy-start.5 = (bf16[1024,128]{1,0:T(8,128)(2,1)}, bf16[1024,128]{1,0:T(8,128)(2,1)S(1)}, u32[]{:S(2)}) copy-start(bf16[1024,128]{1,0:T(8,128)(2,1)S(1)} %get-tuple-element.25.refs_2_) | copy-start | bytes 786436
  59.5 24.3 %copy-start.11 = (f32[128,128]{1,0:T(8,128)S(1)}, f32[128,128]{1,0:T(8,128)}, u32[]{:S(2)}) copy-start(f32[128,128]{1,0:T(8,128)} %refs_7_.1) | copy-start | bytes 196612
  59.5 30.4 %all-to-all-start.1 = ((bf16[32,24,128]{2,1,0:T(8,128)(2,1)}), bf16[32,24,128]{2,1,0:T(8,128)(2,1)S(1)}, u32[]{:S(2)}, u32[]{:S(2)}) async-start(bf16[32,24,128]{2,1,0:T(8,128)(2,1)} %total.1), calls=%async_computation.1 | async-start | bytes 393216 | tf_op jit(solution)/shard_map/all_to_all | solution.py:422
  66.6 13.8 %collective-permute-start.5 = (bf16[1024,128]{1,0:T(8,128)(2,1)S(1)}, bf16[1024,128]{1,0:T(8,128)(2,1)S(1)}, u32[]{:S(2)}, u32[]{:S(2)}) collective-permute-start(bf16[1024,128]{1,0:T(8,128)(2,1)S(1)} %get-tuple-element.25.refs_2_), channel_id=1, source_target_pairs={{1,0},{2,1},{3,2},{4,3},{5,4},{6,5},{7,6},{8,7},{9,8},{10,9},{11,1... | collective-permute-start | bytes 786440 | tf_op jit(solution)/shard_map/ppermute | solution.py:21
  70.9 12.2 %collective-permute-start.4 = (bf16[1024,128]{1,0:T(8,128)(2,1)S(1)}, bf16[1024,128]{1,0:T(8,128)(2,1)S(1)}, u32[]{:S(2)}, u32[]{:S(2)}) collective-permute-start(bf16[1024,128]{1,0:T(8,128)(2,1)S(1)} %get-tuple-element.25.refs_2_), channel_id=1, source_target_pairs={{0,1},{1,2},{2,3},{3,4},{4,5},{5,6},{6,7},{7,8},{8,9},{9,10},{10,1... | collective-permute-start | bytes 786440 | tf_op jit(solution)/shard_map/ppermute | solution.py:21
  72.8 0.7 copy-start.15
  72.8 0.7 copy-start.16
  80.4 0.7 copy-start.7
  83.1 0.7 copy-start.9
  83.8 0.7 copy-start.14
  84.4 0.9 copy-start.6
  85.4 0.9 copy-start.8
  86.3 0.9 copy-start.10
  87.3 2.7 %copy-start.1 = (bf16[1,2,4,16,8,128]{5,4,3,2,1,0:T(8,128)(2,1)S(1)}, bf16[1,2,4,16,8,128]{5,4,3,2,1,0:T(8,128)(2,1)}, u32[]{:S(2)}) copy-start(bf16[1,2,4,16,8,128]{5,4,3,2,1,0:T(8,128)(2,1)} %param.9) | copy-start | bytes 786436
  92.4 15.6 %all-to-all-start.2 = ((f32[16,4,128]{2,1,0:T(4,128)}), f32[16,4,128]{2,1,0:T(4,128)S(1)}, u32[]{:S(2)}, u32[]{:S(2)}) async-start(f32[16,4,128]{2,1,0:T(4,128)} %get-tuple-element.31), calls=%async_computation.2 | async-start | bytes 65536 | tf_op jit(solution)/shard_map/all_to_all | solution.py:448
  108.0 0.7 copy-start.13
